TPU v7x, 32 devices: a whole 2x2x4 slice. The times are simulated.
32 devices in a mesh: seq: 4 (over z), fsdp: 8 (over y, x, core).
Axes of the slice: x: 2, y: 2, z: 4, core: 2. Of those that a mesh axis runs over, the one named last changes fastest.
Arguments:
- layer_input: bfloat16 [8192, 1024], P(('fsdp', 'seq')), may hold values from -6 to 6
- v_first: bfloat16 [8192, 1024], P(('fsdp', 'seq')), may hold values from -6 to 6
- offsets: int32 [8192], P('fsdp'), may hold values from 0 to 4095, as said below
- g_attn: bfloat16 [1024], P(('seq', 'fsdp')), may hold values from 0.099609375 to 1.8984375
- w_query: bfloat16 [1024, 1024], P(('seq', 'fsdp')), may hold values from -0.25 to 0.25
- w_key: bfloat16 [1024, 1024], P(('seq', 'fsdp')), may hold values from -0.25 to 0.25
- w_value: bfloat16 [1024, 1024], P(('seq', 'fsdp')), may hold values from -0.1875 to 0.1875
- w_out: bfloat16 [1024, 1024], P(('seq', 'fsdp')), may hold values from -1.5 to 1.5
- g_ffn: bfloat16 [1024], P(('seq', 'fsdp')), may hold values from 0.099609375 to 1.8984375
- w_gate: bfloat16 [1024, 2816], P(('seq', 'fsdp')), may hold values from -0.1875 to 0.1875
- w_up: bfloat16 [1024, 2816], P(('seq', 'fsdp')), may hold values from -0.1875 to 0.1875
- w_down: bfloat16 [2816, 1024], P(('seq', 'fsdp')), may hold values from -0.109375 to 0.109375
- out_cot: bfloat16 [8192, 1024], P(('fsdp', 'seq')), may hold values from -6 to 6
Outputs:
- layer_output: bfloat16 [8192, 1024], P(('fsdp', 'seq'))
- grad_input: float32 [8192, 1024], P(('fsdp', 'seq'))
- grad_v_first: float32 [8192, 1024], P(('fsdp', 'seq'))
- grad_g_attn: float32 [1024], P(('seq', 'fsdp'))
- grad_w_query: float32 [1024, 1024], P(('seq', 'fsdp'))
- grad_w_key: float32 [1024, 1024], P(('seq', 'fsdp'))
- grad_w_value: float32 [1024, 1024], P(('seq', 'fsdp'))
- grad_w_out: float32 [1024, 1024], P(('seq', 'fsdp'))
- grad_g_ffn: float32 [1024], P(('seq', 'fsdp'))
- grad_w_gate: float32 [1024, 2816], P(('seq', 'fsdp'))
- grad_w_up: float32 [1024, 2816], P(('seq', 'fsdp'))
- grad_w_down: float32 [2816, 1024], P(('seq', 'fsdp'))
Inputs may be any that keep to these rules, and one draw needn't show every extreme that they name: offsets[0] = 0, and offsets[i] is either 0 (a document begins at i) or offsets[i-1] + 1; exactly one document has 4096 tokens.
All inputs are finite; a program needn't handle non-finite values.
Results may differ from a plain program's by a relative error of at most 0.015.
Values may be sent and summed in bfloat16 or wider, within the bound.
A program may use at most 192 MiB of HBM per device.

v0:
```python
import jax
import jax.numpy as jnp
from jax import lax
from jax.sharding import PartitionSpec as P

HEADS = 16
HEAD_DIM = 64


EPSILON = 1e-06
NEGATIVE = -1e30


def rms_scale(tensor):
    return lax.rsqrt(jnp.mean(tensor * tensor, axis=-1, keepdims=True) + EPSILON)


def angle_tables(offsets):
    half_dim = HEAD_DIM // 2
    frequency = jnp.power(10000.0, -jnp.arange(half_dim, dtype=jnp.float32) / half_dim)
    angles = offsets.astype(jnp.float32)[:, None] * frequency[None, :]
    return (jnp.cos(angles)[:, None, :], jnp.sin(angles)[:, None, :])


def rotate(tensor, cosine, sine_tab):
    half_dim = HEAD_DIM // 2
    front_half = tensor[..., :half_dim]
    back_half = tensor[..., half_dim:]
    return jnp.concatenate(
        [front_half * cosine - back_half * sine_tab, back_half * cosine + front_half * sine_tab],
        axis=-1,
    )


def unrotate(tensor, cosine, sine_tab):
    half_dim = HEAD_DIM // 2
    front_half = tensor[..., :half_dim]
    back_half = tensor[..., half_dim:]
    return jnp.concatenate(
        [front_half * cosine + back_half * sine_tab, back_half * cosine - front_half * sine_tab],
        axis=-1,
    )


def matmul(left, right):
    return jnp.dot(left, right, preferred_element_type=jnp.float32)


def contract_rows(left, right):
    return lax.dot_general(
        left, right, (((0,), (0,)), ((), ())), preferred_element_type=jnp.float32
    )


def contract_cols(left, right):
    return lax.dot_general(
        left, right, (((1,), (1,)), ((), ())), preferred_element_type=jnp.float32
    )


def mask_for(q_pos, q_begin, k_first, count):
    k_pos = k_first + jnp.arange(count, dtype=jnp.int32)
    return (k_pos[None, :] <= q_pos[:, None]) & (k_pos[None, :] >= q_begin[:, None])


def is_live(q_pos, q_begin, k_first, count):
    return (k_first <= q_pos[-1]) & (k_first + count - 1 >= q_begin[0])


def fetch_rows(source, number, piece_rows, heads_here):
    return lax.dynamic_slice_in_dim(source, number * piece_rows, piece_rows, 0).reshape(
        piece_rows, heads_here, HEAD_DIM
    )


def masked_scores(q_rows, k_rows, allowed, score_scale):
    scores = (
        jnp.einsum("qhd,khd->hqk", q_rows, k_rows, preferred_element_type=jnp.float32) * score_scale
    )
    return jnp.where(allowed[None], scores, NEGATIVE)


def forward_block(q_rows, q_pos, q_begin, key_rows, value_rows, piece_rows, score_scale):
    heads_here = q_rows.shape[1]
    height = q_rows.shape[0]
    numbers = jnp.arange(key_rows.shape[0] // piece_rows, dtype=jnp.int32)

    def first_pass(running, number):
        k_first = number * piece_rows

        def first_update(current):
            row_top, row_total = current
            allowed = mask_for(q_pos, q_begin, k_first, piece_rows)
            scores = masked_scores(
                q_rows, fetch_rows(key_rows, number, piece_rows, heads_here), allowed, score_scale
            )
            new_top = jnp.maximum(row_top, jnp.max(scores, axis=-1))
            weights = jnp.where(allowed[None], jnp.exp(scores - new_top[..., None]), 0.0)
            return (new_top, row_total * jnp.exp(row_top - new_top) + jnp.sum(weights, axis=-1))

        live = is_live(q_pos, q_begin, k_first, piece_rows)
        return (lax.cond(live, first_update, lambda current: current, running), None)

    start_state = (
        jnp.full((heads_here, height), NEGATIVE, jnp.float32),
        jnp.zeros((heads_here, height), jnp.float32),
    )
    final_state = lax.scan(first_pass, start_state, numbers)[0]
    log_total = final_state[0] + jnp.log(final_state[1])

    def second_pass(running, number):
        k_first = number * piece_rows

        def second_update(out_sum):
            allowed = mask_for(q_pos, q_begin, k_first, piece_rows)
            scores = masked_scores(
                q_rows, fetch_rows(key_rows, number, piece_rows, heads_here), allowed, score_scale
            )
            low_probs = jnp.where(
                allowed[None], jnp.exp(scores - log_total[..., None]), 0.0
            ).astype(jnp.bfloat16)
            return out_sum + jnp.einsum(
                "hqk,khd->qhd",
                low_probs,
                fetch_rows(value_rows, number, piece_rows, heads_here),
                preferred_element_type=jnp.float32,
            )

        live = is_live(q_pos, q_begin, k_first, piece_rows)
        return (lax.cond(live, second_update, lambda out_sum: out_sum, running), None)

    attended = lax.scan(
        second_pass, jnp.zeros((height, heads_here, HEAD_DIM), jnp.float32), numbers
    )[0]
    return (log_total, attended)


def backward_block(
    q_rows,
    grad_rows,
    log_total,
    spread,
    q_pos,
    q_begin,
    key_rows,
    value_rows,
    piece_rows,
    score_scale,
    key_grads,
    value_grads,
):
    heads_here = q_rows.shape[1]
    numbers = jnp.arange(key_rows.shape[0] // piece_rows, dtype=jnp.int32)

    def step_back(running, number):
        local_first = number * piece_rows

        def step_update(current):
            grad_query, grad_keys, grad_values = current
            k_rows = fetch_rows(key_rows, number, piece_rows, heads_here)
            v_rows = fetch_rows(value_rows, number, piece_rows, heads_here)
            allowed = mask_for(q_pos, q_begin, local_first, piece_rows)
            scores = masked_scores(q_rows, k_rows, allowed, score_scale)
            probs = jnp.where(allowed[None], jnp.exp(scores - log_total[..., None]), 0.0)
            low_probs = probs.astype(jnp.bfloat16)
            value_part = jnp.einsum(
                "hqk,qhd->khd", low_probs, grad_rows, preferred_element_type=jnp.float32
            )
            grad_probs = jnp.einsum(
                "qhd,khd->hqk", grad_rows, v_rows, preferred_element_type=jnp.float32
            )
            grad_scores = (probs * (grad_probs - spread[..., None])).astype(jnp.bfloat16)
            grad_query = grad_query + score_scale * jnp.einsum(
                "hqk,khd->qhd", grad_scores, k_rows, preferred_element_type=jnp.float32
            )
            key_part = score_scale * jnp.einsum(
                "hqk,qhd->khd", grad_scores, q_rows, preferred_element_type=jnp.float32
            )
            old_keys = lax.dynamic_slice_in_dim(grad_keys, local_first, piece_rows, 0)
            grad_keys = lax.dynamic_update_slice_in_dim(
                grad_keys, old_keys + key_part.reshape(piece_rows, -1), local_first, 0
            )
            old_values = lax.dynamic_slice_in_dim(grad_values, local_first, piece_rows, 0)
            grad_values = lax.dynamic_update_slice_in_dim(
                grad_values, old_values + value_part.reshape(piece_rows, -1), local_first, 0
            )
            return (grad_query, grad_keys, grad_values)

        live = is_live(q_pos, q_begin, local_first, piece_rows)
        return (lax.cond(live, step_update, lambda current: current, running), None)

    start_state = (jnp.zeros(q_rows.shape, jnp.float32), key_grads, value_grads)
    return lax.scan(step_back, start_state, numbers)[0]


def per_device(
    layer_input,
    v_first,
    offsets,
    g_attn,
    w_query,
    w_key,
    w_value,
    w_out,
    g_ffn,
    w_gate,
    w_up,
    w_down,
    out_cot,
):
    gathered = (
        lax.all_gather(g_attn, ("seq", "fsdp"), axis=0, tiled=True),
        lax.all_gather(w_query, ("seq", "fsdp"), axis=0, tiled=True),
        lax.all_gather(w_key, ("seq", "fsdp"), axis=0, tiled=True),
        lax.all_gather(w_value, ("seq", "fsdp"), axis=0, tiled=True),
        lax.all_gather(w_out, ("seq", "fsdp"), axis=0, tiled=True),
        lax.all_gather(g_ffn, ("seq", "fsdp"), axis=0, tiled=True),
        lax.all_gather(w_gate, ("seq", "fsdp"), axis=0, tiled=True),
        lax.all_gather(w_up, ("seq", "fsdp"), axis=0, tiled=True),
        lax.all_gather(w_down, ("seq", "fsdp"), axis=0, tiled=True),
    )
    (
        gain_attn,
        proj_query,
        proj_key,
        proj_value,
        proj_out,
        gain_ffn,
        proj_gate,
        proj_up,
        proj_down,
    ) = gathered
    tokens = layer_input.shape[0]
    group_size = lax.axis_size("seq")
    group_rows = tokens * group_size
    heads_here = HEADS // group_size
    score_scale = HEAD_DIM ** (-0.5)
    seq_index = lax.axis_index("seq")
    part_index = lax.axis_index("fsdp")
    own_offsets = lax.dynamic_slice_in_dim(offsets, seq_index * tokens, tokens, 0)
    cos_tokens, sin_tokens = angle_tables(own_offsets)
    input_f32 = layer_input.astype(jnp.float32)
    norm_attn = rms_scale(input_f32)
    normed_a = (input_f32 * norm_attn * gain_attn.astype(jnp.float32)).astype(jnp.bfloat16)
    q_tokens = (
        rotate(
            matmul(normed_a, proj_query).reshape(tokens, HEADS, HEAD_DIM), cos_tokens, sin_tokens
        )
        .reshape(tokens, -1)
        .astype(jnp.bfloat16)
    )
    k_tokens = (
        rotate(matmul(normed_a, proj_key).reshape(tokens, HEADS, HEAD_DIM), cos_tokens, sin_tokens)
        .reshape(tokens, -1)
        .astype(jnp.bfloat16)
    )
    mixed_values = (0.5 * matmul(normed_a, proj_value) + 0.5 * v_first.astype(jnp.float32)).astype(
        jnp.bfloat16
    )
    q_heads, k_heads, v_heads = (
        lax.all_to_all(q_tokens, "seq", split_axis=1, concat_axis=0, tiled=True),
        lax.all_to_all(k_tokens, "seq", split_axis=1, concat_axis=0, tiled=True),
        lax.all_to_all(mixed_values, "seq", split_axis=1, concat_axis=0, tiled=True),
    )
    k_whole, v_whole = (
        lax.all_gather(k_heads, "fsdp", axis=0, tiled=True),
        lax.all_gather(v_heads, "fsdp", axis=0, tiled=True),
    )
    positions = part_index * group_rows + jnp.arange(group_rows, dtype=jnp.int32)
    doc_begins = positions - offsets
    block_rows = min(1024, group_rows)
    q_three = q_heads.reshape(group_rows, heads_here, HEAD_DIM)
    lse_parts = []
    out_parts = []
    for number in range(group_rows // block_rows):
        lower = number * block_rows
        upper = lower + block_rows
        log_total, attended = forward_block(
            q_three[lower:upper],
            positions[lower:upper],
            doc_begins[lower:upper],
            k_whole,
            v_whole,
            group_rows,
            score_scale,
        )
        lse_parts.append(log_total)
        out_parts.append(attended)
    attended_all = jnp.concatenate(out_parts, axis=0)
    attended_low = attended_all.reshape(group_rows, -1).astype(jnp.bfloat16)
    attn_tokens = lax.all_to_all(attended_low, "seq", split_axis=0, concat_axis=1, tiled=True)
    after_attn = input_f32 + matmul(attn_tokens, proj_out)
    norm_ffn = rms_scale(after_attn)
    normed_f = (after_attn * norm_ffn * gain_ffn.astype(jnp.float32)).astype(jnp.bfloat16)
    gate_act = matmul(normed_f, proj_gate)
    up_act = matmul(normed_f, proj_up)
    sigmoid_gate = jax.nn.sigmoid(gate_act)
    silu_gate = gate_act * sigmoid_gate
    hidden = (silu_gate * up_act).astype(jnp.bfloat16)
    result = (after_attn + matmul(hidden, proj_down)).astype(jnp.bfloat16)
    regathered = (
        lax.all_gather(g_attn, ("seq", "fsdp"), axis=0, tiled=True),
        lax.all_gather(w_query, ("seq", "fsdp"), axis=0, tiled=True),
        lax.all_gather(w_key, ("seq", "fsdp"), axis=0, tiled=True),
        lax.all_gather(w_value, ("seq", "fsdp"), axis=0, tiled=True),
        lax.all_gather(w_out, ("seq", "fsdp"), axis=0, tiled=True),
        lax.all_gather(g_ffn, ("seq", "fsdp"), axis=0, tiled=True),
        lax.all_gather(w_gate, ("seq", "fsdp"), axis=0, tiled=True),
        lax.all_gather(w_up, ("seq", "fsdp"), axis=0, tiled=True),
        lax.all_gather(w_down, ("seq", "fsdp"), axis=0, tiled=True),
    )
    (
        gain_attn,
        proj_query,
        proj_key,
        proj_value,
        proj_out,
        gain_ffn,
        proj_gate,
        proj_up,
        proj_down,
    ) = regathered
    grad_down = contract_rows(hidden, out_cot)
    grad_hidden = contract_cols(out_cot, proj_down)
    grad_gate_low = (
        grad_hidden * up_act * sigmoid_gate * (1.0 + gate_act * (1.0 - sigmoid_gate))
    ).astype(jnp.bfloat16)
    grad_up_low = (grad_hidden * silu_gate).astype(jnp.bfloat16)
    grad_gate_w = contract_rows(normed_f, grad_gate_low)
    grad_up_w = contract_rows(normed_f, grad_up_low)
    grad_normed_f = contract_cols(grad_gate_low, proj_gate) + contract_cols(grad_up_low, proj_up)
    grad_gain_ffn = jnp.sum(grad_normed_f * after_attn * norm_ffn, axis=0)
    scaled_ffn = grad_normed_f * gain_ffn.astype(jnp.float32)
    grad_after = (
        out_cot.astype(jnp.float32)
        + norm_ffn * scaled_ffn
        - after_attn * norm_ffn**3 * jnp.mean(scaled_ffn * after_attn, axis=-1, keepdims=True)
    )
    grad_attn_low = grad_after.astype(jnp.bfloat16)
    grad_out_w = contract_rows(attn_tokens, grad_attn_low)
    grad_attended = contract_cols(grad_attn_low, proj_out).astype(jnp.bfloat16)
    grad_heads = lax.all_to_all(grad_attended, "seq", split_axis=1, concat_axis=0, tiled=True)
    grad_three = grad_heads.reshape(group_rows, heads_here, HEAD_DIM)
    spread_all = jnp.einsum("qhd,qhd->hq", grad_three.astype(jnp.float32), attended_all)
    key_grads = jnp.zeros((k_whole.shape[0], k_whole.shape[1]), jnp.float32)
    value_grads = jnp.zeros((v_whole.shape[0], v_whole.shape[1]), jnp.float32)
    query_parts = []
    for number in range(group_rows // block_rows):
        lower = number * block_rows
        upper = lower + block_rows
        grad_query, key_grads, value_grads = backward_block(
            q_three[lower:upper],
            grad_three[lower:upper],
            lse_parts[number],
            spread_all[:, lower:upper],
            positions[lower:upper],
            doc_begins[lower:upper],
            k_whole,
            v_whole,
            group_rows,
            score_scale,
            key_grads,
            value_grads,
        )
        query_parts.append(grad_query)
    own_keys, own_values = (
        lax.psum_scatter(
            key_grads.astype(jnp.bfloat16), "fsdp", scatter_dimension=0, tiled=True
        ).astype(jnp.float32),
        lax.psum_scatter(
            value_grads.astype(jnp.bfloat16), "fsdp", scatter_dimension=0, tiled=True
        ).astype(jnp.float32),
    )
    cos_group, sin_group = angle_tables(offsets)
    grad_q_rot = lax.optimization_barrier(
        jnp.concatenate(query_parts, axis=0).astype(jnp.bfloat16)
    ).astype(jnp.float32)
    grad_k_rot = lax.optimization_barrier(own_keys.astype(jnp.bfloat16)).astype(jnp.float32)
    grad_q_pre = (
        unrotate(grad_q_rot, cos_group, sin_group).reshape(group_rows, -1).astype(jnp.bfloat16)
    )
    grad_k_pre = (
        unrotate(grad_k_rot.reshape(group_rows, heads_here, HEAD_DIM), cos_group, sin_group)
        .reshape(group_rows, -1)
        .astype(jnp.bfloat16)
    )
    grad_mixed = own_values.astype(jnp.bfloat16)
    grad_q_tok, grad_k_tok, grad_mix_tok = (
        lax.all_to_all(grad_q_pre, "seq", split_axis=0, concat_axis=1, tiled=True),
        lax.all_to_all(grad_k_pre, "seq", split_axis=0, concat_axis=1, tiled=True),
        lax.all_to_all(grad_mixed, "seq", split_axis=0, concat_axis=1, tiled=True),
    )
    grad_first = 0.5 * grad_mix_tok.astype(jnp.float32)
    grad_value_low = grad_first.astype(jnp.bfloat16)
    grad_query_w = contract_rows(normed_a, grad_q_tok)
    grad_key_w = contract_rows(normed_a, grad_k_tok)
    grad_value_w = contract_rows(normed_a, grad_value_low)
    grad_normed_a = (
        contract_cols(grad_q_tok, proj_query)
        + contract_cols(grad_k_tok, proj_key)
        + contract_cols(grad_value_low, proj_value)
    )
    grad_gain_attn = jnp.sum(grad_normed_a * input_f32 * norm_attn, axis=0)
    scaled_attn = grad_normed_a * gain_attn.astype(jnp.float32)
    grad_layer = (
        grad_after
        + norm_attn * scaled_attn
        - input_f32 * norm_attn**3 * jnp.mean(scaled_attn * input_f32, axis=-1, keepdims=True)
    )
    summed = (
        lax.psum_scatter(grad_gain_attn, ("seq", "fsdp"), scatter_dimension=0, tiled=True),
        lax.psum_scatter(grad_query_w, ("seq", "fsdp"), scatter_dimension=0, tiled=True),
        lax.psum_scatter(grad_key_w, ("seq", "fsdp"), scatter_dimension=0, tiled=True),
        lax.psum_scatter(grad_value_w, ("seq", "fsdp"), scatter_dimension=0, tiled=True),
        lax.psum_scatter(grad_out_w, ("seq", "fsdp"), scatter_dimension=0, tiled=True),
        lax.psum_scatter(grad_gain_ffn, ("seq", "fsdp"), scatter_dimension=0, tiled=True),
        lax.psum_scatter(grad_gate_w, ("seq", "fsdp"), scatter_dimension=0, tiled=True),
        lax.psum_scatter(grad_up_w, ("seq", "fsdp"), scatter_dimension=0, tiled=True),
        lax.psum_scatter(grad_down, ("seq", "fsdp"), scatter_dimension=0, tiled=True),
    )
    return (
        result,
        grad_layer,
        grad_first,
        summed[0],
        summed[1],
        summed[2],
        summed[3],
        summed[4],
        summed[5],
        summed[6],
        summed[7],
        summed[8],
    )


def solution(mesh):
    return jax.shard_map(
        per_device,
        mesh=mesh,
        in_specs=(
            P(("fsdp", "seq"), None),
            P(("fsdp", "seq"), None),
            P("fsdp"),
            P(("seq", "fsdp")),
            P(("seq", "fsdp"), None),
            P(("seq", "fsdp"), None),
            P(("seq", "fsdp"), None),
            P(("seq", "fsdp"), None),
            P(("seq", "fsdp")),
            P(("seq", "fsdp"), None),
            P(("seq", "fsdp"), None),
            P(("seq", "fsdp"), None),
            P(("fsdp", "seq"), None),
        ),
        out_specs=(
            P(("fsdp", "seq"), None),
            P(("fsdp", "seq"), None),
            P(("fsdp", "seq"), None),
            P(("seq", "fsdp")),
            P(("seq", "fsdp"), None),
            P(("seq", "fsdp"), None),
            P(("seq", "fsdp"), None),
            P(("seq", "fsdp"), None),
            P(("seq", "fsdp")),
            P(("seq", "fsdp"), None),
            P(("seq", "fsdp"), None),
            P(("seq", "fsdp"), None),
        ),
        check_vma=False,
    )
```

profile of v0, /device:TPU:0, one launch (start us, length us, event | category | flops | bytes accessed | tf_op | source)
XLA Modules:
  0.0 2050.6 jit_solution(8090032532505276813)
XLA Ops:
  11.1 42.1 %all-reduce.5 = (bf16[1024]{0:T(1024)(128)(2,1)S(1)}, bf16[1024]{0:T(1024)(128)(2,1)S(1)}) all-reduce(bf16[1024]{0:T(1024)(128)(2,1)S(1)} %dynamic-update-slice, bf16[1024]{0:T(1024)(128)(2,1)S(1)} %dynamic-update-slice.1), channel_id=1, replica_groups=mesh['seq'=4,'fsdp'=8] {'seq','fsdp'}, use_global_device_ids=true, to_apply=%add | all-reduce | flops 2048 | bytes 8192
  72.9 55.4 %all-gather.14.cloned.1.call-done = bf16[1024,1024]{1,0:T(8,128)(2,1)} async-done(((bf16[32,1024]{1,0:T(8,128)(2,1)}), bf16[1024,1024]{1,0:T(8,128)(2,1)}) %all-gather.14.cloned.1.call-update) | async-done | bytes 2097168 | tf_op jit(solution)/shard_map/all_gather | solution.py:214
  131.4 19.6 all_to_all.125
  152.0 35.2 %all-gather.10.cloned.1.call-done = bf16[1024,1024]{1,0:T(8,128)(2,1)} async-done(((bf16[32,1024]{1,0:T(8,128)(2,1)}), bf16[1024,1024]{1,0:T(8,128)(2,1)}) %all-gather.10.cloned.1.call-update) | async-done | bytes 2097168 | tf_op jit(solution)/shard_map/all_gather | solution.py:215
  189.6 18.2 all_to_all.126
  237.5 39.4 %while.51 = (s32[]{:T(128)}, f32[4,1024]{1,0:T(4,128)S(1)}, f32[4,1024]{1,0:T(4,128)S(1)}, s32[8]{0:T(128)S(1)}, s32[1024]{0:T(1024)S(1)}, /*index=5*/s32[1024]{...) while((s32[]{:T(128)}, f32[4,1024]{1,0:T(4,128)S(1)}, ...), condition=%wide.region_6.7_spmd, body=%wide.region_1.6_spmd.sunk | while | flops 573580288 | bytes 39027040 | solution.py:108
  278.5 41.0 %while.52 = (s32[]{:T(128)}, f32[1024,4,64]{0,2,1:T(8,128)}, s32[8]{0:T(128)S(1)}, s32[1024]{0:T(1024)S(1)}, s32[1024]{0:T(1024)S(1)}, /*index=5*/bf16[8192,256]...) while((s32[]{:T(128)}, f32[1024,4,64]{0,2,1:T(8,128)}, ...), condition=%wide.region_10.11_spmd, body=%wide.region_7.10_spmd.sunk | while | flops 1098122240 | bytes 7897425 | solution.py:132
  338.6 57.4 %all-gather.22.cloned.1.call-done = bf16[1024,2816]{1,0:T(8,128)(2,1)} async-done(((bf16[32,2816]{1,0:T(8,128)(2,1)}), bf16[1024,2816]{1,0:T(8,128)(2,1)}) %all-gather.22.cloned.1.call-update) | async-done | bytes 5767184 | tf_op jit(solution)/shard_map/all_gather | solution.py:218
  401.9 67.0 %all-gather.24.cloned.1.call-done = bf16[1024,2816]{1,0:T(8,128)(2,1)} async-done(((bf16[32,2816]{1,0:T(8,128)(2,1)}), bf16[1024,2816]{1,0:T(8,128)(2,1)}) %all-gather.24.cloned.1.call-update) | async-done | bytes 5767184 | tf_op jit(solution)/shard_map/all_gather | solution.py:219
  474.8 63.2 %all-gather.26.cloned.1.call-done = bf16[2816,1024]{1,0:T(8,128)(2,1)} async-done(((bf16[88,1024]{1,0:T(8,128)(2,1)}), bf16[2816,1024]{1,0:T(8,128)(2,1)}) %all-gather.26.cloned.1.call-update) | async-done | bytes 5767184 | tf_op jit(solution)/shard_map/all_gather | solution.py:220
  557.5 18.3 all_to_all.127
  589.0 86.0 %while.53 = (s32[]{:T(128)}, f32[1024,4,64]{0,2,1:T(8,128)}, f32[8192,256]{0,1:T(8,128)}, f32[8192,256]{0,1:T(8,128)}, s32[8]{0:T(128)S(1)}, /*index=5*/s32[1024...) while((s32[]{:T(128)}, f32[1024,4,64]{0,2,1:T(8,128)}, ...), condition=%wide.region_16.17_spmd, body=%wide.region_13.0_spmd.sunk | while | flops 2739143680 | bytes 170459696 | solution.py:193
  592.6 58.4 %conditional.8 = ((f32[1024,4,64]{0,2,1:T(8,128)}, f32[8192,256]{0,1:T(8,128)}, f32[8192,256]{0,1:T(8,128)})) conditional(s32[]{:T(128)} %convert_element_type.239, (f32[1024,4,64]{0,2,1:T(8,128)}, f32[8192,256]{0,1:T(8,128)}, f32[8192,256]{0,1:T(8,128)}) %tuple.166, (s32[]{:T(128)}, bf16[8192,256]{0,1:T(8,128)(2,1)}, s32[]{:T(128)}, ...), branch_computations={%region_14.14_spmd, %region_15.15_spmd} | conditional | flops 2739143680 | bytes 170459328 | solution.py:190
  692.0 272.0 %reduce-scatter.10.cloned.1.call-done = bf16[1024,256]{0,1:T(8,128)(2,1)} async-done(((bf16[8192,256]{0,1:T(8,128)(2,1)}), bf16[1024,256]{0,1:T(8,128)(2,1)}) %reduce-scatter.10.cloned.1.call-update) | async-done | bytes 524304 | tf_op jit(solution)/shard_map/reduce_scatter | solution.py:367
  966.8 18.9 all_to_all.128
  1020.3 20.4 all_to_all.130
  1083.6 38.4 %all-reduce.4 = (f32[1024]{0:T(1024)S(1)}, f32[1024]{0:T(1024)S(1)}) all-reduce(f32[1024]{0:T(1024)S(1)} %get-tuple-element.877, f32[1024]{0:T(1024)S(1)} %copy-done.23), channel_id=4, replica_groups=mesh['seq'=4,'fsdp'=8] {'seq','fsdp'}, use_global_device_ids=true, to_apply=%region_21.22.clone | all-reduce | flops 2048 | bytes 16384
  1125.7 37.9 %reduce-scatter.20.cloned.1.call-done = f32[32,1024]{1,0:T(8,128)} async-done(((f32[1024,1024]{1,0:T(8,128)}), f32[32,1024]{1,0:T(8,128)}) %reduce-scatter.20.cloned.1.call-update) | async-done | bytes 131088 | tf_op jit(solution)/shard_map/reduce_scatter | solution.py:415
  1163.5 140.3 %reduce-scatter.14.cloned.1.call-done = f32[32,1024]{1,0:T(8,128)} async-done(((f32[1024,1024]{1,0:T(8,128)}), f32[32,1024]{1,0:T(8,128)}) %reduce-scatter.14.cloned.1.call-update) | async-done | bytes 131088 | tf_op jit(solution)/shard_map/reduce_scatter | solution.py:412
  1303.8 139.6 %reduce-scatter.16.cloned.1.call-done = f32[32,1024]{1,0:T(8,128)} async-done(((f32[1024,1024]{1,0:T(8,128)}), f32[32,1024]{1,0:T(8,128)}) %reduce-scatter.16.cloned.1.call-update) | async-done | bytes 131088 | tf_op jit(solution)/shard_map/reduce_scatter | solution.py:413
  1443.4 139.4 %reduce-scatter.18.cloned.1.call-done = f32[32,1024]{1,0:T(8,128)} async-done(((f32[1024,1024]{1,0:T(8,128)}), f32[32,1024]{1,0:T(8,128)}) %reduce-scatter.18.cloned.1.call-update) | async-done | bytes 131088 | tf_op jit(solution)/shard_map/reduce_scatter | solution.py:414
  1582.8 153.6 %reduce-scatter.22.cloned.1.call-done = f32[32,2816]{1,0:T(8,128)} async-done(((f32[1024,2816]{1,0:T(8,128)}), f32[32,2816]{1,0:T(8,128)}) %reduce-scatter.22.cloned.1.call-update) | async-done | bytes 360464 | tf_op jit(solution)/shard_map/reduce_scatter | solution.py:417
  1736.4 153.4 %reduce-scatter.24.cloned.1.call-done = f32[32,2816]{1,0:T(8,128)} async-done(((f32[1024,2816]{1,0:T(8,128)}), f32[32,2816]{1,0:T(8,128)}) %reduce-scatter.24.cloned.1.call-update) | async-done | bytes 360464 | tf_op jit(solution)/shard_map/reduce_scatter | solution.py:418
  1889.8 153.5 %reduce-scatter.26.cloned.1.call-done = f32[88,1024]{1,0:T(8,128)} async-done(((f32[2816,1024]{1,0:T(8,128)}), f32[88,1024]{1,0:T(8,128)}) %reduce-scatter.26.cloned.1.call-update) | async-done | bytes 360464 | tf_op jit(solution)/shard_map/reduce_scatter | solution.py:419
  (308 shorter events, 364.3 us)
Async XLA Ops:
  7.2 62.9 %all-gather.18.cloned.1.call-start = ((), (), s32[]{:S(2)}) async-start(), calls=%async_computation.21 | async-start | bytes 2162688 | tf_op jit(solution)/shard_map/all_gather | solution.py:213
  7.9 120.3 %all-gather.14.cloned.1.call-start = ((), (), s32[]{:S(2)}) async-start(), calls=%async_computation.19 | async-start | bytes 2162688 | tf_op jit(solution)/shard_map/all_gather | solution.py:214
  8.7 178.5 %all-gather.10.cloned.1.call-start = ((), (), s32[]{:S(2)}) async-start(), calls=%async_computation.17 | async-start | bytes 2162688 | tf_op jit(solution)/shard_map/all_gather | solution.py:215
  9.4 221.6 %all-gather.16.cloned.1.call-start = ((), (), s32[]{:S(2)}) async-start(), calls=%async_computation.20 | async-start | bytes 4718592 | tf_op jit(solution)/shard_map/all_gather | solution.py:266
  152.0 125.5 %all-gather.12.cloned.1.call-start = ((), (), s32[]{:S(2)}) async-start(), calls=%async_computation.18 | async-start | bytes 4718592 | tf_op jit(solution)/shard_map/all_gather | solution.py:267
  208.8 116.8 %all-gather.20.cloned.1.call-start = ((), (), s32[]{:S(2)}) async-start(), calls=%async_computation.22 | async-start | bytes 2162688 | tf_op jit(solution)/shard_map/all_gather | solution.py:216
  209.4 186.7 %all-gather.22.cloned.1.call-start = ((), (), s32[]{:S(2)}) async-start(), calls=%async_computation.23 | async-start | bytes 5947392 | tf_op jit(solution)/shard_map/all_gather | solution.py:218
  210.1 258.8 %all-gather.24.cloned.1.call-start = ((), (), s32[]{:S(2)}) async-start(), calls=%async_computation.24 | async-start | bytes 5947392 | tf_op jit(solution)/shard_map/all_gather | solution.py:219
  210.9 327.1 %all-gather.26.cloned.1.call-start = ((), (), s32[]{:S(2)}) async-start(), calls=%async_computation.25 | async-start | bytes 5947392 | tf_op jit(solution)/shard_map/all_gather | solution.py:220
  212.4 17.7 all-to-all-start.2
  322.1 13.7 all-to-all-start.3
  325.5 638.5 %reduce-scatter.10.cloned.1.call-start = ((), (), s32[]{:S(2)}) async-start(), calls=%async_computation.26 | async-start | bytes 4718592 | tf_op jit(solution)/shard_map/reduce_scatter | solution.py:367
  338.4 217.0 %copy-start.6 = (f32[256,1024]{1,0:T(8,128)}, f32[256,1024]{1,0:T(8,128)S(1)}, u32[]{:S(2)}) copy-start(f32[256,1024]{1,0:T(8,128)S(1)} %get-tuple-element.975) | copy-start | bytes 3145732
  681.1 338.0 %reduce-scatter.12.cloned.1.call-start = ((), (), s32[]{:S(2)}) async-start(), calls=%async_computation.27 | async-start | bytes 4718592 | tf_op jit(solution)/shard_map/reduce_scatter | solution.py:370
  687.2 476.3 %reduce-scatter.20.cloned.1.call-start = ((), (), s32[]{:S(2)}) async-start(), calls=%async_computation.31 | async-start | bytes 4325376 | tf_op jit(solution)/shard_map/reduce_scatter | solution.py:415
  690.0 613.8 %reduce-scatter.14.cloned.1.call-start = ((), (), s32[]{:S(2)}) async-start(), calls=%async_computation.28 | async-start | bytes 4325376 | tf_op jit(solution)/shard_map/reduce_scatter | solution.py:412
  691.9 293.8 %copy-start.2 = (bf16[256,1024]{1,0:T(8,128)(2,1)S(1)}, bf16[256,1024]{1,0:T(8,128)(2,1)}, u32[]{:S(2)}) copy-start(bf16[256,1024]{1,0:T(8,128)(2,1)} %param.25) | copy-start | bytes 1572868
  691.9 293.8 %copy-start.17 = (f32[1024]{0:T(1024)S(1)}, f32[1024]{0:T(1024)}, u32[]{:S(2)}) copy-start(f32[1024]{0:T(1024)} %copy-done.16) | copy-start | bytes 12292
  691.9 293.8 %copy-start.19 = (f32[256]{0:T(256)S(1)}, f32[256]{0:T(256)}, u32[]{:S(2)}) copy-start(f32[256]{0:T(256)} %copy-done.18) | copy-start | bytes 3076
  988.6 454.8 %reduce-scatter.16.cloned.1.call-start = ((), (), s32[]{:S(2)}) async-start(), calls=%async_computation.29 | async-start | bytes 4325376 | tf_op jit(solution)/shard_map/reduce_scatter | solution.py:413
  1009.7 573.1 %reduce-scatter.18.cloned.1.call-start = ((), (), s32[]{:S(2)}) async-start(), calls=%async_computation.30 | async-start | bytes 4325376 | tf_op jit(solution)/shard_map/reduce_scatter | solution.py:414
  1046.7 689.6 %reduce-scatter.22.cloned.1.call-start = ((), (), s32[]{:S(2)}) async-start(), calls=%async_computation.32 | async-start | bytes 11894784 | tf_op jit(solution)/shard_map/reduce_scatter | solution.py:417
  1054.2 835.6 %reduce-scatter.24.cloned.1.call-start = ((), (), s32[]{:S(2)}) async-start(), calls=%async_computation.33 | async-start | bytes 11894784 | tf_op jit(solution)/shard_map/reduce_scatter | solution.py:418
  1061.7 981.6 %reduce-scatter.26.cloned.1.call-start = ((), (), s32[]{:S(2)}) async-start(), calls=%async_computation.34 | async-start | bytes 11894784 | tf_op jit(solution)/shard_map/reduce_scatter | solution.py:419
  (25 other events, 989.1 us)
Sparse Core Ops, SparseCore 0:
  10.9 59.1 all-gather.17
  72.9 55.2 all-gather.13
  131.1 56.0 all-gather.9
  189.5 35.5 all-gather.15
  227.4 36.7 all-gather.11
  266.9 56.3 all-gather.19
  326.1 69.8 all-gather.21
  398.9 69.9 all-gather.23
  471.7 66.2 all-gather.25
  681.2 282.7 reduce-scatter.9
  967.7 51.3 reduce-scatter.11
  1021.8 141.6 reduce-scatter.19
  1166.4 137.3 reduce-scatter.13
  1306.5 136.8 reduce-scatter.15
  1446.1 136.6 reduce-scatter.17
  1585.5 150.7 reduce-scatter.21
  1739.1 150.6 reduce-scatter.23
  1892.5 150.7 reduce-scatter.25
where the time goes:
time: 2060 us; the launch traced here: 2050 us
  waiting for transfers between devices  1520 us (74%)
  blocking collectives  192 us (9%)
  matrix products  136 us (7%)
  local copies, waits for them, and re-layouts  90.8 us (4%)
  loops' own time  49 us (2%)
  other arithmetic  39.9 us (2%)
    reduce_scatter x1, waiting for transfers between devices, per_device(): lax.psum_scatter(key_grads.astype(jnp.bfloat16), 'fsdp', scatter_dimensio...  272 us
    reduce_scatter x1, waiting for transfers between devices, per_device(): lax.psum_scatter(grad_gate_w, ('seq', 'fsdp'), scatter_dimension=0, tiled...  154 us
    reduce_scatter x1, waiting for transfers between devices, per_device(): lax.psum_scatter(grad_down, ('seq', 'fsdp'), scatter_dimension=0, tiled=T...  154 us
    reduce_scatter x1, waiting for transfers between devices, per_device(): lax.psum_scatter(grad_up_w, ('seq', 'fsdp'), scatter_dimension=0, tiled=T...  153 us
    reduce_scatter x1, waiting for transfers between devices, per_device(): lax.psum_scatter(grad_query_w, ('seq', 'fsdp'), scatter_dimension=0, tile...  140 us
    reduce_scatter x1, waiting for transfers between devices, per_device(): lax.psum_scatter(grad_key_w, ('seq', 'fsdp'), scatter_dimension=0, tiled=...  140 us
    reduce_scatter x1, waiting for transfers between devices, per_device(): lax.psum_scatter(grad_value_w, ('seq', 'fsdp'), scatter_dimension=0, tile...  139 us
    unnamed x2, blocking collectives  80.4 us
  transfers between devices with their start and end apart: 20, of which 17 were waited for; matrix products, arithmetic and copies ran while one was open for 8% of the time, Pallas kernels for 0%

commit v1 on v0

--- a/solution.py
+++ b/solution.py
@@ -1,6 +1,9 @@
+import functools, math
 import jax
 import jax.numpy as jnp
 from jax import lax
+from jax.experimental import pallas as pl
+from jax.experimental.pallas import tpu as pltpu
 from jax.sharding import PartitionSpec as P
 
 HEADS = 16
@@ -193,6 +196,444 @@
     return lax.scan(step_back, start_state, numbers)[0]
 
 
+MESH = pl.DeviceIdType.MESH
+
+
+class Grid:
+    def __init__(self):
+        self.seq = lax.axis_size("seq")
+        self.fsdp = lax.axis_size("fsdp")
+        self.size = {"z": self.seq, "y": 2, "x": self.fsdp // 4}
+        self.stride = {"x": 2, "y": 2 * (self.fsdp // 4)}
+        self.total = self.seq * self.fsdp
+        self.plane = self.total // 2
+
+    def locate(self):
+        z, f = lax.axis_index("seq"), lax.axis_index("fsdp")
+        nx = self.size["x"]
+        self.f, self.zi = f, z
+        self.core = lax.rem(f, 2)
+        self.me = {"z": z, "y": lax.div(f, 2 * nx), "x": lax.rem(lax.div(f, 2), nx)}
+
+    def step(self, dim, delta):
+        if dim == "z":
+            return {"seq": self.zi + delta}
+        if dim == "core":
+            return {"fsdp": self.f + 1 - 2 * self.core}
+        return {"fsdp": self.f + delta * self.stride[dim]}
+
+    def partner(self, dim):
+        return self.step(dim, 1 - 2 * self.me[dim])
+
+    def dirs(self, dim):
+        return (0,) if self.size[dim] == 2 else (1, -1)
+
+    def linear(self, at, core):
+        nx = self.size["x"]
+        return at["z"] * self.fsdp + (at["y"] * nx + at["x"]) * 2 + core
+
+    def neighbours(self):
+        found = [(None, self.step("core", 1))]
+        for dim in ("z", "y", "x"):
+            n = self.size[dim]
+            if n == 1:
+                continue
+            if n == 2:
+                found.append((None, self.partner(dim)))
+            else:
+                found.append((self.me[dim] < n - 1, self.step(dim, 1)))
+                found.append((self.me[dim] > 0, self.step(dim, -1)))
+        return found
+
+    def barrier(self):
+        sem = pltpu.get_barrier_semaphore()
+        count = 0
+        for exists, device in self.neighbours():
+            if exists is None:
+                pl.semaphore_signal(sem, inc=1, device_id=device, device_id_type=MESH)
+                count = count + 1
+            else:
+
+                @pl.when(exists)
+                def _(device=device):
+                    pl.semaphore_signal(sem, inc=1, device_id=device, device_id_type=MESH)
+
+                count = count + exists.astype(jnp.int32)
+        pl.semaphore_wait(sem, count)
+
+    def digits(self, order, number):
+        at, ok = {}, None
+        rest = number
+        for dim in order:
+            n = self.size[dim]
+            base = 2 if n == 2 else 2 * n - 1
+            digit = lax.rem(rest, base)
+            rest = lax.div(rest, base)
+            if n == 2:
+                at[dim] = lax.rem(self.me[dim] + digit, 2)
+            elif n == 1:
+                at[dim] = self.me[dim]
+            else:
+                away = lax.div(digit + 1, 2)
+                at[dim] = jnp.where(lax.rem(digit, 2) == 1, self.me[dim] - away, self.me[dim] + away)
+                inside = (at[dim] >= 0) & (at[dim] < n)
+                ok = inside if ok is None else ok & inside
+        return at, ok
+
+    def places(self, order):
+        return math.prod(2 if self.size[d] == 2 else 2 * self.size[d] - 1 for d in order)
+
+    def rank(self, order, at, upto):
+        value, width = 0, 1
+        for dim in order[:upto]:
+            value = value + at[dim] * width
+            width *= self.size[dim]
+        return value
+
+    def slots(self, order):
+        first, count, width = [], 0, 1
+        for dim in order:
+            width *= self.size[dim]
+            first.append(count)
+            if self.size[dim] > 1:
+                count += width * len(self.dirs(dim))
+        return first, count
+
+    def branch(self, order, j, way, at):
+        dim = order[j]
+        n = self.size[dim]
+        ok = None
+        for later in order[j + 1 :]:
+            same = at[later] == self.me[later]
+            ok = same if ok is None else ok & same
+        if n == 2:
+            here = at[dim] == self.me[dim]
+        elif way == 1:
+            here = (at[dim] <= self.me[dim]) & (self.me[dim] < n - 1)
+        else:
+            here = (at[dim] >= self.me[dim]) & (self.me[dim] > 0)
+        return here if ok is None else ok & here
+
+
+ORDERS = {"A": ("z", "x", "y"), "B": ("x", "y", "z"), "C": ("y", "z", "x")}
+
+
+def gather_kernel(pieces, n_arrays, *refs):
+    sources, outs = refs[:n_arrays], refs[n_arrays : 2 * n_arrays]
+    recv, send, core_send, own_sem = refs[2 * n_arrays :]
+    grid = Grid()
+    grid.locate()
+    mine = grid.linear(grid.me, grid.core)
+    own = [
+        pltpu.make_async_copy(sources[i], outs[i].at[mine], own_sem.at[i]) for i in range(n_arrays)
+    ]
+    for copy in own:
+        copy.start()
+    grid.barrier()
+
+    def view(ref, piece):
+        return ref.at[:, pl.ds(piece[1], piece[2])]
+
+    def sends(p, at, source, act):
+        array, _, _, scheme = pieces[p]
+        order = ORDERS[scheme]
+        first, _ = grid.slots(order)
+        number = grid.linear(at, grid.core)
+        target = view(outs[array].at[number], pieces[p])
+        for j, dim in enumerate(order):
+            if grid.size[dim] == 1:
+                continue
+            ways = grid.dirs(dim)
+            for w, way in enumerate(ways):
+                slot = first[j] + grid.rank(order, at, j + 1) * len(ways) + w
+                device = grid.partner(dim) if way == 0 else grid.step(dim, way)
+
+                @pl.when(grid.branch(order, j, way, at))
+                def _(device=device, slot=slot):
+                    act(
+                        pltpu.make_async_remote_copy(
+                            src_ref=source,
+                            dst_ref=target,
+                            send_sem=send.at[p, slot],
+                            recv_sem=recv.at[p, number],
+                            device_id=device,
+                            device_id_type=MESH,
+                        )
+                    )
+
+        act(
+            pltpu.make_async_remote_copy(
+                src_ref=source,
+                dst_ref=target,
+                send_sem=core_send.at[p, grid.rank(order, at, 3)],
+                recv_sem=recv.at[p, number],
+                device_id=grid.step("core", 1),
+                device_id_type=MESH,
+            )
+        )
+
+    def arrival(p, number):
+        array = pieces[p][0]
+        there = view(outs[array].at[number], pieces[p])
+        return pltpu.make_async_remote_copy(
+            src_ref=there,
+            dst_ref=there,
+            send_sem=core_send.at[p, 0],
+            recv_sem=recv.at[p, number],
+            device_id=grid.step("core", 1),
+            device_id_type=MESH,
+        )
+
+    for p in range(len(pieces)):
+        sends(p, grid.me, view(sources[pieces[p][0]], pieces[p]), lambda copy: copy.start())
+
+    def forward(number, carry):
+        for p in range(len(pieces)):
+            at, ok = grid.digits(ORDERS[pieces[p][3]], number)
+
+            def relay(p=p, at=at):
+                where = grid.linear(at, grid.core)
+                arrival(p, where).wait_recv()
+                sends(p, at, view(outs[pieces[p][0]].at[where], pieces[p]), lambda copy: copy.start())
+
+            if ok is None:
+                relay()
+            else:
+                pl.when(ok)(relay)
+        return carry
+
+    lax.fori_loop(1, grid.places(ORDERS["A"]), forward, 0)
+
+    def finish(number, carry):
+        for p in range(len(pieces)):
+            at, ok = grid.digits(ORDERS[pieces[p][3]], number)
+
+            def drain(p=p, at=at):
+                arrival(p, grid.linear(at, 1 - grid.core)).wait_recv()
+                where = grid.linear(at, grid.core)
+                sends(
+                    p, at, view(outs[pieces[p][0]].at[where], pieces[p]), lambda copy: copy.wait_send()
+                )
+
+            if ok is None:
+                drain()
+            else:
+                pl.when(ok)(drain)
+        return carry
+
+    lax.fori_loop(0, grid.places(ORDERS["A"]), finish, 0)
+    for copy in own:
+        copy.wait()
+
+
+def gather_all(arrays, pieces, ident):
+    grid = Grid()
+    n = len(arrays)
+    slots = max(grid.slots(order)[1] for order in ORDERS.values())
+    moved = sum(a.size * a.dtype.itemsize for a in arrays) * grid.total
+    return pl.pallas_call(
+        functools.partial(gather_kernel, pieces, n),
+        out_shape=[jax.ShapeDtypeStruct((grid.total, *a.shape), a.dtype) for a in arrays],
+        in_specs=[pl.BlockSpec(memory_space=pl.ANY)] * n,
+        out_specs=[pl.BlockSpec(memory_space=pl.ANY)] * n,
+        scratch_shapes=[
+            pltpu.SemaphoreType.DMA((len(pieces), grid.total)),
+            pltpu.SemaphoreType.DMA((len(pieces), slots)),
+            pltpu.SemaphoreType.DMA((len(pieces), grid.plane)),
+            pltpu.SemaphoreType.DMA((n,)),
+        ],
+        compiler_params=pltpu.CompilerParams(collective_id=ident, has_side_effects=True),
+        cost_estimate=pl.CostEstimate(flops=0, bytes_accessed=moved, transcendentals=0),
+    )(*arrays)
+
+
+def reduce_kernel(pieces, n_arrays, *refs):
+    parts, outs = refs[:n_arrays], refs[n_arrays : 2 * n_arrays]
+    rest = list(refs[2 * n_arrays :])
+    n = len(pieces)
+    pair, slot_of, own, total = rest[:n], rest[n : 2 * n], rest[2 * n : 3 * n], rest[3 * n : 4 * n]
+    core_send, core_recv, tree_send, tree_recv, own_sem = rest[4 * n :]
+    grid = Grid()
+    grid.locate()
+    grid.barrier()
+    places = grid.places(ORDERS["A"])
+
+    def each(number, act):
+        for p in range(n):
+            at, ok = grid.digits(ORDERS[pieces[p][3]], number)
+
+            def run(p=p, at=at):
+                act(p, at)
+
+            if ok is None:
+                run()
+            else:
+                pl.when(ok)(run)
+
+    def block(p, at, core):
+        array, lower, count, _ = pieces[p]
+        return parts[array].at[grid.linear(at, core), :, pl.ds(lower, count)]
+
+    def to_sibling(p, at):
+        rank = grid.rank(ORDERS[pieces[p][3]], at, 3)
+        return pltpu.make_async_remote_copy(
+            src_ref=block(p, at, 1 - grid.core),
+            dst_ref=pair[p].at[rank],
+            send_sem=core_send.at[p, rank],
+            recv_sem=core_recv.at[p, rank],
+            device_id=grid.step("core", 1),
+            device_id_type=MESH,
+        )
+
+    def fetch(p, at, number):
+        slot = lax.rem(number, 2)
+        return pltpu.make_async_copy(
+            block(p, at, grid.core), own[p].at[slot], own_sem.at[p, slot]
+        )
+
+    def to_parent(p, at, act):
+        order = ORDERS[pieces[p][3]]
+        first, _ = grid.slots(order)
+        rank = grid.rank(order, at, 3)
+        for j, dim in enumerate(order):
+            if grid.size[dim] == 1:
+                continue
+            ways = grid.dirs(dim)
+            ok = None
+            for later in order[j + 1 :]:
+                same = at[later] == grid.me[later]
+                ok = same if ok is None else ok & same
+            for w, way in enumerate(ways):
+                slot = first[j] + grid.rank(order, at, j + 1) * len(ways) + w
+                if way == 0:
+                    here, device = at[dim] != grid.me[dim], grid.partner(dim)
+                elif way == 1:
+                    here, device = at[dim] < grid.me[dim], grid.step(dim, -1)
+                else:
+                    here, device = at[dim] > grid.me[dim], grid.step(dim, 1)
+                here = here if ok is None else ok & here
+
+                @pl.when(here)
+                def _(slot=slot, device=device):
+                    act(
+                        pltpu.make_async_remote_copy(
+                            src_ref=pair[p].at[rank],
+                            dst_ref=slot_of[p].at[slot],
+                            send_sem=tree_send.at[p, rank],
+                            recv_sem=tree_recv.at[p, slot],
+                            device_id=device,
+                            device_id_type=MESH,
+                        )
+                    )
+
+    def combine(p, at, number):
+        order = ORDERS[pieces[p][3]]
+        first, _ = grid.slots(order)
+        rank = grid.rank(order, at, 3)
+        to_sibling(p, at).wait_recv()
+        fetch(p, at, number).wait()
+        total[p][...] = own[p][lax.rem(number, 2)].astype(jnp.float32) + pair[p][rank].astype(
+            jnp.float32
+        )
+        for j in reversed(range(3)):
+            dim = order[j]
+            if grid.size[dim] == 1:
+                continue
+            ways = grid.dirs(dim)
+            for w, way in enumerate(ways):
+                slot = first[j] + grid.rank(order, at, j + 1) * len(ways) + w
+
+                @pl.when(grid.branch(order, j, way, at))
+                def _(slot=slot):
+                    pltpu.make_async_remote_copy(
+                        src_ref=slot_of[p].at[slot],
+                        dst_ref=slot_of[p].at[slot],
+                        send_sem=tree_send.at[p, rank],
+                        recv_sem=tree_recv.at[p, slot],
+                        device_id=grid.step("core", 1),
+                        device_id_type=MESH,
+                    ).wait_recv()
+                    total[p][...] += slot_of[p][slot].astype(jnp.float32)
+
+    def start_all(step, carry):
+        each(places - 1 - step, lambda p, at: to_sibling(p, at).start())
+        return carry
+
+    each(places - 1, lambda p, at: fetch(p, at, places - 1).start())
+    lax.fori_loop(0, places, start_all, 0)
+
+    def climb(step, carry):
+        number = places - 1 - step
+        each(number - 1, lambda p, at: fetch(p, at, number - 1).start())
+
+        def work(p, at):
+            combine(p, at, number)
+            rank = grid.rank(ORDERS[pieces[p][3]], at, 3)
+            pair[p][rank] = total[p][...].astype(pair[p].dtype)
+            to_parent(p, at, lambda copy: copy.start())
+
+        each(number, work)
+        return carry
+
+    lax.fori_loop(0, places - 1, climb, 0)
+
+    def root(p, at):
+        combine(p, at, 0)
+        array, lower, count, _ = pieces[p]
+        outs[array][:, lower : lower + count] = total[p][...]
+
+    each(0, root)
+
+    def finish(step, carry):
+        number = places - 1 - step
+
+        def drain(p, at):
+            to_sibling(p, at).wait_send()
+
+            @pl.when(number > 0)
+            def _():
+                to_parent(p, at, lambda copy: copy.wait_send())
+
+        each(number, drain)
+        return carry
+
+    lax.fori_loop(0, places, finish, 0)
+
+
+def reduce_all(arrays, pieces, ident):
+    grid = Grid()
+    n = len(arrays)
+    most = max(grid.slots(order)[1] for order in ORDERS.values())
+    moved = sum(a.size * a.dtype.itemsize for a in arrays)
+    shape = [(arrays[p[0]].shape[1], p[2]) for p in pieces]
+    kind = [arrays[p[0]].dtype for p in pieces]
+    count = [grid.slots(ORDERS[p[3]])[1] for p in pieces]
+    return pl.pallas_call(
+        functools.partial(reduce_kernel, pieces, n),
+        out_shape=[jax.ShapeDtypeStruct(a.shape[1:], jnp.float32) for a in arrays],
+        in_specs=[pl.BlockSpec(memory_space=pl.ANY)] * n,
+        out_specs=[pl.BlockSpec(memory_space=pltpu.VMEM)] * n,
+        scratch_shapes=[pltpu.VMEM((grid.plane, *s), k) for s, k in zip(shape, kind)]
+        + [pltpu.VMEM((c, *s), k) for c, s, k in zip(count, shape, kind)]
+        + [pltpu.VMEM((2, *s), k) for s, k in zip(shape, kind)]
+        + [pltpu.VMEM(s, jnp.float32) for s in shape]
+        + [
+            pltpu.SemaphoreType.DMA((len(pieces), grid.plane)),
+            pltpu.SemaphoreType.DMA((len(pieces), grid.plane)),
+            pltpu.SemaphoreType.DMA((len(pieces), grid.plane)),
+            pltpu.SemaphoreType.DMA((len(pieces), most)),
+            pltpu.SemaphoreType.DMA((len(pieces), 2)),
+        ],
+        compiler_params=pltpu.CompilerParams(
+            collective_id=ident, has_side_effects=True, vmem_limit_bytes=60 << 20
+        ),
+        cost_estimate=pl.CostEstimate(flops=0, bytes_accessed=2 * moved, transcendentals=0),
+    )(*arrays)
+
+
+SCHEMES = ("A", "A", "A", "B", "C", "C", "C", "C")
+
+
 def per_device(
     layer_input,
     v_first,
@@ -208,28 +649,17 @@
     w_down,
     out_cot,
 ):
-    gathered = (
-        lax.all_gather(g_attn, ("seq", "fsdp"), axis=0, tiled=True),
-        lax.all_gather(w_query, ("seq", "fsdp"), axis=0, tiled=True),
-        lax.all_gather(w_key, ("seq", "fsdp"), axis=0, tiled=True),
-        lax.all_gather(w_value, ("seq", "fsdp"), axis=0, tiled=True),
-        lax.all_gather(w_out, ("seq", "fsdp"), axis=0, tiled=True),
-        lax.all_gather(g_ffn, ("seq", "fsdp"), axis=0, tiled=True),
-        lax.all_gather(w_gate, ("seq", "fsdp"), axis=0, tiled=True),
-        lax.all_gather(w_up, ("seq", "fsdp"), axis=0, tiled=True),
-        lax.all_gather(w_down, ("seq", "fsdp"), axis=0, tiled=True),
-    )
-    (
-        gain_attn,
-        proj_query,
-        proj_key,
-        proj_value,
-        proj_out,
-        gain_ffn,
-        proj_gate,
-        proj_up,
-        proj_down,
-    ) = gathered
+    gains = jnp.zeros((16, 128), jnp.bfloat16)
+    gains = lax.dynamic_update_slice(gains, g_attn[None], (0, 0))
+    gains = lax.dynamic_update_slice(gains, g_ffn[None], (1, 0))
+    shards = (w_gate, w_up, w_query, w_key, w_down, w_value, w_out, gains)
+    pieces = [(i, 0, shard.shape[1], scheme) for i, (shard, scheme) in enumerate(zip(shards, SCHEMES))]
+    *wholes, whole_gains = gather_all(shards, pieces, 0)
+    proj_gate, proj_up, proj_query, proj_key, proj_down, proj_value, proj_out = (
+        whole.reshape(-1, whole.shape[2]) for whole in wholes
+    )
+    gain_attn = whole_gains[:, 0, : g_attn.shape[0]].reshape(-1)
+    gain_ffn = whole_gains[:, 1, : g_ffn.shape[0]].reshape(-1)
     tokens = layer_input.shape[0]
     group_size = lax.axis_size("seq")
     group_rows = tokens * group_size
@@ -298,28 +728,6 @@
     silu_gate = gate_act * sigmoid_gate
     hidden = (silu_gate * up_act).astype(jnp.bfloat16)
     result = (after_attn + matmul(hidden, proj_down)).astype(jnp.bfloat16)
-    regathered = (
-        lax.all_gather(g_attn, ("seq", "fsdp"), axis=0, tiled=True),
-        lax.all_gather(w_query, ("seq", "fsdp"), axis=0, tiled=True),
-        lax.all_gather(w_key, ("seq", "fsdp"), axis=0, tiled=True),
-        lax.all_gather(w_value, ("seq", "fsdp"), axis=0, tiled=True),
-        lax.all_gather(w_out, ("seq", "fsdp"), axis=0, tiled=True),
-        lax.all_gather(g_ffn, ("seq", "fsdp"), axis=0, tiled=True),
-        lax.all_gather(w_gate, ("seq", "fsdp"), axis=0, tiled=True),
-        lax.all_gather(w_up, ("seq", "fsdp"), axis=0, tiled=True),
-        lax.all_gather(w_down, ("seq", "fsdp"), axis=0, tiled=True),
-    )
-    (
-        gain_attn,
-        proj_query,
-        proj_key,
-        proj_value,
-        proj_out,
-        gain_ffn,
-        proj_gate,
-        proj_up,
-        proj_down,
-    ) = regathered
     grad_down = contract_rows(hidden, out_cot)
     grad_hidden = contract_cols(out_cot, proj_down)
     grad_gate_low = (
@@ -407,30 +815,31 @@
         + norm_attn * scaled_attn
         - input_f32 * norm_attn**3 * jnp.mean(scaled_attn * input_f32, axis=-1, keepdims=True)
     )
-    summed = (
-        lax.psum_scatter(grad_gain_attn, ("seq", "fsdp"), scatter_dimension=0, tiled=True),
-        lax.psum_scatter(grad_query_w, ("seq", "fsdp"), scatter_dimension=0, tiled=True),
-        lax.psum_scatter(grad_key_w, ("seq", "fsdp"), scatter_dimension=0, tiled=True),
-        lax.psum_scatter(grad_value_w, ("seq", "fsdp"), scatter_dimension=0, tiled=True),
-        lax.psum_scatter(grad_out_w, ("seq", "fsdp"), scatter_dimension=0, tiled=True),
-        lax.psum_scatter(grad_gain_ffn, ("seq", "fsdp"), scatter_dimension=0, tiled=True),
-        lax.psum_scatter(grad_gate_w, ("seq", "fsdp"), scatter_dimension=0, tiled=True),
-        lax.psum_scatter(grad_up_w, ("seq", "fsdp"), scatter_dimension=0, tiled=True),
-        lax.psum_scatter(grad_down, ("seq", "fsdp"), scatter_dimension=0, tiled=True),
-    )
+    devices = lax.axis_size("seq") * lax.axis_size("fsdp")
+    terms = [
+        grad.astype(jnp.bfloat16).reshape(devices, -1, grad.shape[1])
+        for grad in (grad_gate_w, grad_up_w, grad_query_w, grad_key_w, grad_down, grad_value_w, grad_out_w)
+    ]
+    gain_terms = jnp.zeros((devices, 8, 128), jnp.float32)
+    for row, grad in enumerate((grad_gain_attn, grad_gain_ffn)):
+        gain_terms = lax.dynamic_update_slice(
+            gain_terms, grad.reshape(devices, 1, -1), (0, row, 0)
+        )
+    sums = reduce_all([*terms, gain_terms], pieces, 1)
+    sum_gate, sum_up, sum_query, sum_key, sum_down, sum_value, sum_out, sum_gains = sums
     return (
         result,
         grad_layer,
         grad_first,
-        summed[0],
-        summed[1],
-        summed[2],
-        summed[3],
-        summed[4],
-        summed[5],
-        summed[6],
-        summed[7],
-        summed[8],
+        sum_gains[0, : g_attn.shape[0]],
+        sum_query,
+        sum_key,
+        sum_value,
+        sum_out,
+        sum_gains[1, : g_ffn.shape[0]],
+        sum_gate,
+        sum_up,
+        sum_down,
     )
 
 

time: 2060 us -> 1050 us (0.51)
  waiting for transfers between devices: 1520 us -> 430 us
  Pallas kernels: 0 us -> 226 us
  blocking collectives: 192 us -> 35.2 us
  matrix products: 136 us -> 110 us
    reduce_scatter x7 -> x0, waiting for transfers between devices: 918 us -> none  [the longest x1 154 us: per_device(): lax.psum_scatter(grad_gate_w, ('seq', 'fsdp'), scatter_dimension=0, tiled...]
    reduce_scatter x1, waiting for transfers between devices: 9.36 us -> 351 us  [per_device(): lax.psum_scatter(value_grads.astype(jnp.bfloat16), 'fsdp', scatter_dimens...]
    all_gather x7 -> x0, waiting for transfers between devices: 292 us -> none  [the longest x1 67 us: per_device(): lax.all_gather(w_up, ('seq', 'fsdp'), axis=0, tiled=True)]
    reduce_scatter x1, waiting for transfers between devices: 272 us -> 37.6 us  [per_device(): lax.psum_scatter(key_grads.astype(jnp.bfloat16), 'fsdp', scatter_dimensio...]
    pallas_call x0 -> x2, Pallas kernels: none -> 226 us  [the longest x1 118 us: reduce_all(): pl.pallas_call(functools.partial(reduce_kernel, pieces, n), out_shape=[ja...]
    unnamed x2 -> x0, blocking collectives: 80.4 us -> none
    all_to_all x4 -> x0, blocking collectives: 74.1 us -> none  [the longest x1 20.4 us: per_device(): lax.all_to_all(grad_mixed, 'seq', split_axis=0, concat_axis=1, tiled=True)]
  transfers between devices with their start and end apart: 20 -> 10, of which waited for: 17 -> 7; matrix products, arithmetic and copies ran while one was open for 8% -> 8% of each run, Pallas kernels for 0% -> 0%
where the time goes in v1:
time: 1050 us; the launch traced here: 1040 us
  waiting for transfers between devices  430 us (41%)
  Pallas kernels  226 us (22%)
  matrix products  110 us (10%)
  local copies, waits for them, and re-layouts  108 us (10%)
  loops' own time  50.7 us (5%)
  other arithmetic  43.1 us (4%)
  blocking collectives  35.2 us (3%)
  starting transfers between devices  24.9 us (2%)
  between operations  14.8 us (1%)
    reduce_scatter x1, waiting for transfers between devices, per_device(): lax.psum_scatter(value_grads.astype(jnp.bfloat16), 'fsdp', scatter_dimens...  351 us
    pallas_call x1, Pallas kernels, reduce_all(): pl.pallas_call(functools.partial(reduce_kernel, pieces, n), out_shape=[ja...  118 us
    pallas_call x1, Pallas kernels, gather_all(): pl.pallas_call(functools.partial(gather_kernel, pieces, n), out_shape=[ja...  108 us
    reduce_scatter x1, waiting for transfers between devices, per_device(): lax.psum_scatter(key_grads.astype(jnp.bfloat16), 'fsdp', scatter_dimensio...  37.6 us
    slice x48, local copies, waits for them, and re-layouts, is_live(): return (k_first <= q_pos[-1]) & (k_first + count - 1 >= q_begin[0])  26.6 us
    dot_general x7, matrix products, contract_rows(): lax.dot_general(left, right, (((0,), (0,)), ((), ())), preferred_element_...  23.5 us
    dot_general x7, matrix products, matmul(): return jnp.dot(left, right, preferred_element_type=jnp.float32)  21.9 us
  transfers between devices with their start and end apart: 10, of which 7 were waited for; matrix products, arithmetic and copies ran while one was open for 8% of the time, Pallas kernels for 0%

profile of v1, /device:TPU:0, one launch (start us, length us, event | category | flops | bytes accessed | tf_op | source)
XLA Modules:
  0.0 1042.9 jit_solution(8089142278787089784)
XLA Ops:
  9.3 107.7 %shard_map.220 = (bf16[32,32,2816]{2,1,0:T(8,128)(2,1)}, bf16[32,32,2816]{2,1,0:T(8,128)(2,1)}, bf16[32,32,1024]{2,1,0:T(8,128)(2,1)}, bf16[32,32,1024]{2,1,0:T(...) custom-call(bf16[32,2816]{1,0:T(8,128)(2,1)} %refs_0_.1, ...), custom_call_target="tpu_custom_call" | custom-call | bytes 25821184 | tf_op jit(solution)/shard_map/pallas_call | solution.py:434
  134.1 19.3 %all_to_all.125 = bf16[256,4,256]{0,2,1:T(8,128)(2,1)S(1)} all-to-all(bf16[256,4,256]{0,2,1:T(8,128)(2,1)S(1)} %bitcast.251), channel_id=1, replica_groups=mesh['seq'=4,'fsdp'=8] {'seq'}, dimensions={1} | all-to-all | bytes 1048576 | tf_op jit(solution)/shard_map/all_to_all | solution.py:692
  156.8 15.9 %all_to_all.126 = bf16[256,4,256]{2,0,1:T(8,128)(2,1)S(1)} all-to-all(bf16[256,4,256]{2,0,1:T(8,128)(2,1)S(1)} %bitcast.253), channel_id=1, replica_groups=mesh['seq'=4,'fsdp'=8] {'seq'}, dimensions={1} | all-to-all | bytes 1048576 | tf_op jit(solution)/shard_map/all_to_all | solution.py:693
  179.2 12.9 %all-to-all-done.2 = bf16[256,4,256]{0,2,1:T(8,128)(2,1)S(1)} async-done(((bf16[256,4,256]{0,2,1:T(8,128)(2,1)}), bf16[256,4,256]{0,2,1:T(8,128)(2,1)S(1)}, u32[]{:S(2)}, u32[]{:S(2)}) %all-to-all-start.2) | async-done | bytes 524320 | tf_op jit(solution)/shard_map/all_to_all | solution.py:691
  192.9 39.4 %while.51 = (s32[]{:T(128)}, f32[4,1024]{1,0:T(4,128)S(1)}, f32[4,1024]{1,0:T(4,128)S(1)}, s32[8]{0:T(128)S(1)}, s32[1024]{0:T(1024)S(1)}, /*index=5*/s32[1024]{...) while((s32[]{:T(128)}, f32[4,1024]{1,0:T(4,128)S(1)}, ...), condition=%wide.region_6.7_spmd, body=%wide.region_1.6_spmd.sunk | while | flops 573580288 | bytes 39027040 | solution.py:111
  196.5 10.0 conditional.6
  233.5 40.9 %while.52 = (s32[]{:T(128)}, f32[1024,4,64]{0,2,1:T(8,128)}, s32[8]{0:T(128)S(1)}, s32[1024]{0:T(1024)S(1)}, s32[1024]{0:T(1024)S(1)}, /*index=5*/bf16[8192,256]...) while((s32[]{:T(128)}, f32[1024,4,64]{0,2,1:T(8,128)}, ...), condition=%wide.region_10.11_spmd, body=%wide.region_7.10_spmd.sunk | while | flops 1098122240 | bytes 7897425 | solution.py:135
  237.3 11.3 %conditional.7 = (f32[1024,4,64]{0,2,1:T(8,128)}) conditional(s32[]{:T(128)} %convert_element_type.313, f32[1024,4,64]{0,2,1:T(8,128)} %get-tuple-element.1186, (s32[]{:T(128)}, bf16[8192,256]{0,1:T(8,128)(2,1)}, s32[]{:T(128)}, s32[1024]{0:T(1024)S(1)}, s32[1024]{0:T(1024)S(1)}, /*index=5*/bf16[8192,256]{0,1:T(8,128)(2,1)}, ...), branch_computations={%region_8.8_spmd, %region_9.9_spmd} | conditional | flops 1098122240 | bytes 7897150 | solution.py:133
  240.1 8.5 fusion.7
  280.7 10.2 all-to-all-done.3
  315.1 10.2 all-to-all-done.4
  338.5 88.7 %while.53 = (s32[]{:T(128)}, f32[1024,4,64]{0,2,1:T(8,128)}, f32[8192,256]{0,1:T(8,128)}, f32[8192,256]{0,1:T(8,128)}, s32[8]{0:T(128)S(1)}, /*index=5*/s32[1024...) while((s32[]{:T(128)}, f32[1024,4,64]{0,2,1:T(8,128)}, ...), condition=%wide.region_16.17_spmd, body=%wide.region_13.0_spmd.sunk | while | flops 2739143680 | bytes 170459696 | solution.py:196
  342.6 58.4 %conditional.8 = ((f32[1024,4,64]{0,2,1:T(8,128)}, f32[8192,256]{0,1:T(8,128)}, f32[8192,256]{0,1:T(8,128)})) conditional(s32[]{:T(128)} %convert_element_type.314, (f32[1024,4,64]{0,2,1:T(8,128)}, f32[8192,256]{0,1:T(8,128)}, f32[8192,256]{0,1:T(8,128)}) %tuple.161, (s32[]{:T(128)}, bf16[8192,256]{0,1:T(8,128)(2,1)}, s32[]{:T(128)}, ...), branch_computations={%region_14.14_spmd, %region_15.15_spmd} | conditional | flops 2739143680 | bytes 170459328 | solution.py:193
  352.2 10.4 fusion.11
  362.6 6.2 fusion.20
  368.8 12.2 %fusion.16 = f32[4,1024,64]{1,2,0:T(8,128)} fusion(bf16[1024,4,64]{0,2,1:T(8,128)(2,1)} %get-tuple-element.710, f32[4,1024,1024]{2,1,0:T(8,128)} %copy-done, f32[4,1024]{1,0:T(4,128)} %get-tuple-element.708, pred[1024,1024]{0,1:T(8,128)(4,1)} %compare_and_fusion.2), kind=kOutput, calls=%fused_computation.29 | convolution fusion | flops 557842432 | bytes 19415040 | tf_op jit(solution)/shard_map/while/body/eval_jaxpr/cond/branch_1_fun/hqk,qhd->khd/dot_general | solution.py:169
  381.1 6.1 convolution_multiply_fusion
  389.5 5.7 dynamic_update_slice.12
  427.2 5.9 convert_element_type.211
  433.1 6.0 convert_element_type.209
  449.4 351.5 %reduce-scatter.5.cloned.1.call-done = bf16[1024,256]{0,1:T(8,128)(2,1)} async-done(((bf16[8192,256]{0,1:T(8,128)(2,1)}), bf16[1024,256]{0,1:T(8,128)(2,1)}) %reduce-scatter.5.cloned.1.call-update) | async-done | bytes 524304 | tf_op jit(solution)/shard_map/reduce_scatter | solution.py:778
  818.2 37.6 %reduce-scatter.3.cloned.1.call-done = bf16[1024,256]{0,1:T(8,128)(2,1)} async-done(((bf16[8192,256]{0,1:T(8,128)(2,1)}), bf16[1024,256]{0,1:T(8,128)(2,1)}) %reduce-scatter.3.cloned.1.call-update) | async-done | bytes 524304 | tf_op jit(solution)/shard_map/reduce_scatter | solution.py:775
  893.9 6.4 all-to-all-done.6
  908.9 117.9 %shard_map.221 = (f32[32,2816]{1,0:T(8,128)}, f32[32,2816]{1,0:T(8,128)}, f32[32,1024]{1,0:T(8,128)}, f32[32,1024]{1,0:T(8,128)}, f32[88,1024]{1,0:T(8,128)}, /*...) custom-call(bf16[32,32,2816]{2,1,0:T(8,128)(2,1)} %bitcast.221, bf16[32,32,2816]{2,1,0:T(8,128)(2,1)} %bitcast.222, ...), custom_call_target="tpu_custom_call" | custom-call | bytes 51642368 | tf_op jit(solution)/shard_map/pallas_call | solution.py:611
  (318 shorter events, 227.3 us)
Async XLA Ops:
  7.2 185.6 %all-gather.5.cloned.1.call-start = ((), (), s32[]{:S(2)}) async-start(), calls=%async_computation.11 | async-start | bytes 4718592 | tf_op jit(solution)/shard_map/all_gather | solution.py:696
  7.2 125.5 %copy-start.39 = (f32[32]{0:T(128)}, f32[32]{0:T(128)S(1)}, u32[]{:S(2)}) copy-start(f32[32]{0:T(128)S(1)} %multiply_power_fusion) | copy-start | bytes 388
  118.1 36.2 %copy-start.28 = (f32[1024]{0:T(1024)}, f32[1024]{0:T(1024)S(1)}, u32[]{:S(2)}) copy-start(f32[1024]{0:T(1024)S(1)} %reshape.495) | copy-start | bytes 12292
  119.9 34.4 %copy-start.32 = (f32[256]{0:T(256)}, f32[256]{0:T(256)S(1)}, u32[]{:S(2)}) copy-start(f32[256]{0:T(256)S(1)} %get-tuple-element.928) | copy-start | bytes 3076
  154.2 19.5 %copy-start.22 = (bf16[256,16,32]{0,2,1:T(8,128)(2,1)S(1)}, bf16[256,16,32]{0,2,1:T(8,128)(2,1)}, u32[]{:S(2)}) copy-start(bf16[256,16,32]{0,2,1:T(8,128)(2,1)} %get-tuple-element.910) | copy-start | bytes 786436
  154.2 78.1 %all-gather.3.cloned.1.call-start = ((), (), s32[]{:S(2)}) async-start(), calls=%async_computation.10 | async-start | bytes 4718592 | tf_op jit(solution)/shard_map/all_gather | solution.py:697
  174.5 17.5 %all-to-all-start.2 = ((bf16[256,4,256]{0,2,1:T(8,128)(2,1)}), bf16[256,4,256]{0,2,1:T(8,128)(2,1)S(1)}, u32[]{:S(2)}, u32[]{:S(2)}) async-start(bf16[256,4,256]{0,2,1:T(8,128)(2,1)} %bitcast.40), calls=%async_computation.2 | async-start | bytes 1048576 | tf_op jit(solution)/shard_map/all_to_all | solution.py:691
  276.9 13.9 %all-to-all-start.3 = ((bf16[4,256,256]{1,2,0:T(8,128)(2,1)}), bf16[4,256,256]{1,2,0:T(8,128)(2,1)S(1)}, u32[]{:S(2)}, u32[]{:S(2)}) async-start(bf16[4,256,256]{1,2,0:T(8,128)(2,1)} %copy.92), calls=%async_computation.3 | async-start | bytes 1048576 | tf_op jit(solution)/shard_map/all_to_all | solution.py:721
  293.5 15.1 %copy-start.6 = (f32[256,1024]{1,0:T(8,128)}, f32[256,1024]{1,0:T(8,128)S(1)}, u32[]{:S(2)}) copy-start(f32[256,1024]{1,0:T(8,128)S(1)} %get-tuple-element.932) | copy-start | bytes 3145732
  311.6 13.7 %all-to-all-start.4 = ((bf16[256,4,256]{2,0,1:T(8,128)(2,1)}), bf16[256,4,256]{2,0,1:T(8,128)(2,1)S(1)}, u32[]{:S(2)}, u32[]{:S(2)}) async-start(bf16[256,4,256]{2,0,1:T(8,128)(2,1)} %bitcast.197), calls=%async_computation.4 | async-start | bytes 1048576 | tf_op jit(solution)/shard_map/all_to_all | solution.py:750
  315.1 485.8 %reduce-scatter.5.cloned.1.call-start = ((), (), s32[]{:S(2)}) async-start(), calls=%async_computation.13 | async-start | bytes 4718592 | tf_op jit(solution)/shard_map/reduce_scatter | solution.py:778
  346.7 15.9 %copy-start = (f32[4,1024,1024]{2,1,0:T(8,128)}, f32[4,1024,1024]{2,1,0:T(8,128)S(1)}, u32[]{:S(2)}) copy-start(f32[4,1024,1024]{2,1,0:T(8,128)S(1)} %fusion.53) | copy-start | bytes 50331652 | tf_op jit(solution)/shard_map/while/body/eval_jaxpr/cond
  433.1 422.7 %reduce-scatter.3.cloned.1.call-start = ((), (), s32[]{:S(2)}) async-start(), calls=%async_computation.12 | async-start | bytes 4718592 | tf_op jit(solution)/shard_map/reduce_scatter | solution.py:775
  445.2 362.3 %copy-start.13 = (bf16[256,2816]{1,0:T(8,128)(2,1)S(1)}, bf16[256,2816]{1,0:T(8,128)(2,1)}, u32[]{:S(2)}) copy-start(bf16[256,2816]{1,0:T(8,128)(2,1)} %get-tuple-element.904) | copy-start | bytes 4325380
  802.9 59.1 %all-to-all-start.7 = ((bf16[4,256,256]{2,1,0:T(8,128)(2,1)}), bf16[4,256,256]{2,1,0:T(8,128)(2,1)S(1)}, u32[]{:S(2)}, u32[]{:S(2)}) async-start(bf16[4,256,256]{2,1,0:T(8,128)(2,1)} %bitcast.56), calls=%async_computation.9 | async-start | bytes 1048576 | tf_op jit(solution)/shard_map/all_to_all | solution.py:799
  813.7 43.3 %copy-start.24 = (f32[1024,32]{0,1:T(8,128)S(1)}, f32[1024,32]{0,1:T(8,128)}, u32[]{:S(2)}) copy-start(f32[1024,32]{0,1:T(8,128)} %get-tuple-element.919) | copy-start | bytes 393220
  857.0 10.4 copy-start.7
  862.8 19.1 %all-to-all-start.5 = ((bf16[4,256,256]{1,2,0:T(8,128)(2,1)}), bf16[4,256,256]{1,2,0:T(8,128)(2,1)S(1)}, u32[]{:S(2)}, u32[]{:S(2)}) async-start(bf16[4,256,256]{1,2,0:T(8,128)(2,1)} %copy.96), calls=%async_computation.5 | async-start | bytes 1048576 | tf_op jit(solution)/shard_map/all_to_all | solution.py:797
  872.9 13.3 %copy-start.3 = (bf16[256,1024]{1,0:T(8,128)(2,1)S(1)}, bf16[256,1024]{1,0:T(8,128)(2,1)}, u32[]{:S(2)}) copy-start(bf16[256,1024]{1,0:T(8,128)(2,1)} %param.25) | copy-start | bytes 1572868
  872.9 13.3 %copy-start.29 = (f32[1024]{0:T(1024)S(1)}, f32[1024]{0:T(1024)}, u32[]{:S(2)}) copy-start(f32[1024]{0:T(1024)} %copy-done.28) | copy-start | bytes 12292
  872.9 13.3 %copy-start.33 = (f32[256]{0:T(256)S(1)}, f32[256]{0:T(256)}, u32[]{:S(2)}) copy-start(f32[256]{0:T(256)} %copy-done.32) | copy-start | bytes 3076
  881.9 18.4 %all-to-all-start.6 = ((bf16[4,256,256]{1,2,0:T(8,128)(2,1)}), bf16[4,256,256]{1,2,0:T(8,128)(2,1)}, u32[]{:S(2)}, u32[]{:S(2)}) async-start(bf16[4,256,256]{1,2,0:T(8,128)(2,1)} %copy.97), calls=%async_computation.7 | async-start | bytes 1048576 | tf_op jit(solution)/shard_map/all_to_all | solution.py:798
  893.9 12.5 %copy-start.16 = (bf16[4,256,256]{1,2,0:T(8,128)(2,1)S(1)}, bf16[4,256,256]{1,2,0:T(8,128)(2,1)}, u32[]{:S(2)}) copy-start(bf16[4,256,256]{1,2,0:T(8,128)(2,1)} %get-tuple-element.914) | copy-start | bytes 1572868
  908.9 119.3 %copy-start.38 = (f32[256]{0:T(256)S(1)}, f32[256]{0:T(256)}, u32[]{:S(2)}) copy-start(f32[256]{0:T(256)} %get-tuple-element.927) | copy-start | bytes 3076
  (33 other events, 143.8 us)
Sparse Core Ops, SparseCore 0:
  154.3 34.8 all-gather.4
  191.7 36.7 all-gather.2
  433.2 367.6 reduce-scatter.4
  804.4 51.3 reduce-scatter.2

commit v2 on v1

--- a/solution.py
+++ b/solution.py
@@ -6,196 +6,7 @@
 from jax.experimental.pallas import tpu as pltpu
 from jax.sharding import PartitionSpec as P
 
-HEADS = 16
-HEAD_DIM = 64
-
-
 EPSILON = 1e-06
-NEGATIVE = -1e30
-
-
-def rms_scale(tensor):
-    return lax.rsqrt(jnp.mean(tensor * tensor, axis=-1, keepdims=True) + EPSILON)
-
-
-def angle_tables(offsets):
-    half_dim = HEAD_DIM // 2
-    frequency = jnp.power(10000.0, -jnp.arange(half_dim, dtype=jnp.float32) / half_dim)
-    angles = offsets.astype(jnp.float32)[:, None] * frequency[None, :]
-    return (jnp.cos(angles)[:, None, :], jnp.sin(angles)[:, None, :])
-
-
-def rotate(tensor, cosine, sine_tab):
-    half_dim = HEAD_DIM // 2
-    front_half = tensor[..., :half_dim]
-    back_half = tensor[..., half_dim:]
-    return jnp.concatenate(
-        [front_half * cosine - back_half * sine_tab, back_half * cosine + front_half * sine_tab],
-        axis=-1,
-    )
-
-
-def unrotate(tensor, cosine, sine_tab):
-    half_dim = HEAD_DIM // 2
-    front_half = tensor[..., :half_dim]
-    back_half = tensor[..., half_dim:]
-    return jnp.concatenate(
-        [front_half * cosine + back_half * sine_tab, back_half * cosine - front_half * sine_tab],
-        axis=-1,
-    )
-
-
-def matmul(left, right):
-    return jnp.dot(left, right, preferred_element_type=jnp.float32)
-
-
-def contract_rows(left, right):
-    return lax.dot_general(
-        left, right, (((0,), (0,)), ((), ())), preferred_element_type=jnp.float32
-    )
-
-
-def contract_cols(left, right):
-    return lax.dot_general(
-        left, right, (((1,), (1,)), ((), ())), preferred_element_type=jnp.float32
-    )
-
-
-def mask_for(q_pos, q_begin, k_first, count):
-    k_pos = k_first + jnp.arange(count, dtype=jnp.int32)
-    return (k_pos[None, :] <= q_pos[:, None]) & (k_pos[None, :] >= q_begin[:, None])
-
-
-def is_live(q_pos, q_begin, k_first, count):
-    return (k_first <= q_pos[-1]) & (k_first + count - 1 >= q_begin[0])
-
-
-def fetch_rows(source, number, piece_rows, heads_here):
-    return lax.dynamic_slice_in_dim(source, number * piece_rows, piece_rows, 0).reshape(
-        piece_rows, heads_here, HEAD_DIM
-    )
-
-
-def masked_scores(q_rows, k_rows, allowed, score_scale):
-    scores = (
-        jnp.einsum("qhd,khd->hqk", q_rows, k_rows, preferred_element_type=jnp.float32) * score_scale
-    )
-    return jnp.where(allowed[None], scores, NEGATIVE)
-
-
-def forward_block(q_rows, q_pos, q_begin, key_rows, value_rows, piece_rows, score_scale):
-    heads_here = q_rows.shape[1]
-    height = q_rows.shape[0]
-    numbers = jnp.arange(key_rows.shape[0] // piece_rows, dtype=jnp.int32)
-
-    def first_pass(running, number):
-        k_first = number * piece_rows
-
-        def first_update(current):
-            row_top, row_total = current
-            allowed = mask_for(q_pos, q_begin, k_first, piece_rows)
-            scores = masked_scores(
-                q_rows, fetch_rows(key_rows, number, piece_rows, heads_here), allowed, score_scale
-            )
-            new_top = jnp.maximum(row_top, jnp.max(scores, axis=-1))
-            weights = jnp.where(allowed[None], jnp.exp(scores - new_top[..., None]), 0.0)
-            return (new_top, row_total * jnp.exp(row_top - new_top) + jnp.sum(weights, axis=-1))
-
-        live = is_live(q_pos, q_begin, k_first, piece_rows)
-        return (lax.cond(live, first_update, lambda current: current, running), None)
-
-    start_state = (
-        jnp.full((heads_here, height), NEGATIVE, jnp.float32),
-        jnp.zeros((heads_here, height), jnp.float32),
-    )
-    final_state = lax.scan(first_pass, start_state, numbers)[0]
-    log_total = final_state[0] + jnp.log(final_state[1])
-
-    def second_pass(running, number):
-        k_first = number * piece_rows
-
-        def second_update(out_sum):
-            allowed = mask_for(q_pos, q_begin, k_first, piece_rows)
-            scores = masked_scores(
-                q_rows, fetch_rows(key_rows, number, piece_rows, heads_here), allowed, score_scale
-            )
-            low_probs = jnp.where(
-                allowed[None], jnp.exp(scores - log_total[..., None]), 0.0
-            ).astype(jnp.bfloat16)
-            return out_sum + jnp.einsum(
-                "hqk,khd->qhd",
-                low_probs,
-                fetch_rows(value_rows, number, piece_rows, heads_here),
-                preferred_element_type=jnp.float32,
-            )
-
-        live = is_live(q_pos, q_begin, k_first, piece_rows)
-        return (lax.cond(live, second_update, lambda out_sum: out_sum, running), None)
-
-    attended = lax.scan(
-        second_pass, jnp.zeros((height, heads_here, HEAD_DIM), jnp.float32), numbers
-    )[0]
-    return (log_total, attended)
-
-
-def backward_block(
-    q_rows,
-    grad_rows,
-    log_total,
-    spread,
-    q_pos,
-    q_begin,
-    key_rows,
-    value_rows,
-    piece_rows,
-    score_scale,
-    key_grads,
-    value_grads,
-):
-    heads_here = q_rows.shape[1]
-    numbers = jnp.arange(key_rows.shape[0] // piece_rows, dtype=jnp.int32)
-
-    def step_back(running, number):
-        local_first = number * piece_rows
-
-        def step_update(current):
-            grad_query, grad_keys, grad_values = current
-            k_rows = fetch_rows(key_rows, number, piece_rows, heads_here)
-            v_rows = fetch_rows(value_rows, number, piece_rows, heads_here)
-            allowed = mask_for(q_pos, q_begin, local_first, piece_rows)
-            scores = masked_scores(q_rows, k_rows, allowed, score_scale)
-            probs = jnp.where(allowed[None], jnp.exp(scores - log_total[..., None]), 0.0)
-            low_probs = probs.astype(jnp.bfloat16)
-            value_part = jnp.einsum(
-                "hqk,qhd->khd", low_probs, grad_rows, preferred_element_type=jnp.float32
-            )
-            grad_probs = jnp.einsum(
-                "qhd,khd->hqk", grad_rows, v_rows, preferred_element_type=jnp.float32
-            )
-            grad_scores = (probs * (grad_probs - spread[..., None])).astype(jnp.bfloat16)
-            grad_query = grad_query + score_scale * jnp.einsum(
-                "hqk,khd->qhd", grad_scores, k_rows, preferred_element_type=jnp.float32
-            )
-            key_part = score_scale * jnp.einsum(
-                "hqk,qhd->khd", grad_scores, q_rows, preferred_element_type=jnp.float32
-            )
-            old_keys = lax.dynamic_slice_in_dim(grad_keys, local_first, piece_rows, 0)
-            grad_keys = lax.dynamic_update_slice_in_dim(
-                grad_keys, old_keys + key_part.reshape(piece_rows, -1), local_first, 0
-            )
-            old_values = lax.dynamic_slice_in_dim(grad_values, local_first, piece_rows, 0)
-            grad_values = lax.dynamic_update_slice_in_dim(
-                grad_values, old_values + value_part.reshape(piece_rows, -1), local_first, 0
-            )
-            return (grad_query, grad_keys, grad_values)
-
-        live = is_live(q_pos, q_begin, local_first, piece_rows)
-        return (lax.cond(live, step_update, lambda current: current, running), None)
-
-    start_state = (jnp.zeros(q_rows.shape, jnp.float32), key_grads, value_grads)
-    return lax.scan(step_back, start_state, numbers)[0]
-
-
 MESH = pl.DeviceIdType.MESH
 
 
@@ -631,7 +442,666 @@
     )(*arrays)
 
 
+HEADS = 16
+HEAD_DIM = 64
+UNIT = 128
+NEGATIVE = -1e30
+
+
+class Owners:
+    def __init__(self, tokens):
+        self.seq, self.fsdp = lax.axis_size("seq"), lax.axis_size("fsdp")
+        self.total = self.seq * self.fsdp
+        self.members = self.total // HEADS
+        self.heads_here = HEADS // self.seq
+        self.tokens = tokens
+        self.halves = tokens // UNIT
+        self.units = self.halves * self.total // self.members
+
+    def locate(self):
+        s, f = lax.axis_index("seq"), lax.axis_index("fsdp")
+        self.s, self.f = s, f
+        self.linear = s * self.fsdp + f
+        self.block = f * self.seq + s
+        self.head = s * self.heads_here + lax.div(f, self.members)
+        self.member = lax.rem(f, self.members)
+
+    def of_head(self, head, member):
+        return {
+            "seq": lax.div(head, self.heads_here),
+            "fsdp": lax.rem(head, self.heads_here) * self.members + member,
+        }
+
+    def of_block(self, block):
+        return {"seq": lax.rem(block, self.seq), "fsdp": lax.div(block, self.seq)}
+
+    def barrier(self):
+        sem = pltpu.get_barrier_semaphore()
+
+        def greet(delta, carry):
+            other = lax.rem(self.linear + delta, self.total)
+            device = {"seq": lax.div(other, self.fsdp), "fsdp": lax.rem(other, self.fsdp)}
+            pl.semaphore_signal(sem, inc=1, device_id=device, device_id_type=MESH)
+            return carry
+
+        lax.fori_loop(1, self.total, greet, 0)
+        pl.semaphore_wait(sem, self.total - 1)
+
+
+def remote(source, target, send_sem, recv_sem, device):
+    return pltpu.make_async_remote_copy(
+        src_ref=source,
+        dst_ref=target,
+        send_sem=send_sem,
+        recv_sem=recv_sem,
+        device_id=device,
+        device_id_type=MESH,
+    )
+
+
+def head_rows(head):
+    return pl.ds(pl.multiple_of(head * HEAD_DIM, HEAD_DIM), HEAD_DIM)
+
+
+def lanes(number, width):
+    return pl.ds(pl.multiple_of(number * width, width), width)
+
+
+def spread_units(own, source, target, send, recv, local, act):
+    def to_head(delta, carry):
+        head = lax.rem(own.head + delta, HEADS)
+        for half in range(own.halves):
+            unit = own.halves * own.block + half
+            member = lax.rem(unit, own.members)
+            place = lax.div(unit, own.members)
+            piece = source.at[head_rows(head), pl.ds(half * UNIT, UNIT)]
+            there = target.at[:, lanes(place, UNIT)]
+            here = (head == own.head) & (member == own.member)
+
+            @pl.when(here)
+            def _(piece=piece, there=there, half=half):
+                copy = pltpu.make_async_copy(piece, there, local.at[half])
+                copy.start() if act == "start" else copy.wait()
+
+            @pl.when(jnp.logical_not(here))
+            def _(piece=piece, there=there, half=half, member=member, place=place, head=head):
+                copy = remote(
+                    piece, there, send.at[head, half], recv.at[place], own.of_head(head, member)
+                )
+                copy.start() if act == "start" else copy.wait_send()
+
+        return carry
+
+    lax.fori_loop(0, HEADS, to_head, 0)
+
+
+def await_units(own, target, send, recv):
+    def one(place, carry):
+        unit = place * own.members + own.member
+        there = target.at[:, lanes(place, UNIT)]
+
+        @pl.when(lax.div(unit, own.halves) != own.block)
+        def _():
+            remote(
+                there, there, send.at[0, 0], recv.at[place], own.of_block(0)
+            ).wait_recv()
+
+        return carry
+
+    lax.fori_loop(0, own.units, one, 0)
+
+
+def collect_units(own, source, target, send, recv, local, act):
+    def one(step, carry):
+        place = lax.rem(step + lax.div(own.block * own.halves, own.members), own.units)
+        unit = place * own.members + own.member
+        block, half = lax.div(unit, own.halves), lax.rem(unit, own.halves)
+        piece = source.at[:, lanes(place, UNIT)]
+        there = target.at[head_rows(own.head), lanes(half, UNIT)]
+
+        @pl.when(block == own.block)
+        def _():
+            copy = pltpu.make_async_copy(piece, there, local.at[half])
+            copy.start() if act == "start" else copy.wait()
+
+        @pl.when(block != own.block)
+        def _():
+            copy = remote(
+                piece, there, send.at[place], recv.at[own.head, half], own.of_block(block)
+            )
+            copy.start() if act == "start" else copy.wait_send()
+
+        return carry
+
+    lax.fori_loop(0, own.units, one, 0)
+
+
+def await_heads(own, target, send, recv):
+    def one(head, carry):
+        for half in range(own.halves):
+            unit = own.halves * own.block + half
+            there = target.at[head_rows(head), pl.ds(half * UNIT, UNIT)]
+
+            @pl.when((head != own.head) | (lax.rem(unit, own.members) != own.member))
+            def _(there=there, half=half):
+                remote(
+                    there, there, send.at[0], recv.at[head, half], own.of_block(0)
+                ).wait_recv()
+
+        return carry
+
+    lax.fori_loop(0, HEADS, one, 0)
+
+
+def to_heads_kernel(tokens, q_ref, k_ref, v_ref, q_out, k_out, v_out, *sems):
+    q_send, q_recv, q_local, kv_send, kv_recv, kv_local, hand_send = sems
+    own = Owners(tokens)
+    own.locate()
+    own.barrier()
+    pairs = ((k_ref, k_out), (v_ref, v_out))
+
+    def keys(act):
+        def to_head(delta, carry):
+            head = lax.rem(own.head + delta, HEADS)
+            for i, (source, target) in enumerate(pairs):
+                piece = source.at[head_rows(head), :]
+                there = target.at[:, lanes(own.block, tokens)]
+
+                @pl.when(head == own.head)
+                def _(piece=piece, there=there, i=i):
+                    copy = pltpu.make_async_copy(piece, there, kv_local.at[i])
+                    copy.start() if act == "start" else copy.wait()
+
+                @pl.when(head != own.head)
+                def _(piece=piece, there=there, i=i):
+                    copy = remote(
+                        piece,
+                        there,
+                        kv_send.at[i, head],
+                        kv_recv.at[i, own.block],
+                        own.of_head(head, own.member),
+                    )
+                    copy.start() if act == "start" else copy.wait_send()
+
+            return carry
+
+        return to_head
+
+    lax.fori_loop(0, HEADS, keys("start"), 0)
+    spread_units(own, q_ref, q_out, q_send, q_recv, q_local, "start")
+
+    def hand(i, order, block, source, act):
+        for away in range(1, own.members):
+            member = lax.rem(own.member + away, own.members)
+            copy = remote(
+                source,
+                pairs[i][1].at[:, lanes(block, tokens)],
+                hand_send.at[i, order * (own.members - 1) + away - 1],
+                kv_recv.at[i, block],
+                own.of_head(own.head, member),
+            )
+            copy.start() if act == "start" else copy.wait_send()
+
+    shares = own.total // own.members
+
+    def block_of(order):
+        f = own.member + own.members * lax.div(order, own.seq)
+        return f * own.seq + lax.rem(order, own.seq)
+
+    for i, (source, _) in enumerate(pairs):
+        hand(i, shares - 1, own.block, source.at[head_rows(own.head), :], "start")
+
+    mine = lax.div(own.f, own.members) * own.seq + own.s
+
+    def relay(step, carry):
+        order = lax.rem(mine + step, shares)
+        block = block_of(order)
+        for i, (_, target) in enumerate(pairs):
+            there = target.at[:, lanes(block, tokens)]
+            remote(
+                there, there, kv_send.at[i, 0], kv_recv.at[i, block], own.of_block(0)
+            ).wait_recv()
+            hand(i, step - 1, block, there, "start")
+        return carry
+
+    lax.fori_loop(1, shares, relay, 0)
+
+    def rest(block, carry):
+        @pl.when(lax.rem(lax.div(block, own.seq), own.members) != own.member)
+        def _():
+            for i, (_, target) in enumerate(pairs):
+                there = target.at[:, lanes(block, tokens)]
+                remote(
+                    there, there, kv_send.at[i, 0], kv_recv.at[i, block], own.of_block(0)
+                ).wait_recv()
+
+        return carry
+
+    lax.fori_loop(0, own.total, rest, 0)
+    await_units(own, q_out, q_send, q_recv)
+    lax.fori_loop(0, HEADS, keys("wait"), 0)
+    spread_units(own, q_ref, q_out, q_send, q_recv, q_local, "wait")
+    for i, (source, _) in enumerate(pairs):
+        hand(i, shares - 1, own.block, source.at[head_rows(own.head), :], "wait")
+
+    def settle(step, carry):
+        block = block_of(lax.rem(mine + step, shares))
+        for i, (_, target) in enumerate(pairs):
+            hand(i, step - 1, block, target.at[:, lanes(block, tokens)], "wait")
+        return carry
+
+    lax.fori_loop(1, shares, settle, 0)
+
+
+ANY = pl.BlockSpec(memory_space=pl.ANY)
+
+
+def comm_params(ident):
+    return pltpu.CompilerParams(collective_id=ident, has_side_effects=True)
+
+
+def to_heads(q, k, v, ident):
+    tokens = q.shape[1]
+    own = Owners(tokens)
+    whole = jax.ShapeDtypeStruct((HEAD_DIM, tokens * own.total), q.dtype)
+    few = jax.ShapeDtypeStruct((HEAD_DIM, own.units * UNIT), q.dtype)
+    dma = pltpu.SemaphoreType.DMA
+    return pl.pallas_call(
+        functools.partial(to_heads_kernel, tokens),
+        out_shape=[few, whole, whole],
+        in_specs=[ANY] * 3,
+        out_specs=[ANY] * 3,
+        scratch_shapes=[
+            dma((HEADS, own.halves)),
+            dma((own.units,)),
+            dma((own.halves,)),
+            dma((2, HEADS)),
+            dma((2, own.total)),
+            dma((2,)),
+            dma((2, own.total // own.members * (own.members - 1))),
+        ],
+        compiler_params=comm_params(ident),
+        cost_estimate=pl.CostEstimate(flops=0, bytes_accessed=whole.size * 8, transcendentals=0),
+    )(q, k, v)
+
+
+def units_to_heads_kernel(tokens, source, target, send, recv, local):
+    own = Owners(tokens)
+    own.locate()
+    own.barrier()
+    spread_units(own, source, target, send, recv, local, "start")
+    await_units(own, target, send, recv)
+    spread_units(own, source, target, send, recv, local, "wait")
+
+
+def units_to_heads(value, ident):
+    tokens = value.shape[1]
+    own = Owners(tokens)
+    dma = pltpu.SemaphoreType.DMA
+    few = jax.ShapeDtypeStruct((HEAD_DIM, own.units * UNIT), value.dtype)
+    return pl.pallas_call(
+        functools.partial(units_to_heads_kernel, tokens),
+        out_shape=few,
+        in_specs=[ANY],
+        out_specs=ANY,
+        scratch_shapes=[dma((HEADS, own.halves)), dma((own.units,)), dma((own.halves,))],
+        compiler_params=comm_params(ident),
+        cost_estimate=pl.CostEstimate(flops=0, bytes_accessed=few.size * 4, transcendentals=0),
+    )(value)
+
+
+def units_to_tokens_kernel(tokens, source, target, send, recv, local):
+    own = Owners(tokens)
+    own.locate()
+    own.barrier()
+    collect_units(own, source, target, send, recv, local, "start")
+    await_heads(own, target, send, recv)
+    collect_units(own, source, target, send, recv, local, "wait")
+
+
+def units_to_tokens(value, tokens, ident):
+    own = Owners(tokens)
+    dma = pltpu.SemaphoreType.DMA
+    back = jax.ShapeDtypeStruct((HEADS * HEAD_DIM, tokens), value.dtype)
+    return pl.pallas_call(
+        functools.partial(units_to_tokens_kernel, tokens),
+        out_shape=back,
+        in_specs=[ANY],
+        out_specs=ANY,
+        scratch_shapes=[dma((own.units,)), dma((HEADS, own.halves)), dma((own.halves,))],
+        compiler_params=comm_params(ident),
+        cost_estimate=pl.CostEstimate(flops=0, bytes_accessed=back.size * 4, transcendentals=0),
+    )(value)
+
+
+def grads_to_tokens_kernel(
+    tokens, dq_ref, dk_ref, dv_ref, dq_out, dk_out, dv_out, given, held, total, *sems
+):
+    q_send, q_recv, q_local, give_send, give_recv, back_send, back_recv, own_sem, local = sems
+    own = Owners(tokens)
+    own.locate()
+    own.barrier()
+    pairs = ((dk_ref, dk_out), (dv_ref, dv_out))
+    shares = own.total // own.members
+    others = own.members - 1
+    mine = lax.div(own.f, own.members) * own.seq + own.s
+
+    def block_of(order, member):
+        f = member + own.members * lax.div(order, own.seq)
+        return f * own.seq + lax.rem(order, own.seq)
+
+    def give(act):
+        def one(step, carry):
+            order = lax.rem(mine + step, shares)
+            for away in range(1, own.members):
+                member = lax.rem(own.member + away, own.members)
+                block = block_of(order, member)
+                for i, (source, _) in enumerate(pairs):
+                    copy = remote(
+                        source.at[:, lanes(block, tokens)],
+                        given.at[i, order * others + others - away],
+                        give_send.at[i, order * others + away - 1],
+                        give_recv.at[i, order * others + others - away],
+                        own.of_head(own.head, member),
+                    )
+                    copy.start() if act == "start" else copy.wait_send()
+            return carry
+
+        return one
+
+    def take(order, i):
+        return pltpu.make_async_copy(
+            pairs[i][0].at[:, lanes(block_of(order, own.member), tokens)],
+            held.at[i, order],
+            own_sem.at[i, order],
+        )
+
+    def load(order, carry):
+        for i in range(2):
+            take(order, i).start()
+        return carry
+
+    lax.fori_loop(1, shares + 1, lambda s, c: give("start")(lax.rem(s, shares), c), 0)
+    lax.fori_loop(0, shares, load, 0)
+    collect_units(own, dq_ref, dq_out, q_send, q_recv, q_local, "start")
+
+    def back(order, i, act):
+        block = block_of(order, own.member)
+        there = pairs[i][1].at[head_rows(own.head), :]
+
+        @pl.when(block == own.block)
+        def _():
+            copy = pltpu.make_async_copy(held.at[i, order], there, local.at[i])
+            copy.start() if act == "start" else copy.wait()
+
+        @pl.when(block != own.block)
+        def _():
+            copy = remote(
+                held.at[i, order],
+                there,
+                back_send.at[i, order],
+                back_recv.at[i, own.head],
+                own.of_block(block),
+            )
+            copy.start() if act == "start" else copy.wait_send()
+
+    def add(step, carry):
+        order = lax.rem(mine + step, shares)
+        for i in range(2):
+            take(order, i).wait()
+            total[...] = held[i, order].astype(jnp.float32)
+            for j in range(others):
+                slot = order * others + j
+                remote(
+                    given.at[i, slot],
+                    given.at[i, slot],
+                    give_send.at[i, 0],
+                    give_recv.at[i, slot],
+                    own.of_block(0),
+                ).wait_recv()
+                total[...] += given[i, slot].astype(jnp.float32)
+            held[i, order] = total[...].astype(held.dtype)
+            back(order, i, "start")
+        return carry
+
+    lax.fori_loop(1, shares + 1, add, 0)
+    await_heads(own, dq_out, q_send, q_recv)
+
+    def arrive(head, carry):
+        @pl.when(head != own.head)
+        def _():
+            for i, (_, target) in enumerate(pairs):
+                there = target.at[head_rows(head), :]
+                remote(
+                    there, there, back_send.at[i, 0], back_recv.at[i, head], own.of_block(0)
+                ).wait_recv()
+
+        return carry
+
+    lax.fori_loop(0, HEADS, arrive, 0)
+    lax.fori_loop(0, shares, give("wait"), 0)
+    collect_units(own, dq_ref, dq_out, q_send, q_recv, q_local, "wait")
+
+    def settle(order, carry):
+        for i in range(2):
+            back(order, i, "wait")
+        return carry
+
+    lax.fori_loop(0, shares, settle, 0)
+
+
+def grads_to_tokens(dq, dk, dv, tokens, ident):
+    own = Owners(tokens)
+    dma = pltpu.SemaphoreType.DMA
+    back = jax.ShapeDtypeStruct((HEADS * HEAD_DIM, tokens), dq.dtype)
+    shares = own.total // own.members
+    others = own.members - 1
+    return pl.pallas_call(
+        functools.partial(grads_to_tokens_kernel, tokens),
+        out_shape=[back] * 3,
+        in_specs=[ANY] * 3,
+        out_specs=[ANY] * 3,
+        scratch_shapes=[
+            pltpu.VMEM((2, shares * others, HEAD_DIM, tokens), dq.dtype),
+            pltpu.VMEM((2, shares, HEAD_DIM, tokens), dq.dtype),
+            pltpu.VMEM((HEAD_DIM, tokens), jnp.float32),
+            dma((own.units,)),
+            dma((HEADS, own.halves)),
+            dma((own.halves,)),
+            dma((2, shares * others)),
+            dma((2, shares * others)),
+            dma((2, shares)),
+            dma((2, HEADS)),
+            dma((2, shares)),
+            dma((2,)),
+        ],
+        compiler_params=comm_params(ident),
+        cost_estimate=pl.CostEstimate(flops=0, bytes_accessed=back.size * 12, transcendentals=0),
+    )(dq, dk, dv)
+
+
+QUERIES = 512
+KEYS = 512
+VMEM_LIMIT = 60 << 20
+
+
+def first_dims(left, right):
+    return lax.dot_general(left, right, (((0,), (0,)), ((), ())), preferred_element_type=jnp.float32)
+
+
+def plain(left, right):
+    return lax.dot_general(left, right, (((1,), (0,)), ((), ())), preferred_element_type=jnp.float32)
+
+
+def last_dims(left, right):
+    return lax.dot_general(left, right, (((1,), (1,)), ((), ())), preferred_element_type=jnp.float32)
+
+
+def tile_bounds(places, begins, group, width):
+    pos, begin = places.reshape(-1, group), begins.reshape(-1, group)
+    low, high = begin[:, 0] // width, pos[:, -1] // width + 1
+    inner, outer = (begin[:, -1] + width - 1) // width, (pos[:, 0] + 1) // width
+    some = inner < outer
+    return jnp.stack([low, jnp.where(some, inner, high), jnp.where(some, outer, high), high])
+
+
+def over_tiles(bounds, group, body, state):
+    low, inner, outer, high = (bounds[i, group] for i in range(4))
+    before = inner - low
+
+    def edge(step, current):
+        return body(jnp.where(step < before, low + step, outer + step - before), True, current)
+
+    state = lax.fori_loop(0, before + high - outer, edge, state)
+    return lax.fori_loop(inner, outer, lambda tile, current: body(tile, False, current), state)
+
+
+def key_lanes(tile):
+    return pl.ds(pl.multiple_of(tile * KEYS, KEYS), KEYS)
+
+
+def visible(tile, pos, begin):
+    number = tile * KEYS + lax.broadcasted_iota(jnp.int32, (KEYS, 1), 0)
+    return (number <= pos) & (number >= begin)
+
+
+def attend_kernel(bounds, q_ref, k_ref, v_ref, pos_ref, begin_ref, low_ref, out_ref, lse_ref):
+    def one_group(group, carry):
+        here = pl.ds(pl.multiple_of(group * QUERIES, QUERIES), QUERIES)
+        queries = q_ref[:, here]
+        pos, begin = pos_ref[:, here], begin_ref[:, here]
+
+        def tile_step(tile, masked, current):
+            top, total, summed = current
+            scores = first_dims(k_ref[:, key_lanes(tile)], queries)
+            if masked:
+                scores = jnp.where(visible(tile, pos, begin), scores, NEGATIVE)
+            new_top = jnp.maximum(top, jnp.max(scores, axis=0, keepdims=True))
+            weights = jnp.exp(scores - new_top)
+            shrink = jnp.exp(top - new_top)
+            total = total * shrink + jnp.sum(weights, axis=0, keepdims=True)
+            summed = summed * shrink + plain(v_ref[:, key_lanes(tile)], weights.astype(jnp.bfloat16))
+            return new_top, total, summed
+
+        top, total, summed = over_tiles(
+            bounds,
+            group,
+            tile_step,
+            (
+                jnp.full((1, QUERIES), NEGATIVE, jnp.float32),
+                jnp.zeros((1, QUERIES), jnp.float32),
+                jnp.zeros((HEAD_DIM, QUERIES), jnp.float32),
+            ),
+        )
+        attended = summed / total
+        out_ref[:, here] = attended
+        low_ref[:, here] = attended.astype(jnp.bfloat16)
+        lse_ref[:, here] = top + jnp.log(total)
+        return carry
+
+    lax.fori_loop(0, q_ref.shape[1] // QUERIES, one_group, 0)
+
+
+WHOLE = pl.BlockSpec(memory_space=pltpu.VMEM)
+
+
+def attend(bounds, q, k, v, pos, begin):
+    count = q.shape[1]
+    pairs = count * k.shape[1] // 4
+    return pl.pallas_call(
+        attend_kernel,
+        out_shape=[
+            jax.ShapeDtypeStruct((HEAD_DIM, count), jnp.bfloat16),
+            jax.ShapeDtypeStruct((HEAD_DIM, count), jnp.float32),
+            jax.ShapeDtypeStruct((1, count), jnp.float32),
+        ],
+        in_specs=[pl.BlockSpec(memory_space=pltpu.SMEM)] + [WHOLE] * 5,
+        out_specs=[WHOLE] * 3,
+        compiler_params=pltpu.CompilerParams(vmem_limit_bytes=VMEM_LIMIT),
+        cost_estimate=pl.CostEstimate(
+            flops=pairs * 4 * HEAD_DIM, bytes_accessed=4 * k.size, transcendentals=pairs
+        ),
+    )(bounds, q, k, v, pos, begin)
+
+
+def attend_back_kernel(
+    bounds, q_ref, k_ref, v_ref, g_ref, out_ref, lse_ref, pos_ref, begin_ref, dq_ref, dk_ref, dv_ref,
+    dk_sum, dv_sum,
+):
+    dk_sum[...] = jnp.zeros_like(dk_sum)
+    dv_sum[...] = jnp.zeros_like(dv_sum)
+
+    def one_group(group, carry):
+        here = pl.ds(pl.multiple_of(group * QUERIES, QUERIES), QUERIES)
+        queries, grads = q_ref[:, here], g_ref[:, here]
+        pos, begin, lse = pos_ref[:, here], begin_ref[:, here], lse_ref[:, here]
+        delta = jnp.sum(grads.astype(jnp.float32) * out_ref[:, here], axis=0, keepdims=True)
+
+        def tile_step(tile, masked, dq):
+            there = key_lanes(tile)
+            keys, values = k_ref[:, there], v_ref[:, there]
+            scores = first_dims(keys, queries)
+            if masked:
+                scores = jnp.where(visible(tile, pos, begin), scores, NEGATIVE)
+            probs = jnp.exp(scores - lse)
+            dv_sum[:, there] += last_dims(grads, probs.astype(jnp.bfloat16))
+            dscores = (probs * (first_dims(values, grads) - delta)).astype(jnp.bfloat16)
+            dk_sum[:, there] += last_dims(queries, dscores)
+            return dq + plain(keys, dscores)
+
+        dq = over_tiles(bounds, group, tile_step, jnp.zeros((HEAD_DIM, QUERIES), jnp.float32))
+        dq_ref[:, here] = (dq * HEAD_DIM**-0.5).astype(dq_ref.dtype)
+        return carry
+
+    lax.fori_loop(0, q_ref.shape[1] // QUERIES, one_group, 0)
+    dk_ref[...] = dk_sum[...].astype(dk_ref.dtype)
+    dv_ref[...] = dv_sum[...].astype(dv_ref.dtype)
+
+
+def attend_back(bounds, q, k, v, grads, out, lse, pos, begin):
+    pairs = q.shape[1] * k.shape[1] // 4
+    return pl.pallas_call(
+        attend_back_kernel,
+        out_shape=[jax.ShapeDtypeStruct(a.shape, jnp.bfloat16) for a in (q, k, v)],
+        in_specs=[pl.BlockSpec(memory_space=pltpu.SMEM)] + [WHOLE] * 8,
+        out_specs=[WHOLE] * 3,
+        scratch_shapes=[pltpu.VMEM(k.shape, jnp.float32)] * 2,
+        compiler_params=pltpu.CompilerParams(vmem_limit_bytes=VMEM_LIMIT),
+        cost_estimate=pl.CostEstimate(
+            flops=pairs * 10 * HEAD_DIM, bytes_accessed=6 * k.size, transcendentals=pairs
+        ),
+    )(bounds, q, k, v, grads, out, lse, pos, begin)
+
+
 SCHEMES = ("A", "A", "A", "B", "C", "C", "C", "C")
+
+
+def rms_scale(tensor):
+    return lax.rsqrt(jnp.mean(tensor * tensor, axis=-1, keepdims=True) + EPSILON)
+
+
+def angle_tables(offsets):
+    half_dim = HEAD_DIM // 2
+    frequency = jnp.power(10000.0, -jnp.arange(half_dim, dtype=jnp.float32) / half_dim)
+    angles = frequency[:, None] * offsets.astype(jnp.float32)[None, :]
+    return jnp.cos(angles)[None], jnp.sin(angles)[None]
+
+
+def rotate(tensor, cosine, sine_tab):
+    pairs = tensor.reshape(HEADS, 2, HEAD_DIM // 2, -1)
+    front, back = pairs[:, 0], pairs[:, 1]
+    turned = jnp.stack([front * cosine - back * sine_tab, back * cosine + front * sine_tab], axis=1)
+    return turned.reshape(tensor.shape)
+
+
+def matmul(left, right):
+    return jnp.dot(left, right, preferred_element_type=jnp.float32)
+
+
+def contract(left, right, left_dim, right_dim):
+    return lax.dot_general(
+        left, right, (((left_dim,), (right_dim,)), ((), ())), preferred_element_type=jnp.float32
+    )
 
 
 def per_device(
@@ -649,183 +1119,119 @@
     w_down,
     out_cot,
 ):
-    gains = jnp.zeros((16, 128), jnp.bfloat16)
+    low = jnp.bfloat16
+    tokens = layer_input.shape[0]
+    seq, fsdp = lax.axis_size("seq"), lax.axis_size("fsdp")
+    devices = seq * fsdp
+    seq_index = lax.axis_index("seq")
+    own_offsets = lax.dynamic_slice_in_dim(offsets, seq_index * tokens, tokens, 0)
+
+    gains = jnp.zeros((16, 128), low)
     gains = lax.dynamic_update_slice(gains, g_attn[None], (0, 0))
     gains = lax.dynamic_update_slice(gains, g_ffn[None], (1, 0))
-    shards = (w_gate, w_up, w_query, w_key, w_down, w_value, w_out, gains)
-    pieces = [(i, 0, shard.shape[1], scheme) for i, (shard, scheme) in enumerate(zip(shards, SCHEMES))]
-    *wholes, whole_gains = gather_all(shards, pieces, 0)
+    places = jnp.zeros((8, 128), jnp.int32)
+    places = lax.dynamic_update_slice(places, own_offsets.reshape(-1, 128), (0, 0))
+    shards = (w_gate, w_up, w_query, w_key, w_down, w_value, w_out, gains, places)
+    pieces = [(i, 0, shard.shape[1], scheme) for i, (shard, scheme) in enumerate(zip(shards, SCHEMES + ("C",)))]
+    *wholes, whole_gains, whole_places = gather_all(shards, pieces, 0)
     proj_gate, proj_up, proj_query, proj_key, proj_down, proj_value, proj_out = (
         whole.reshape(-1, whole.shape[2]) for whole in wholes
     )
-    gain_attn = whole_gains[:, 0, : g_attn.shape[0]].reshape(-1)
-    gain_ffn = whole_gains[:, 1, : g_ffn.shape[0]].reshape(-1)
-    tokens = layer_input.shape[0]
-    group_size = lax.axis_size("seq")
-    group_rows = tokens * group_size
-    heads_here = HEADS // group_size
-    score_scale = HEAD_DIM ** (-0.5)
-    seq_index = lax.axis_index("seq")
-    part_index = lax.axis_index("fsdp")
-    own_offsets = lax.dynamic_slice_in_dim(offsets, seq_index * tokens, tokens, 0)
-    cos_tokens, sin_tokens = angle_tables(own_offsets)
+    gain_attn = whole_gains[:, 0, : g_attn.shape[0]].reshape(-1).astype(jnp.float32)
+    gain_ffn = whole_gains[:, 1, : g_ffn.shape[0]].reshape(-1).astype(jnp.float32)
+    all_offsets = (
+        whole_places[:, : tokens // 128].reshape(seq, fsdp, tokens).transpose(1, 0, 2).reshape(-1)
+    )
+
+    own = Owners(tokens)
+    member = lax.rem(lax.axis_index("fsdp"), own.members)
+    unit_begins = (jnp.arange(devices * tokens, dtype=jnp.int32) - all_offsets).reshape(
+        own.units, own.members, UNIT
+    )
+    begin = lax.dynamic_index_in_dim(unit_begins, member, 1, keepdims=False).reshape(1, -1)
+    pos = (
+        (jnp.arange(own.units, dtype=jnp.int32)[:, None] * own.members + member) * UNIT
+        + jnp.arange(UNIT, dtype=jnp.int32)[None]
+    ).reshape(1, -1)
+    bounds = tile_bounds(pos, begin, QUERIES, KEYS)
+
+    cosine, sine_tab = angle_tables(own_offsets)
     input_f32 = layer_input.astype(jnp.float32)
     norm_attn = rms_scale(input_f32)
-    normed_a = (input_f32 * norm_attn * gain_attn.astype(jnp.float32)).astype(jnp.bfloat16)
-    q_tokens = (
-        rotate(
-            matmul(normed_a, proj_query).reshape(tokens, HEADS, HEAD_DIM), cos_tokens, sin_tokens
-        )
-        .reshape(tokens, -1)
-        .astype(jnp.bfloat16)
-    )
-    k_tokens = (
-        rotate(matmul(normed_a, proj_key).reshape(tokens, HEADS, HEAD_DIM), cos_tokens, sin_tokens)
-        .reshape(tokens, -1)
-        .astype(jnp.bfloat16)
-    )
-    mixed_values = (0.5 * matmul(normed_a, proj_value) + 0.5 * v_first.astype(jnp.float32)).astype(
-        jnp.bfloat16
-    )
-    q_heads, k_heads, v_heads = (
-        lax.all_to_all(q_tokens, "seq", split_axis=1, concat_axis=0, tiled=True),
-        lax.all_to_all(k_tokens, "seq", split_axis=1, concat_axis=0, tiled=True),
-        lax.all_to_all(mixed_values, "seq", split_axis=1, concat_axis=0, tiled=True),
-    )
-    k_whole, v_whole = (
-        lax.all_gather(k_heads, "fsdp", axis=0, tiled=True),
-        lax.all_gather(v_heads, "fsdp", axis=0, tiled=True),
-    )
-    positions = part_index * group_rows + jnp.arange(group_rows, dtype=jnp.int32)
-    doc_begins = positions - offsets
-    block_rows = min(1024, group_rows)
-    q_three = q_heads.reshape(group_rows, heads_here, HEAD_DIM)
-    lse_parts = []
-    out_parts = []
-    for number in range(group_rows // block_rows):
-        lower = number * block_rows
-        upper = lower + block_rows
-        log_total, attended = forward_block(
-            q_three[lower:upper],
-            positions[lower:upper],
-            doc_begins[lower:upper],
-            k_whole,
-            v_whole,
-            group_rows,
-            score_scale,
-        )
-        lse_parts.append(log_total)
-        out_parts.append(attended)
-    attended_all = jnp.concatenate(out_parts, axis=0)
-    attended_low = attended_all.reshape(group_rows, -1).astype(jnp.bfloat16)
-    attn_tokens = lax.all_to_all(attended_low, "seq", split_axis=0, concat_axis=1, tiled=True)
-    after_attn = input_f32 + matmul(attn_tokens, proj_out)
+    normed_a = (input_f32 * norm_attn * gain_attn).astype(low)
+    scale = jnp.asarray(HEAD_DIM**-0.5, low)
+    q_tokens = rotate(contract(proj_query, normed_a, 0, 1), cosine, sine_tab).astype(low) * scale
+    k_tokens = rotate(contract(proj_key, normed_a, 0, 1), cosine, sine_tab).astype(low)
+    mixed = (
+        0.5 * contract(proj_value, normed_a, 0, 1) + 0.5 * v_first.astype(jnp.float32).T
+    ).astype(low)
+    q_head, k_head, v_head = to_heads(q_tokens, k_tokens, mixed, 1)
+    attended_low, attended, lse = attend(bounds, q_head, k_head, v_head, pos, begin)
+    attn_tokens = units_to_tokens(attended_low, tokens, 2)
+
+    after_attn = input_f32 + contract(attn_tokens, proj_out, 0, 0)
     norm_ffn = rms_scale(after_attn)
-    normed_f = (after_attn * norm_ffn * gain_ffn.astype(jnp.float32)).astype(jnp.bfloat16)
+    normed_f = (after_attn * norm_ffn * gain_ffn).astype(low)
     gate_act = matmul(normed_f, proj_gate)
     up_act = matmul(normed_f, proj_up)
     sigmoid_gate = jax.nn.sigmoid(gate_act)
     silu_gate = gate_act * sigmoid_gate
-    hidden = (silu_gate * up_act).astype(jnp.bfloat16)
-    result = (after_attn + matmul(hidden, proj_down)).astype(jnp.bfloat16)
-    grad_down = contract_rows(hidden, out_cot)
-    grad_hidden = contract_cols(out_cot, proj_down)
+    hidden = (silu_gate * up_act).astype(low)
+    result = (after_attn + matmul(hidden, proj_down)).astype(low)
+
+    grad_down = contract(hidden, out_cot, 0, 0)
+    grad_hidden = contract(out_cot, proj_down, 1, 1)
     grad_gate_low = (
         grad_hidden * up_act * sigmoid_gate * (1.0 + gate_act * (1.0 - sigmoid_gate))
-    ).astype(jnp.bfloat16)
-    grad_up_low = (grad_hidden * silu_gate).astype(jnp.bfloat16)
-    grad_gate_w = contract_rows(normed_f, grad_gate_low)
-    grad_up_w = contract_rows(normed_f, grad_up_low)
-    grad_normed_f = contract_cols(grad_gate_low, proj_gate) + contract_cols(grad_up_low, proj_up)
+    ).astype(low)
+    grad_up_low = (grad_hidden * silu_gate).astype(low)
+    grad_gate_w = contract(normed_f, grad_gate_low, 0, 0)
+    grad_up_w = contract(normed_f, grad_up_low, 0, 0)
+    grad_normed_f = contract(grad_gate_low, proj_gate, 1, 1) + contract(grad_up_low, proj_up, 1, 1)
     grad_gain_ffn = jnp.sum(grad_normed_f * after_attn * norm_ffn, axis=0)
-    scaled_ffn = grad_normed_f * gain_ffn.astype(jnp.float32)
+    scaled_ffn = grad_normed_f * gain_ffn
     grad_after = (
         out_cot.astype(jnp.float32)
         + norm_ffn * scaled_ffn
         - after_attn * norm_ffn**3 * jnp.mean(scaled_ffn * after_attn, axis=-1, keepdims=True)
     )
-    grad_attn_low = grad_after.astype(jnp.bfloat16)
-    grad_out_w = contract_rows(attn_tokens, grad_attn_low)
-    grad_attended = contract_cols(grad_attn_low, proj_out).astype(jnp.bfloat16)
-    grad_heads = lax.all_to_all(grad_attended, "seq", split_axis=1, concat_axis=0, tiled=True)
-    grad_three = grad_heads.reshape(group_rows, heads_here, HEAD_DIM)
-    spread_all = jnp.einsum("qhd,qhd->hq", grad_three.astype(jnp.float32), attended_all)
-    key_grads = jnp.zeros((k_whole.shape[0], k_whole.shape[1]), jnp.float32)
-    value_grads = jnp.zeros((v_whole.shape[0], v_whole.shape[1]), jnp.float32)
-    query_parts = []
-    for number in range(group_rows // block_rows):
-        lower = number * block_rows
-        upper = lower + block_rows
-        grad_query, key_grads, value_grads = backward_block(
-            q_three[lower:upper],
-            grad_three[lower:upper],
-            lse_parts[number],
-            spread_all[:, lower:upper],
-            positions[lower:upper],
-            doc_begins[lower:upper],
-            k_whole,
-            v_whole,
-            group_rows,
-            score_scale,
-            key_grads,
-            value_grads,
-        )
-        query_parts.append(grad_query)
-    own_keys, own_values = (
-        lax.psum_scatter(
-            key_grads.astype(jnp.bfloat16), "fsdp", scatter_dimension=0, tiled=True
-        ).astype(jnp.float32),
-        lax.psum_scatter(
-            value_grads.astype(jnp.bfloat16), "fsdp", scatter_dimension=0, tiled=True
-        ).astype(jnp.float32),
+    grad_attn_low = grad_after.astype(low)
+    grad_out_w = contract(attn_tokens, grad_attn_low, 1, 0)
+    grad_attended = contract(proj_out, grad_attn_low, 1, 1).astype(low)
+
+    grad_head = units_to_heads(grad_attended, 3)
+    dq_head, dk_head, dv_head = attend_back(
+        bounds, q_head, k_head, v_head, grad_head, attended, lse, pos, begin
     )
-    cos_group, sin_group = angle_tables(offsets)
-    grad_q_rot = lax.optimization_barrier(
-        jnp.concatenate(query_parts, axis=0).astype(jnp.bfloat16)
-    ).astype(jnp.float32)
-    grad_k_rot = lax.optimization_barrier(own_keys.astype(jnp.bfloat16)).astype(jnp.float32)
-    grad_q_pre = (
-        unrotate(grad_q_rot, cos_group, sin_group).reshape(group_rows, -1).astype(jnp.bfloat16)
-    )
-    grad_k_pre = (
-        unrotate(grad_k_rot.reshape(group_rows, heads_here, HEAD_DIM), cos_group, sin_group)
-        .reshape(group_rows, -1)
-        .astype(jnp.bfloat16)
-    )
-    grad_mixed = own_values.astype(jnp.bfloat16)
-    grad_q_tok, grad_k_tok, grad_mix_tok = (
-        lax.all_to_all(grad_q_pre, "seq", split_axis=0, concat_axis=1, tiled=True),
-        lax.all_to_all(grad_k_pre, "seq", split_axis=0, concat_axis=1, tiled=True),
-        lax.all_to_all(grad_mixed, "seq", split_axis=0, concat_axis=1, tiled=True),
-    )
-    grad_first = 0.5 * grad_mix_tok.astype(jnp.float32)
-    grad_value_low = grad_first.astype(jnp.bfloat16)
-    grad_query_w = contract_rows(normed_a, grad_q_tok)
-    grad_key_w = contract_rows(normed_a, grad_k_tok)
-    grad_value_w = contract_rows(normed_a, grad_value_low)
+    dq_rot, dk_rot, grad_mixed = grads_to_tokens(dq_head, dk_head, dv_head, tokens, 4)
+    grad_q = rotate(dq_rot.astype(jnp.float32), cosine, -sine_tab).astype(low)
+    grad_k = rotate(dk_rot.astype(jnp.float32), cosine, -sine_tab).astype(low)
+    grad_v = grad_mixed * jnp.asarray(0.5, low)
+    grad_first = grad_v.T.astype(jnp.float32)
+    grad_query_w = contract(normed_a, grad_q, 0, 1)
+    grad_key_w = contract(normed_a, grad_k, 0, 1)
+    grad_value_w = contract(normed_a, grad_v, 0, 1)
     grad_normed_a = (
-        contract_cols(grad_q_tok, proj_query)
-        + contract_cols(grad_k_tok, proj_key)
-        + contract_cols(grad_value_low, proj_value)
+        contract(grad_q, proj_query, 0, 1)
+        + contract(grad_k, proj_key, 0, 1)
+        + contract(grad_v, proj_value, 0, 1)
     )
     grad_gain_attn = jnp.sum(grad_normed_a * input_f32 * norm_attn, axis=0)
-    scaled_attn = grad_normed_a * gain_attn.astype(jnp.float32)
+    scaled_attn = grad_normed_a * gain_attn
     grad_layer = (
         grad_after
         + norm_attn * scaled_attn
         - input_f32 * norm_attn**3 * jnp.mean(scaled_attn * input_f32, axis=-1, keepdims=True)
     )
-    devices = lax.axis_size("seq") * lax.axis_size("fsdp")
+
     terms = [
-        grad.astype(jnp.bfloat16).reshape(devices, -1, grad.shape[1])
+        grad.astype(low).reshape(devices, -1, grad.shape[1])
         for grad in (grad_gate_w, grad_up_w, grad_query_w, grad_key_w, grad_down, grad_value_w, grad_out_w)
     ]
     gain_terms = jnp.zeros((devices, 8, 128), jnp.float32)
     for row, grad in enumerate((grad_gain_attn, grad_gain_ffn)):
-        gain_terms = lax.dynamic_update_slice(
-            gain_terms, grad.reshape(devices, 1, -1), (0, row, 0)
-        )
-    sums = reduce_all([*terms, gain_terms], pieces, 1)
+        gain_terms = lax.dynamic_update_slice(gain_terms, grad.reshape(devices, 1, -1), (0, row, 0))
+    sums = reduce_all([*terms, gain_terms], pieces[:-1], 5)
     sum_gate, sum_up, sum_query, sum_key, sum_down, sum_value, sum_out, sum_gains = sums
     return (
         result,

time: 1050 us -> 528 us (0.50)
  waiting for transfers between devices: 430 us -> 0 us
  Pallas kernels: 226 us -> 416 us
  local copies, waits for them, and re-layouts: 108 us -> 36.9 us
  matrix products: 110 us -> 52.4 us
  loops' own time: 50.7 us -> 0 us
  blocking collectives: 35.2 us -> 0 us
  other arithmetic: 43.1 us -> 12.2 us
  starting transfers between devices: 24.9 us -> 0 us
  between operations: 14.8 us -> 1.48 us
    reduce_scatter x2 -> x0, waiting for transfers between devices: 389 us -> none  [the longest x1 351 us: per_device(): lax.psum_scatter(value_grads.astype(jnp.bfloat16), 'fsdp', scatter_dimens...]
    pallas_call x0 -> x6, Pallas kernels: none -> 189 us  [the longest x1 46.3 us: grads_to_tokens(): pl.pallas_call(functools.partial(grads_to_tokens_kernel, tokens), out_sha...]
    another operation x27 -> x0, loops' own time: 50.7 us -> none  [the longest x1 16.3 us: backward_block(): return lax.scan(step_back, start_state, numbers)[0]]
    dot_general x21 -> x18, matrix products: 88.6 us -> 43.7 us  [contract(): lax.dot_general(left, right, (((left_dim,), (right_dim,)), ((), ())), pre...]
    all_to_all x6 -> x0, waiting for transfers between devices: 40.9 us -> none  [the longest x1 12.9 us: per_device(): lax.all_to_all(q_tokens, 'seq', split_axis=1, concat_axis=0, tiled=True)]
    all_to_all x2 -> x0, blocking collectives: 35.2 us -> none  [the longest x1 19.3 us: per_device(): lax.all_to_all(k_tokens, 'seq', split_axis=1, concat_axis=0, tiled=True)]
    slice x48 -> x1, local copies, waits for them, and re-layouts: 26.6 us -> 0.91 us  [per_device(): whole_places[:, :tokens // 128].reshape(seq, fsdp, tokens)]
    all_to_all x6 -> x0, starting transfers between devices: 24.7 us -> none  [the longest x1 4.61 us: per_device(): lax.all_to_all(grad_mixed, 'seq', split_axis=0, concat_axis=1, tiled=True)]
  transfers between devices with their start and end apart: 10 -> 0, of which waited for: 7 -> 0; matrix products, arithmetic and copies ran while one was open for 8% -> 0% of each run, Pallas kernels for 0% -> 0%
where the time goes in v2:
time: 528 us; the launch traced here: 519 us
  Pallas kernels  416 us (79%)
  matrix products  52.4 us (10%)
  local copies, waits for them, and re-layouts  36.9 us (7%)
  other arithmetic  12.2 us (2%)
    pallas_call x1, Pallas kernels, reduce_all(): pl.pallas_call(functools.partial(reduce_kernel, pieces, n), out_shape=[ja...  118 us
    pallas_call x1, Pallas kernels, gather_all(): pl.pallas_call(functools.partial(gather_kernel, pieces, n), out_shape=[ja...  109 us
    pallas_call x1, Pallas kernels, grads_to_tokens(): pl.pallas_call(functools.partial(grads_to_tokens_kernel, tokens), out_sha...  46.3 us
    dot_general x18, matrix products, contract(): lax.dot_general(left, right, (((left_dim,), (right_dim,)), ((), ())), pre...  43.7 us
    pallas_call x1, Pallas kernels, to_heads(): pl.pallas_call(functools.partial(to_heads_kernel, tokens), out_shape=[few...  40.2 us
    pallas_call x1, Pallas kernels, attend_back(): pl.pallas_call(attend_back_kernel, out_shape=[jax.ShapeDtypeStruct(a.shap...  38.7 us
    pallas_call x1, Pallas kernels, attend(): pl.pallas_call(attend_kernel, out_shape=[jax.ShapeDtypeStruct((HEAD_DIM,...  28.3 us
    pallas_call x1, Pallas kernels, units_to_tokens(): pl.pallas_call(functools.partial(units_to_tokens_kernel, tokens), out_sha...  22 us

profile of v2, /device:TPU:0, one launch (start us, length us, event | category | flops | bytes accessed | tf_op | source)
XLA Modules:
  0.0 519.4 jit_solution(14180941985028319929)
XLA Ops:
  7.1 108.9 %shard_map.220 = (bf16[32,32,2816]{2,1,0:T(8,128)(2,1)}, bf16[32,32,2816]{2,1,0:T(8,128)(2,1)}, bf16[32,32,1024]{2,1,0:T(8,128)(2,1)}, bf16[32,32,1024]{2,1,0:T(...) custom-call(bf16[32,2816]{1,0:T(8,128)(2,1)} %refs_0_.1, ...), custom_call_target="tpu_custom_call" | custom-call | bytes 25952256 | tf_op jit(solution)/shard_map/pallas_call | solution.py:245
  120.8 3.4 fusion.3.v_ref
  124.2 2.6 copy.38
  126.7 3.5 fusion.12
  130.3 2.6 copy.37
  132.8 2.5 fusion.14
  136.8 40.2 %shard_map.221 = (bf16[64,4096]{1,0:T(8,128)(2,1)}, bf16[64,8192]{1,0:T(8,128)(2,1)}, bf16[64,8192]{1,0:T(8,128)(2,1)}) custom-call(bf16[1024,256]{1,0:T(8,128)(2,1)} %bitcast.141, bf16[1024,256]{1,0:T(8,128)(2,1)} %bitcast.142, bf16[1024,256]{1,0:T(8,128)(2,1)} %fusion.3.v_ref), custom_call_target="tpu_custom_call" | custom-call | bytes 4194304 | tf_op jit(solution)/shard_map/pallas_call | solution.py:709
  177.1 28.3 %shard_map.222 = (bf16[64,4096]{1,0:T(8,128)(2,1)}, f32[64,4096]{1,0:T(8,128)}, f32[1,4096]{1,0:T(1,128)}) custom-call(s32[4,8]{1,0:T(4,128)} %pad_add_fusion.bounds, bf16[64,4096]{1,0:T(8,128)(2,1)} %get-tuple-element.46.q_ref, bf16[64,8192]{1,0:T(8,128)(2,1)} %get-tuple-element.47.k_ref, bf16[64,8192]{1,0:T(8,128)(2,1)} %get-tuple-element.48.v_ref, ...), custom_call_target="tpu_custom_call" | custom-call | flops 2147483648 | bytes 2097152 | tf_op jit(solution)/shard_map/pallas_call | solution.py:1011
  205.3 22.0 %shard_map.223 = bf16[1024,256]{1,0:T(8,128)(2,1)} custom-call(bf16[64,4096]{1,0:T(8,128)(2,1)} %get-tuple-element.49.source), custom_call_target="tpu_custom_call" | custom-call | bytes 1048576 | tf_op jit(solution)/shard_map/pallas_call | solution.py:766
  229.4 4.4 fusion.38
  235.7 3.4 multiply_convert_fusion
  239.0 2.5 fusion.2
  248.3 13.8 %shard_map.224.g_ref = bf16[64,4096]{1,0:T(8,128)(2,1)} custom-call(bf16[1024,256]{1,0:T(8,128)(2,1)} %convolution_convert_fusion.7.source), custom_call_target="tpu_custom_call" | custom-call | bytes 1048576 | tf_op jit(solution)/shard_map/pallas_call | solution.py:742
  262.1 38.7 %shard_map.225 = (bf16[64,4096]{1,0:T(8,128)(2,1)}, bf16[64,8192]{1,0:T(8,128)(2,1)}, bf16[64,8192]{1,0:T(8,128)(2,1)}) custom-call(s32[4,8]{1,0:T(4,128)} %pad_add_fusion.bounds, bf16[64,4096]{1,0:T(8,128)(2,1)} %get-tuple-element.46.q_ref, bf16[64,8192]{1,0:T(8,128)(2,1)} %get-tuple-element.47.k_ref, bf16[64,8192]{1,0:T(8,128)(2,1)} %get-tuple-element.48.v_ref, ...), custom_call_target="tpu_custom_call" | custom-call | flops 5368709120 | bytes 3145728 | tf_op jit(solution)/shard_map/pallas_call | solution.py:1063
  300.8 46.3 %shard_map.226 = (bf16[1024,256]{1,0:T(8,128)(2,1)}, bf16[1024,256]{1,0:T(8,128)(2,1)}, bf16[1024,256]{1,0:T(8,128)(2,1)}) custom-call(bf16[64,4096]{1,0:T(8,128)(2,1)} %get-tuple-element.56.dq_ref, bf16[64,8192]{1,0:T(8,128)(2,1)} %get-tuple-element.57.dk_ref, bf16[64,8192]{1,0:T(8,128)(2,1)} %get-tuple-element.58.dv_ref), custom_call_target="tpu_custom_call" | custom-call | bytes 3145728 | tf_op jit(solution)/shard_map/pallas_call | solution.py:899
  356.4 9.9 %dynamic_update_slice.19.refs_7_ = f32[32,8,128]{2,1,0:T(8,128)S(1)} dynamic-update-slice(f32[32,8,128]{2,1,0:T(8,128)S(1)} %dynamic_update_slice.18, f32[32,1,32]{2,1,0:T(1,128)S(1)} %reshape.627, s32[]{:T(128)} %constant.79.clone.1, s32[]{:T(128)} %constant.78.clone.1, s32[]{:T(128)} %constant.79.clone.1) | dynamic-update-slice | bytes 8196 | tf_op jit(solution)/shard_map/dynamic_update_slice | solution.py:1233
  366.4 2.1 convolution_convert_fusion.3
  369.8 2.2 convolution_convert_fusion.4
  372.1 2.2 convolution_convert_fusion.5
  374.3 2.2 convolution_convert_fusion.6
  376.5 4.2 convolution_convert_fusion
  380.7 4.3 convolution_convert_fusion.1
  385.0 4.2 convolution_convert_fusion.2
  389.1 118.3 %shard_map.227 = (f32[32,2816]{1,0:T(8,128)}, f32[32,2816]{1,0:T(8,128)}, f32[32,1024]{1,0:T(8,128)}, f32[32,1024]{1,0:T(8,128)}, f32[88,1024]{1,0:T(8,128)}, /*...) custom-call(bf16[32,32,2816]{2,1,0:T(8,128)(2,1)} %bitcast.124, bf16[32,32,2816]{2,1,0:T(8,128)(2,1)} %bitcast.123, ...), custom_call_target="tpu_custom_call" | custom-call | bytes 51642368 | tf_op jit(solution)/shard_map/pallas_call | solution.py:422
  (129 shorter events, 45.4 us)
Async XLA Ops:
  0.6 120.2 %copy-start = (bf16[256,1024]{1,0:T(8,128)(2,1)S(1)}, bf16[256,1024]{1,0:T(8,128)(2,1)}, u32[]{:S(2)}) copy-start(bf16[256,1024]{1,0:T(8,128)(2,1)} %param.13) | copy-start | bytes 1572868
  4.8 2.3 copy-start.24
  120.8 3.4 copy-start.3
  126.7 3.5 copy-start.1
  132.8 2.5 copy-start.21
  177.1 50.2 %copy-start.10 = (bf16[32,32,1024]{2,1,0:T(8,128)(2,1)S(1)}, bf16[32,32,1024]{2,1,0:T(8,128)(2,1)}, u32[]{:S(2)}) copy-start(bf16[32,32,1024]{2,1,0:T(8,128)(2,1)} %get-tuple-element.50) | copy-start | bytes 6291460
  229.2 4.6 slice-start.2
  229.4 4.5 slice-start.3
  229.4 6.2 %slice-start.4 = ((s8[5767168]{0:T(1024)(128)(4,1)}), s8[4194304]{0:T(1024)(128)(4,1)S(1)}, s32[]{:S(2)}) async-start(s8[5767168]{0:T(1024)(128)(4,1)} %bitcast.160), calls=%async_computation.4 | async-start | bytes 8388608
  233.9 9.4 %slice-start = ((s8[5767168]{0:T(1024)(128)(4,1)}), s8[4194304]{0:T(1024)(128)(4,1)S(1)}, s32[]{:S(2)}) async-start(s8[5767168]{0:T(1024)(128)(4,1)} %bitcast.153), calls=%async_computation | async-start | bytes 8388608
  235.7 7.6 %slice-start.1 = ((s8[5767168]{0:T(1024)(128)(4,1)}), s8[1572864]{0:T(1024)(128)(4,1)S(1)}, s32[]{:S(2)}) async-start(s8[5767168]{0:T(1024)(128)(4,1)} %bitcast.153), calls=%async_computation.1 | async-start | bytes 3145728
  239.0 2.5 copy-start.8
  239.0 2.5 copy-start.17
  239.0 4.2 copy-start.19
  350.0 2.1 copy-start.6
  350.0 2.1 copy-start.4
  355.0 11.3 %copy-start.5 = (bf16[1024,256]{1,0:T(8,128)(2,1)S(1)}, bf16[1024,256]{1,0:T(8,128)(2,1)}, u32[]{:S(2)}) copy-start(bf16[1024,256]{1,0:T(8,128)(2,1)} %shard_map.223) | copy-start | bytes 1572868
  366.3 2.2 copy-start.22
  369.8 2.2 copy-start.7
  374.3 2.2 copy-start.9
  374.3 2.2 copy-start.16
  376.5 4.2 copy-start.20
  380.7 4.3 copy-start.18
  507.5 11.0 %copy-start.23 = (f32[88,1024]{1,0:T(8,128)S(1)}, f32[88,1024]{1,0:T(8,128)}, u32[]{:S(2)}) copy-start(f32[88,1024]{1,0:T(8,128)} %get-tuple-element.176) | copy-start | bytes 1081348
  (8 other events, 13.2 us)

commit v3 on v2

v3 whole, which is shorter than its diff:
```python
import functools, math
import jax
import jax.numpy as jnp
from jax import lax
from jax.experimental import pallas as pl
from jax.experimental.pallas import tpu as pltpu
from jax.sharding import PartitionSpec as P

EPSILON = 1e-06
MESH = pl.DeviceIdType.MESH


class Grid:
    def __init__(self):
        self.seq = lax.axis_size("seq")
        self.fsdp = lax.axis_size("fsdp")
        self.size = {"z": self.seq, "y": 2, "x": self.fsdp // 4}
        self.stride = {"x": 2, "y": 2 * (self.fsdp // 4)}
        self.total = self.seq * self.fsdp
        self.plane = self.total // 2

    def locate(self):
        z, f = lax.axis_index("seq"), lax.axis_index("fsdp")
        nx = self.size["x"]
        self.f, self.zi = f, z
        self.core = lax.rem(f, 2)
        self.me = {"z": z, "y": lax.div(f, 2 * nx), "x": lax.rem(lax.div(f, 2), nx)}

    def step(self, dim, delta):
        if dim == "z":
            return {"seq": self.zi + delta}
        if dim == "core":
            return {"fsdp": self.f + 1 - 2 * self.core}
        return {"fsdp": self.f + delta * self.stride[dim]}

    def partner(self, dim):
        return self.step(dim, 1 - 2 * self.me[dim])

    def dirs(self, dim):
        return (0,) if self.size[dim] == 2 else (1, -1)

    def linear(self, at, core):
        nx = self.size["x"]
        return at["z"] * self.fsdp + (at["y"] * nx + at["x"]) * 2 + core

    def neighbours(self):
        found = [(None, self.step("core", 1))]
        for dim in ("z", "y", "x"):
            n = self.size[dim]
            if n == 1:
                continue
            if n == 2:
                found.append((None, self.partner(dim)))
            else:
                found.append((self.me[dim] < n - 1, self.step(dim, 1)))
                found.append((self.me[dim] > 0, self.step(dim, -1)))
        return found

    def barrier(self):
        sem = pltpu.get_barrier_semaphore()
        count = 0
        for exists, device in self.neighbours():
            if exists is None:
                pl.semaphore_signal(sem, inc=1, device_id=device, device_id_type=MESH)
                count = count + 1
            else:

                @pl.when(exists)
                def _(device=device):
                    pl.semaphore_signal(sem, inc=1, device_id=device, device_id_type=MESH)

                count = count + exists.astype(jnp.int32)
        pl.semaphore_wait(sem, count)

    def digits(self, order, number):
        at, ok = {}, None
        rest = number
        for dim in order:
            n = self.size[dim]
            base = 2 if n == 2 else 2 * n - 1
            digit = lax.rem(rest, base)
            rest = lax.div(rest, base)
            if n == 2:
                at[dim] = lax.rem(self.me[dim] + digit, 2)
            elif n == 1:
                at[dim] = self.me[dim]
            else:
                away = lax.div(digit + 1, 2)
                at[dim] = jnp.where(lax.rem(digit, 2) == 1, self.me[dim] - away, self.me[dim] + away)
                inside = (at[dim] >= 0) & (at[dim] < n)
                ok = inside if ok is None else ok & inside
        return at, ok

    def places(self, order):
        return math.prod(2 if self.size[d] == 2 else 2 * self.size[d] - 1 for d in order)

    def rank(self, order, at, upto):
        value, width = 0, 1
        for dim in order[:upto]:
            value = value + at[dim] * width
            width *= self.size[dim]
        return value

    def slots(self, order):
        first, count, width = [], 0, 1
        for dim in order:
            width *= self.size[dim]
            first.append(count)
            if self.size[dim] > 1:
                count += width * len(self.dirs(dim))
        return first, count

    def branch(self, order, j, way, at):
        dim = order[j]
        n = self.size[dim]
        ok = None
        for later in order[j + 1 :]:
            same = at[later] == self.me[later]
            ok = same if ok is None else ok & same
        if n == 2:
            here = at[dim] == self.me[dim]
        elif way == 1:
            here = (at[dim] <= self.me[dim]) & (self.me[dim] < n - 1)
        else:
            here = (at[dim] >= self.me[dim]) & (self.me[dim] > 0)
        return here if ok is None else ok & here


ORDERS = {"A": ("z", "x", "y"), "B": ("x", "y", "z"), "C": ("y", "z", "x")}


class Gather:
    def __init__(self, grid, pieces, sources, outs, sems):
        self.grid, self.pieces, self.sources, self.outs = grid, pieces, sources, outs
        self.recv, self.send, self.core_send, self.own_sem = sems
        self.places = grid.places(ORDERS["A"])

    @staticmethod
    def semaphores(grid, pieces, arrays):
        slots = max(grid.slots(order)[1] for order in ORDERS.values())
        dma = pltpu.SemaphoreType.DMA
        return [
            dma((len(pieces), grid.total)),
            dma((len(pieces), slots)),
            dma((len(pieces), grid.plane)),
            dma((arrays,)),
        ]

    def own(self, i):
        mine = self.grid.linear(self.grid.me, self.grid.core)
        return pltpu.make_async_copy(self.sources[i], self.outs[i].at[mine], self.own_sem.at[i])

    def view(self, ref, p):
        return ref.at[:, pl.ds(self.pieces[p][1], self.pieces[p][2])]

    def sends(self, p, at, source, act):
        grid = self.grid
        order = ORDERS[self.pieces[p][3]]
        first, _ = grid.slots(order)
        number = grid.linear(at, grid.core)
        target = self.view(self.outs[self.pieces[p][0]].at[number], p)

        def copy(sem, device):
            return pltpu.make_async_remote_copy(
                src_ref=source,
                dst_ref=target,
                send_sem=sem,
                recv_sem=self.recv.at[p, number],
                device_id=device,
                device_id_type=MESH,
            )

        for j, dim in enumerate(order):
            if grid.size[dim] == 1:
                continue
            ways = grid.dirs(dim)
            for w, way in enumerate(ways):
                slot = first[j] + grid.rank(order, at, j + 1) * len(ways) + w
                device = grid.partner(dim) if way == 0 else grid.step(dim, way)

                @pl.when(grid.branch(order, j, way, at))
                def _(device=device, slot=slot):
                    act(copy(self.send.at[p, slot], device))

        act(copy(self.core_send.at[p, grid.rank(order, at, 3)], grid.step("core", 1)))

    def arrive(self, p, number):
        there = self.view(self.outs[self.pieces[p][0]].at[number], p)
        pltpu.make_async_remote_copy(
            src_ref=there,
            dst_ref=there,
            send_sem=self.core_send.at[p, 0],
            recv_sem=self.recv.at[p, number],
            device_id=self.grid.step("core", 1),
            device_id_type=MESH,
        ).wait_recv()

    def each(self, number, act):
        for p in range(len(self.pieces)):
            at, ok = self.grid.digits(ORDERS[self.pieces[p][3]], number)

            def run(p=p, at=at):
                act(p, at)

            if ok is None:
                run()
            else:
                pl.when(ok)(run)

    def start(self):
        for i in range(len(self.sources)):
            self.own(i).start()
        for p in range(len(self.pieces)):
            self.sends(
                p, self.grid.me, self.view(self.sources[self.pieces[p][0]], p), lambda c: c.start()
            )

    def relay(self, number):
        def act(p, at):
            where = self.grid.linear(at, self.grid.core)
            self.arrive(p, where)
            self.sends(p, at, self.view(self.outs[self.pieces[p][0]].at[where], p), lambda c: c.start())

        self.each(number, act)

    def finish(self):
        def act(p, at):
            self.arrive(p, self.grid.linear(at, 1 - self.grid.core))
            where = self.grid.linear(at, self.grid.core)
            self.sends(
                p, at, self.view(self.outs[self.pieces[p][0]].at[where], p), lambda c: c.wait_send()
            )

        def one(number, carry):
            self.each(number, act)
            return carry

        lax.fori_loop(0, self.places, one, 0)
        for i in range(len(self.sources)):
            self.own(i).wait()


def gather_kernel(pieces, n_arrays, *refs):
    grid = Grid()
    grid.locate()
    tree = Gather(grid, pieces, refs[:n_arrays], refs[n_arrays : 2 * n_arrays], refs[2 * n_arrays :])
    grid.barrier()
    tree.start()

    def forward(number, carry):
        tree.relay(number)
        return carry

    lax.fori_loop(1, tree.places, forward, 0)
    tree.finish()


def gathered_shapes(grid, arrays):
    return [jax.ShapeDtypeStruct((grid.total, *a.shape), a.dtype) for a in arrays]


def gather_all(arrays, pieces, ident):
    grid = Grid()
    n = len(arrays)
    moved = sum(a.size * a.dtype.itemsize for a in arrays) * grid.total
    return pl.pallas_call(
        functools.partial(gather_kernel, pieces, n),
        out_shape=gathered_shapes(grid, arrays),
        in_specs=[pl.BlockSpec(memory_space=pl.ANY)] * n,
        out_specs=[pl.BlockSpec(memory_space=pl.ANY)] * n,
        scratch_shapes=Gather.semaphores(grid, pieces, n),
        compiler_params=pltpu.CompilerParams(collective_id=ident, has_side_effects=True),
        cost_estimate=pl.CostEstimate(flops=0, bytes_accessed=moved, transcendentals=0),
    )(*arrays)


class Reduce:
    def __init__(self, grid, pieces, parts, outs, scratch):
        n = len(pieces)
        self.grid, self.pieces, self.parts, self.outs = grid, pieces, parts, outs
        self.pair, self.slot, self.held, self.total = (
            scratch[i * n : (i + 1) * n] for i in range(4)
        )
        sems = scratch[4 * n :]
        self.core_send, self.core_recv, self.tree_send, self.tree_recv, self.own_sem = sems
        self.places = grid.places(ORDERS["A"])

    @staticmethod
    def scratch(grid, pieces, arrays):
        most = max(grid.slots(order)[1] for order in ORDERS.values())
        shape = [(arrays[p[0]].shape[1], p[2]) for p in pieces]
        kind = [arrays[p[0]].dtype for p in pieces]
        count = [grid.slots(ORDERS[p[3]])[1] for p in pieces]
        dma = pltpu.SemaphoreType.DMA
        n = len(pieces)
        return (
            [pltpu.VMEM((grid.plane, *s), k) for s, k in zip(shape, kind)]
            + [pltpu.VMEM((c, *s), k) for c, s, k in zip(count, shape, kind)]
            + [pltpu.VMEM((2, *s), k) for s, k in zip(shape, kind)]
            + [pltpu.VMEM(s, jnp.float32) for s in shape]
            + [dma((n, grid.plane)), dma((n, grid.plane)), dma((n, grid.plane)), dma((n, most)), dma((n, 2))]
        )

    def each(self, number, act):
        for p in range(len(self.pieces)):
            at, ok = self.grid.digits(ORDERS[self.pieces[p][3]], number)

            def run(p=p, at=at):
                act(p, at)

            if ok is None:
                run()
            else:
                pl.when(ok)(run)

    def block(self, p, at, core):
        array, lower, count, _ = self.pieces[p]
        return self.parts[array].at[self.grid.linear(at, core), :, pl.ds(lower, count)]

    def rank(self, p, at):
        return self.grid.rank(ORDERS[self.pieces[p][3]], at, 3)

    def to_sibling(self, p, at):
        rank = self.rank(p, at)
        return pltpu.make_async_remote_copy(
            src_ref=self.block(p, at, 1 - self.grid.core),
            dst_ref=self.pair[p].at[rank],
            send_sem=self.core_send.at[p, rank],
            recv_sem=self.core_recv.at[p, rank],
            device_id=self.grid.step("core", 1),
            device_id_type=MESH,
        )

    def fetch(self, p, at, number):
        slot = lax.rem(number, 2)
        return pltpu.make_async_copy(
            self.block(p, at, self.grid.core), self.held[p].at[slot], self.own_sem.at[p, slot]
        )

    def to_parent(self, p, at, act):
        grid = self.grid
        order = ORDERS[self.pieces[p][3]]
        first, _ = grid.slots(order)
        rank = self.rank(p, at)
        for j, dim in enumerate(order):
            if grid.size[dim] == 1:
                continue
            ways = grid.dirs(dim)
            ok = None
            for later in order[j + 1 :]:
                same = at[later] == grid.me[later]
                ok = same if ok is None else ok & same
            for w, way in enumerate(ways):
                slot = first[j] + grid.rank(order, at, j + 1) * len(ways) + w
                if way == 0:
                    here, device = at[dim] != grid.me[dim], grid.partner(dim)
                elif way == 1:
                    here, device = at[dim] < grid.me[dim], grid.step(dim, -1)
                else:
                    here, device = at[dim] > grid.me[dim], grid.step(dim, 1)
                here = here if ok is None else ok & here

                @pl.when(here)
                def _(slot=slot, device=device):
                    act(
                        pltpu.make_async_remote_copy(
                            src_ref=self.pair[p].at[rank],
                            dst_ref=self.slot[p].at[slot],
                            send_sem=self.tree_send.at[p, rank],
                            recv_sem=self.tree_recv.at[p, slot],
                            device_id=device,
                            device_id_type=MESH,
                        )
                    )

    def combine(self, p, at, number):
        grid = self.grid
        order = ORDERS[self.pieces[p][3]]
        first, _ = grid.slots(order)
        rank = self.rank(p, at)
        total, slots = self.total[p], self.slot[p]
        self.to_sibling(p, at).wait_recv()
        self.fetch(p, at, number).wait()
        total[...] = self.held[p][lax.rem(number, 2)].astype(jnp.float32) + self.pair[p][
            rank
        ].astype(jnp.float32)
        for j in reversed(range(3)):
            dim = order[j]
            if grid.size[dim] == 1:
                continue
            ways = grid.dirs(dim)
            for w, way in enumerate(ways):
                slot = first[j] + grid.rank(order, at, j + 1) * len(ways) + w

                @pl.when(grid.branch(order, j, way, at))
                def _(slot=slot):
                    pltpu.make_async_remote_copy(
                        src_ref=slots.at[slot],
                        dst_ref=slots.at[slot],
                        send_sem=self.tree_send.at[p, rank],
                        recv_sem=self.tree_recv.at[p, slot],
                        device_id=grid.step("core", 1),
                        device_id_type=MESH,
                    ).wait_recv()
                    total[...] += slots[slot].astype(jnp.float32)

    def start(self):
        places = self.places

        def one(step, carry):
            self.each(places - 1 - step, lambda p, at: self.to_sibling(p, at).start())
            return carry

        self.each(places - 1, lambda p, at: self.fetch(p, at, places - 1).start())
        lax.fori_loop(0, places, one, 0)

    def climb(self, step):
        number = self.places - 1 - step
        self.each(number - 1, lambda p, at: self.fetch(p, at, number - 1).start())

        def work(p, at):
            self.combine(p, at, number)
            self.pair[p][self.rank(p, at)] = self.total[p][...].astype(self.pair[p].dtype)
            self.to_parent(p, at, lambda copy: copy.start())

        self.each(number, work)

    def finish(self):
        def root(p, at):
            self.combine(p, at, 0)
            array, lower, count, _ = self.pieces[p]
            self.outs[array][:, lower : lower + count] = self.total[p][...]

        self.each(0, root)

        def one(number, carry):
            def drain(p, at):
                self.to_sibling(p, at).wait_send()

                @pl.when(number > 0)
                def _():
                    self.to_parent(p, at, lambda copy: copy.wait_send())

            self.each(number, drain)
            return carry

        lax.fori_loop(0, self.places, one, 0)


def reduce_kernel(pieces, n_arrays, *refs):
    grid = Grid()
    grid.locate()
    tree = Reduce(grid, pieces, refs[:n_arrays], refs[n_arrays : 2 * n_arrays], refs[2 * n_arrays :])
    grid.barrier()
    tree.start()

    def climb(step, carry):
        tree.climb(step)
        return carry

    lax.fori_loop(0, tree.places - 1, climb, 0)
    tree.finish()


VMEM_LIMIT = 60 << 20


def summed_shapes(arrays):
    return [jax.ShapeDtypeStruct(a.shape[1:], jnp.float32) for a in arrays]


def reduce_all(arrays, pieces, ident):
    grid = Grid()
    n = len(arrays)
    moved = sum(a.size * a.dtype.itemsize for a in arrays)
    return pl.pallas_call(
        functools.partial(reduce_kernel, pieces, n),
        out_shape=summed_shapes(arrays),
        in_specs=[pl.BlockSpec(memory_space=pl.ANY)] * n,
        out_specs=[pl.BlockSpec(memory_space=pltpu.VMEM)] * n,
        scratch_shapes=Reduce.scratch(grid, pieces, arrays),
        compiler_params=pltpu.CompilerParams(
            collective_id=ident, has_side_effects=True, vmem_limit_bytes=VMEM_LIMIT
        ),
        cost_estimate=pl.CostEstimate(flops=0, bytes_accessed=2 * moved, transcendentals=0),
    )(*arrays)


HEADS = 16
HEAD_DIM = 64
UNIT = 128
NEGATIVE = -1e30


class Owners:
    def __init__(self, tokens):
        self.seq, self.fsdp = lax.axis_size("seq"), lax.axis_size("fsdp")
        self.total = self.seq * self.fsdp
        self.members = self.total // HEADS
        self.heads_here = HEADS // self.seq
        self.tokens = tokens
        self.halves = tokens // UNIT
        self.units = self.halves * self.total // self.members

    def locate(self):
        s, f = lax.axis_index("seq"), lax.axis_index("fsdp")
        self.s, self.f = s, f
        self.linear = s * self.fsdp + f
        self.block = f * self.seq + s
        self.head = s * self.heads_here + lax.div(f, self.members)
        self.member = lax.rem(f, self.members)

    def of_head(self, head, member):
        return {
            "seq": lax.div(head, self.heads_here),
            "fsdp": lax.rem(head, self.heads_here) * self.members + member,
        }

    def of_block(self, block):
        return {"seq": lax.rem(block, self.seq), "fsdp": lax.div(block, self.seq)}

    def barrier(self):
        sem = pltpu.get_barrier_semaphore()

        def greet(delta, carry):
            other = lax.rem(self.linear + delta, self.total)
            device = {"seq": lax.div(other, self.fsdp), "fsdp": lax.rem(other, self.fsdp)}
            pl.semaphore_signal(sem, inc=1, device_id=device, device_id_type=MESH)
            return carry

        lax.fori_loop(1, self.total, greet, 0)
        pl.semaphore_wait(sem, self.total - 1)


def remote(source, target, send_sem, recv_sem, device):
    return pltpu.make_async_remote_copy(
        src_ref=source,
        dst_ref=target,
        send_sem=send_sem,
        recv_sem=recv_sem,
        device_id=device,
        device_id_type=MESH,
    )


def head_rows(head):
    return pl.ds(pl.multiple_of(head * HEAD_DIM, HEAD_DIM), HEAD_DIM)


def lanes(number, width):
    return pl.ds(pl.multiple_of(number * width, width), width)


def spread_units(own, source, target, send, recv, local, act):
    def to_head(delta, carry):
        head = lax.rem(own.head + delta, HEADS)
        for half in range(own.halves):
            unit = own.halves * own.block + half
            member = lax.rem(unit, own.members)
            place = lax.div(unit, own.members)
            piece = source.at[head_rows(head), pl.ds(half * UNIT, UNIT)]
            there = target.at[:, lanes(place, UNIT)]
            here = (head == own.head) & (member == own.member)

            @pl.when(here)
            def _(piece=piece, there=there, half=half):
                copy = pltpu.make_async_copy(piece, there, local.at[half])
                copy.start() if act == "start" else copy.wait()

            @pl.when(jnp.logical_not(here))
            def _(piece=piece, there=there, half=half, member=member, place=place, head=head):
                copy = remote(
                    piece, there, send.at[head, half], recv.at[place], own.of_head(head, member)
                )
                copy.start() if act == "start" else copy.wait_send()

        return carry

    lax.fori_loop(0, HEADS, to_head, 0)


def await_units(own, target, send, recv):
    def one(place, carry):
        unit = place * own.members + own.member
        there = target.at[:, lanes(place, UNIT)]

        @pl.when(lax.div(unit, own.halves) != own.block)
        def _():
            remote(
                there, there, send.at[0, 0], recv.at[place], own.of_block(0)
            ).wait_recv()

        return carry

    lax.fori_loop(0, own.units, one, 0)


def collect_units(own, source, target, send, recv, local, act, first, count):
    def one(step, carry):
        place = first + step
        unit = place * own.members + own.member
        block, half = lax.div(unit, own.halves), lax.rem(unit, own.halves)
        piece = source.at[:, lanes(place, UNIT)]
        there = target.at[head_rows(own.head), lanes(half, UNIT)]

        @pl.when(block == own.block)
        def _():
            copy = pltpu.make_async_copy(piece, there, local.at[half])
            copy.start() if act == "start" else copy.wait()

        @pl.when(block != own.block)
        def _():
            copy = remote(
                piece, there, send.at[place], recv.at[own.head, half], own.of_block(block)
            )
            copy.start() if act == "start" else copy.wait_send()

        return carry

    lax.fori_loop(0, count, one, 0)


def await_heads(own, target, send, recv):
    def one(head, carry):
        for half in range(own.halves):
            unit = own.halves * own.block + half
            there = target.at[head_rows(head), pl.ds(half * UNIT, UNIT)]

            @pl.when((head != own.head) | (lax.rem(unit, own.members) != own.member))
            def _(there=there, half=half):
                remote(
                    there, there, send.at[0], recv.at[head, half], own.of_block(0)
                ).wait_recv()

        return carry

    lax.fori_loop(0, HEADS, one, 0)


QUERIES = 512
KEYS = 1024
BESIDE_EXCHANGE = 2
BESIDE_TILES = 2
ANY = pl.BlockSpec(memory_space=pl.ANY)
WHOLE = pl.BlockSpec(memory_space=pltpu.VMEM)


def plain(left, right):
    return lax.dot_general(left, right, (((1,), (0,)), ((), ())), preferred_element_type=jnp.float32)


def first_dims(left, right):
    return lax.dot_general(left, right, (((0,), (0,)), ((), ())), preferred_element_type=jnp.float32)


def last_dims(left, right):
    return lax.dot_general(left, right, (((1,), (1,)), ((), ())), preferred_element_type=jnp.float32)


class Tiles:
    def __init__(self, own):
        self.span = QUERIES * own.members
        self.groups = own.units * UNIT // QUERIES
        self.longest = own.total * own.tokens // 2

    def fold(self, group, body, state):
        start = group * self.span
        low = lax.div(jnp.maximum(start - self.longest + 1, 0), KEYS)
        edge, high = lax.div(start, KEYS), lax.div(start + self.span + KEYS - 1, KEYS)
        state = lax.fori_loop(low, edge, lambda tile, s: body(tile, False, s), state)
        return lax.fori_loop(edge, high, lambda tile, s: body(tile, True, s), state)


def key_lanes(tile):
    return pl.ds(pl.multiple_of(tile * KEYS, KEYS), KEYS)


def group_lanes(group):
    return pl.ds(pl.multiple_of(group * QUERIES, QUERIES), QUERIES)


def shown(scores, tile, causal, pos, begin):
    number = tile * KEYS + lax.broadcasted_iota(jnp.int32, (KEYS, 1), 0)
    allowed = number >= begin
    if causal:
        allowed = allowed & (number <= pos)
    return jnp.where(allowed, scores, NEGATIVE)


def attend_group(tiles, group, q_ref, k_ref, v_ref, pos_ref, begin_ref, step, number):
    here = group_lanes(group)
    queries, pos, begin = q_ref[:, here], pos_ref[:, here], begin_ref[:, here]

    def body(tile, causal, current):
        number, top, total, summed = current
        number = step(number)
        scores = shown(first_dims(k_ref[:, key_lanes(tile)], queries), tile, causal, pos, begin)
        new_top = jnp.maximum(top, jnp.max(scores, axis=0, keepdims=True))
        weights = jnp.exp(scores - new_top)
        shrink = jnp.exp(top - new_top)
        total = total * shrink + jnp.sum(weights, axis=0, keepdims=True)
        summed = summed * shrink + plain(v_ref[:, key_lanes(tile)], weights.astype(jnp.bfloat16))
        return number, new_top, total, summed

    number, top, total, summed = tiles.fold(
        group,
        body,
        (
            number,
            jnp.full((1, QUERIES), NEGATIVE, jnp.float32),
            jnp.zeros((1, QUERIES), jnp.float32),
            jnp.zeros((HEAD_DIM, QUERIES), jnp.float32),
        ),
    )
    return summed / total, top + jnp.log(total), number


class ToHeads:
    def __init__(self, own, sources, targets, sems):
        self.own = own
        self.q_ref, *pairs = sources
        self.q_out, *outs = targets
        self.pairs = tuple(zip(pairs, outs))
        self.q_send, self.q_recv, self.q_local, self.send, self.recv, self.local, self.hand_send = sems
        self.shares = own.total // own.members
        self.mine = lax.div(own.f, own.members) * own.seq + own.s

    @staticmethod
    def semaphores(own):
        dma = pltpu.SemaphoreType.DMA
        return [
            dma((HEADS, own.halves)),
            dma((own.units,)),
            dma((own.halves,)),
            dma((2, HEADS)),
            dma((2, own.total)),
            dma((2,)),
            dma((2, own.total // own.members * (own.members - 1))),
        ]

    def keys(self, act):
        own = self.own

        def to_head(delta, carry):
            head = lax.rem(own.head + delta, HEADS)
            for i, (source, target) in enumerate(self.pairs):
                piece = source.at[head_rows(head), :]
                there = target.at[:, lanes(own.block, own.tokens)]

                @pl.when(head == own.head)
                def _(piece=piece, there=there, i=i):
                    copy = pltpu.make_async_copy(piece, there, self.local.at[i])
                    copy.start() if act == "start" else copy.wait()

                @pl.when(head != own.head)
                def _(piece=piece, there=there, i=i):
                    copy = remote(
                        piece,
                        there,
                        self.send.at[i, head],
                        self.recv.at[i, own.block],
                        own.of_head(head, own.member),
                    )
                    copy.start() if act == "start" else copy.wait_send()

            return carry

        lax.fori_loop(0, HEADS, to_head, 0)

    def hand(self, i, order, block, source, act):
        own = self.own
        for away in range(1, own.members):
            member = lax.rem(own.member + away, own.members)
            copy = remote(
                source,
                self.pairs[i][1].at[:, lanes(block, own.tokens)],
                self.hand_send.at[i, order * (own.members - 1) + away - 1],
                self.recv.at[i, block],
                own.of_head(own.head, member),
            )
            copy.start() if act == "start" else copy.wait_send()

    def hand_own(self, act):
        for i, (source, _) in enumerate(self.pairs):
            self.hand(i, self.shares - 1, self.own.block, source.at[head_rows(self.own.head), :], act)

    def block_of(self, step):
        order = lax.rem(self.mine + step, self.shares)
        f = self.own.member + self.own.members * lax.div(order, self.own.seq)
        return f * self.own.seq + lax.rem(order, self.own.seq)

    def arrive(self, i, block):
        there = self.pairs[i][1].at[:, lanes(block, self.own.tokens)]
        remote(
            there, there, self.send.at[i, 0], self.recv.at[i, block], self.own.of_block(0)
        ).wait_recv()
        return there

    def start(self):
        self.keys("start")
        spread_units(self.own, self.q_ref, self.q_out, self.q_send, self.q_recv, self.q_local, "start")
        self.hand_own("start")

    def relay(self, step):
        block = self.block_of(step)
        for i in range(2):
            self.hand(i, step - 1, block, self.arrive(i, block), "start")

    def finish(self):
        own = self.own

        def rest(block, carry):
            @pl.when(lax.rem(lax.div(block, own.seq), own.members) != own.member)
            def _():
                for i in range(2):
                    self.arrive(i, block)

            return carry

        lax.fori_loop(0, own.total, rest, 0)
        await_units(own, self.q_out, self.q_send, self.q_recv)
        self.keys("wait")
        spread_units(own, self.q_ref, self.q_out, self.q_send, self.q_recv, self.q_local, "wait")
        self.hand_own("wait")

        def settle(step, carry):
            block = self.block_of(step)
            for i, (_, target) in enumerate(self.pairs):
                self.hand(i, step - 1, block, target.at[:, lanes(block, own.tokens)], "wait")
            return carry

        lax.fori_loop(1, self.shares, settle, 0)


def forward_kernel(tokens, pieces, n, *refs):
    tokens_of = refs[:3]
    pos_ref, begin_ref = refs[3:5]
    sources = refs[5 : 5 + n]
    wholes = refs[5 + n : 5 + 2 * n]
    keep = refs[5 + 2 * n : 8 + 2 * n]
    out_ref, lse_ref, back_ref = refs[8 + 2 * n : 11 + 2 * n]
    *heads, low_ref = refs[11 + 2 * n : 15 + 2 * n]
    sems = refs[15 + 2 * n :]
    grid, own = Grid(), Owners(tokens)
    grid.locate()
    own.locate()
    tree = Gather(grid, pieces, sources, wholes, sems[:4])
    exchange = ToHeads(own, tokens_of, heads, sems[4:11])
    out_send, out_recv, out_local, keep_sem = sems[11:]
    tiles = Tiles(own)

    own.barrier()
    exchange.start()
    tree.start()

    def paced(every, first):
        def advance(count):
            number = lax.div(count, every)

            @pl.when((lax.rem(count, every) == 0) & (number < tree.places))
            def _():
                tree.relay(number)

            return count + 1

        return advance, first * every

    beside, count = paced(BESIDE_EXCHANGE, 1)

    def relay(step, count):
        exchange.relay(step)
        return beside(count)

    count = lax.fori_loop(1, exchange.shares, relay, jnp.int32(count))
    number = lax.div(count + BESIDE_EXCHANGE - 1, BESIDE_EXCHANGE)
    advance, number = paced(BESIDE_TILES, number)
    exchange.finish()
    keeping = [pltpu.make_async_copy(heads[i], keep[i], keep_sem.at[i]) for i in range(3)]
    for copy in keeping:
        copy.start()
    units = QUERIES // UNIT

    def one_group(group, number):
        here = group_lanes(group)
        attended, lse, number = attend_group(
            tiles, group, *heads, pos_ref, begin_ref, advance, number
        )
        out_ref[:, here] = attended
        lse_ref[:, here] = lse
        low_ref[:, here] = attended.astype(low_ref.dtype)
        collect_units(
            own, low_ref, back_ref, out_send, out_recv, out_local, "start", group * units, units
        )
        return number

    number = lax.fori_loop(0, tiles.groups, one_group, number)
    number = lax.div(number + BESIDE_TILES - 1, BESIDE_TILES)

    def last(number, carry):
        tree.relay(number)
        return carry

    lax.fori_loop(number, tree.places, last, 0)
    await_heads(own, back_ref, out_send, out_recv)
    collect_units(own, low_ref, back_ref, out_send, out_recv, out_local, "wait", 0, own.units)
    tree.finish()
    for copy in keeping:
        copy.wait()


def forward(q, k, v, pos, begin, arrays, pieces, ident):
    tokens, kind = q.shape[1], q.dtype
    grid, own = Grid(), Owners(tokens)
    n = len(arrays)
    count = own.units * UNIT
    dma = pltpu.SemaphoreType.DMA
    heads = [(HEAD_DIM, count)] + [(HEAD_DIM, own.total * tokens)] * 2
    pairs = count * own.total * tokens // 3
    moved = sum(a.size * a.dtype.itemsize for a in arrays) * grid.total
    outs = pl.pallas_call(
        functools.partial(forward_kernel, tokens, pieces, n),
        out_shape=gathered_shapes(grid, arrays)
        + [jax.ShapeDtypeStruct(s, kind) for s in heads]
        + [
            jax.ShapeDtypeStruct((HEAD_DIM, count), jnp.float32),
            jax.ShapeDtypeStruct((1, count), jnp.float32),
            jax.ShapeDtypeStruct(q.shape, kind),
        ],
        in_specs=[ANY] * 3 + [WHOLE] * 2 + [ANY] * n,
        out_specs=[ANY] * (n + 3) + [WHOLE] * 2 + [ANY],
        scratch_shapes=[pltpu.VMEM(s, kind) for s in heads]
        + [pltpu.VMEM((HEAD_DIM, count), kind)]
        + Gather.semaphores(grid, pieces, n)
        + ToHeads.semaphores(own)
        + [dma((own.units,)), dma((HEADS, own.halves)), dma((own.halves,)), dma((3,))],
        compiler_params=pltpu.CompilerParams(
            collective_id=ident, has_side_effects=True, vmem_limit_bytes=VMEM_LIMIT
        ),
        cost_estimate=pl.CostEstimate(
            flops=pairs * 4 * HEAD_DIM, bytes_accessed=moved, transcendentals=pairs
        ),
    )(q, k, v, pos, begin, *arrays)
    return outs[:n], outs[n : n + 3], outs[n + 3 :]


class GradsBack:
    def __init__(self, own, sums, outs, give_from, given, held, sems):
        self.own, self.sums, self.outs = own, sums, outs
        self.give_from, self.given, self.held = give_from, given, held
        self.give_send, self.give_recv, self.send, self.recv, self.local = sems
        self.shares = own.total // own.members
        self.others = own.members - 1
        self.mine = lax.div(own.f, own.members) * own.seq + own.s

    @staticmethod
    def scratch(own, kind):
        shares, others = own.total // own.members, own.members - 1
        dma = pltpu.SemaphoreType.DMA
        blocks = (2, shares * others, HEAD_DIM, own.tokens)
        return [
            pltpu.VMEM(blocks, kind),
            pltpu.VMEM(blocks, kind),
            pltpu.VMEM((2, shares, HEAD_DIM, own.tokens), kind),
            dma((2, shares * others)),
            dma((2, shares * others)),
            dma((2, shares)),
            dma((2, HEADS)),
            dma((2,)),
        ]

    def block_of(self, order, member):
        f = member + self.own.members * lax.div(order, self.own.seq)
        return f * self.own.seq + lax.rem(order, self.own.seq)

    def given_at(self, i, slot):
        there = self.given.at[i, slot]
        remote(
            there, there, self.give_send.at[i, 0], self.give_recv.at[i, slot], self.own.of_block(0)
        ).wait_recv()
        return self.given[i, slot].astype(jnp.float32)

    def give(self, act):
        own = self.own

        def one(step, carry):
            order = lax.rem(self.mine + step, self.shares)
            for away in range(1, own.members):
                member = lax.rem(own.member + away, own.members)
                columns = lanes(self.block_of(order, member), own.tokens)
                out, back = order * self.others + away - 1, order * self.others + self.others - away
                for i in range(2):
                    if act == "start":
                        self.give_from[i, out] = self.sums[i][:, columns].astype(self.held.dtype)
                    copy = remote(
                        self.give_from.at[i, out],
                        self.given.at[i, back],
                        self.give_send.at[i, out],
                        self.give_recv.at[i, back],
                        own.of_head(own.head, member),
                    )
                    copy.start() if act == "start" else copy.wait_send()
            return carry

        lax.fori_loop(1, self.shares + 1, one, 0)

    def back(self, order, i, act):
        own = self.own
        block = self.block_of(order, own.member)
        there = self.outs[i].at[head_rows(own.head), :]

        @pl.when(block == own.block)
        def _():
            copy = pltpu.make_async_copy(self.held.at[i, order], there, self.local.at[i])
            copy.start() if act == "start" else copy.wait()

        @pl.when(block != own.block)
        def _():
            copy = remote(
                self.held.at[i, order],
                there,
                self.send.at[i, order],
                self.recv.at[i, own.head],
                own.of_block(block),
            )
            copy.start() if act == "start" else copy.wait_send()

    def add(self, step):
        order = lax.rem(self.mine + step, self.shares)
        columns = lanes(self.block_of(order, self.own.member), self.own.tokens)
        for i in range(2):
            total = self.sums[i][:, columns]
            for j in range(self.others):
                total = total + self.given_at(i, order * self.others + j)
            self.held[i, order] = total.astype(self.held.dtype)
            self.back(order, i, "start")

    def finish(self):
        def arrive(head, carry):
            @pl.when(head != self.own.head)
            def _():
                for i in range(2):
                    there = self.outs[i].at[head_rows(head), :]
                    remote(
                        there, there, self.send.at[i, 0], self.recv.at[i, head], self.own.of_block(0)
                    ).wait_recv()

            return carry

        lax.fori_loop(0, HEADS, arrive, 0)
        self.give("wait")

        def settle(order, carry):
            for i in range(2):
                self.back(order, i, "wait")
            return carry

        lax.fori_loop(0, self.shares, settle, 0)


def backward_kernel(tokens, pieces, n, n_tree, *refs):
    g_ref, q_ref, k_ref, v_ref, out_ref, lse_ref, pos_ref, begin_ref = refs[:8]
    parts = refs[8 : 8 + n]
    dq_out, dk_out, dv_out = refs[8 + n : 11 + n]
    sums = refs[11 + n : 11 + 2 * n]
    rest = refs[11 + 2 * n :]
    tree_scratch, rest = rest[:n_tree], rest[n_tree:]
    grads_ref, dq_ref, dk_sum, dv_sum = rest[:4]
    back_scratch, sems = rest[4:12], rest[12:]
    own = Owners(tokens)
    own.locate()
    tree = None
    if n:
        grid = Grid()
        grid.locate()
        tree = Reduce(grid, pieces, parts, sums, tree_scratch)
    grads_back = GradsBack(own, (dk_sum, dv_sum), (dk_out, dv_out), *back_scratch[:3], back_scratch[3:])
    g_send, g_recv, g_local, dq_send, dq_recv, dq_local = sems
    tiles = Tiles(own)

    own.barrier()
    spread_units(own, g_ref, grads_ref, g_send, g_recv, g_local, "start")
    if tree:
        tree.start()
    dk_sum[...] = jnp.zeros_like(dk_sum)
    dv_sum[...] = jnp.zeros_like(dv_sum)

    def advance(number):
        if tree:

            @pl.when(number < tree.places - 1)
            def _():
                tree.climb(number)

        return number + 1

    number = advance(jnp.int32(0))
    await_units(own, grads_ref, g_send, g_recv)
    spread_units(own, g_ref, grads_ref, g_send, g_recv, g_local, "wait")
    units = QUERIES // UNIT

    def one_group(group, number):
        here = group_lanes(group)
        queries, grads = q_ref[:, here], grads_ref[:, here]
        pos, begin, lse = pos_ref[:, here], begin_ref[:, here], lse_ref[:, here]
        delta = jnp.sum(grads.astype(jnp.float32) * out_ref[:, here], axis=0, keepdims=True)

        def body(tile, causal, current):
            number, dq = current
            number = advance(number)
            there = key_lanes(tile)
            keys = k_ref[:, there]
            scores = shown(first_dims(keys, queries), tile, causal, pos, begin)
            probs = jnp.exp(scores - lse)
            dv_sum[:, there] += last_dims(grads, probs.astype(jnp.bfloat16))
            dscores = (probs * (first_dims(v_ref[:, there], grads) - delta)).astype(jnp.bfloat16)
            dk_sum[:, there] += last_dims(queries, dscores)
            return number, dq + plain(keys, dscores)

        number, dq = tiles.fold(
            group, body, (number, jnp.zeros((HEAD_DIM, QUERIES), jnp.float32))
        )
        dq_ref[:, here] = (dq * HEAD_DIM**-0.5).astype(dq_ref.dtype)
        collect_units(
            own, dq_ref, dq_out, dq_send, dq_recv, dq_local, "start", group * units, units
        )
        return number

    number = lax.fori_loop(0, tiles.groups, one_group, number)
    grads_back.give("start")

    def add(step, number):
        grads_back.add(step)
        return number

    number = lax.fori_loop(1, grads_back.shares + 1, add, number)
    if tree:

        def last(number, carry):
            tree.climb(number)
            return carry

        lax.fori_loop(number, tree.places - 1, last, 0)
    await_heads(own, dq_out, dq_send, dq_recv)
    collect_units(own, dq_ref, dq_out, dq_send, dq_recv, dq_local, "wait", 0, own.units)
    grads_back.finish()
    if tree:
        tree.finish()


def backward(grads, q, k, v, out, lse, pos, begin, arrays, pieces, ident):
    tokens, kind = grads.shape[1], grads.dtype
    grid, own = Grid(), Owners(tokens)
    n = len(arrays)
    count = own.units * UNIT
    dma = pltpu.SemaphoreType.DMA
    tree_scratch = Reduce.scratch(grid, pieces, arrays) if n else []
    pairs = count * own.total * tokens // 3
    moved = sum(a.size * a.dtype.itemsize for a in arrays) + 6 * k.size
    unit_sems = [
        [dma((HEADS, own.halves)), dma((own.units,)), dma((own.halves,))],
        [dma((own.units,)), dma((HEADS, own.halves)), dma((own.halves,))],
    ]
    outs = pl.pallas_call(
        functools.partial(backward_kernel, tokens, pieces, n, len(tree_scratch)),
        out_shape=[jax.ShapeDtypeStruct(grads.shape, kind)] * 3 + summed_shapes(arrays),
        in_specs=[ANY] + [WHOLE] * 7 + [ANY] * n,
        out_specs=[ANY] * 3 + [WHOLE] * n,
        scratch_shapes=tree_scratch
        + [pltpu.VMEM((HEAD_DIM, count), kind)] * 2
        + [pltpu.VMEM(k.shape, jnp.float32)] * 2
        + GradsBack.scratch(own, kind)
        + unit_sems[0]
        + unit_sems[1],
        compiler_params=pltpu.CompilerParams(
            collective_id=ident, has_side_effects=True, vmem_limit_bytes=VMEM_LIMIT
        ),
        cost_estimate=pl.CostEstimate(
            flops=pairs * 10 * HEAD_DIM, bytes_accessed=moved, transcendentals=pairs
        ),
    )(grads, q, k, v, out, lse, pos, begin, *arrays)
    return outs[:3], outs[3:]


def publish_kernel(*refs):
    half = len(refs) // 2
    for source, target in zip(refs[:half], refs[half:]):
        target[...] = source[...]


def publish(arrays):
    return pl.pallas_call(
        publish_kernel,
        out_shape=[jax.ShapeDtypeStruct(a.shape, a.dtype) for a in arrays],
        in_specs=[WHOLE] * len(arrays),
        out_specs=[WHOLE] * len(arrays),
        compiler_params=pltpu.CompilerParams(vmem_limit_bytes=VMEM_LIMIT),
    )(*arrays)


def plan(columns, *pieces):
    found, used = [], [0] * len(columns)
    for array, part, order in pieces:
        count = columns[array] if part is None else part
        count = min(count, columns[array] - used[array])
        found.append((array, used[array], count, order))
        used[array] += count
    return found


def rms_scale(tensor):
    return lax.rsqrt(jnp.mean(tensor * tensor, axis=-1, keepdims=True) + EPSILON)


def angle_tables(offsets):
    half_dim = HEAD_DIM // 2
    frequency = jnp.power(10000.0, -jnp.arange(half_dim, dtype=jnp.float32) / half_dim)
    angles = frequency[:, None] * offsets.astype(jnp.float32)[None, :]
    return jnp.cos(angles)[None], jnp.sin(angles)[None]


def rotate(tensor, cosine, sine_tab):
    pairs = tensor.reshape(HEADS, 2, HEAD_DIM // 2, -1)
    front, back = pairs[:, 0], pairs[:, 1]
    turned = jnp.stack([front * cosine - back * sine_tab, back * cosine + front * sine_tab], axis=1)
    return turned.reshape(tensor.shape)


def matmul(left, right):
    return jnp.dot(left, right, preferred_element_type=jnp.float32)


def contract(left, right, left_dim, right_dim):
    return lax.dot_general(
        left, right, (((left_dim,), (right_dim,)), ((), ())), preferred_element_type=jnp.float32
    )


def per_device(
    layer_input,
    v_first,
    offsets,
    g_attn,
    w_query,
    w_key,
    w_value,
    w_out,
    g_ffn,
    w_gate,
    w_up,
    w_down,
    out_cot,
):
    low = jnp.bfloat16
    tokens = layer_input.shape[0]
    seq, fsdp = lax.axis_size("seq"), lax.axis_size("fsdp")
    devices = seq * fsdp
    seq_index = lax.axis_index("seq")
    own_offsets = lax.dynamic_slice_in_dim(offsets, seq_index * tokens, tokens, 0)

    share = g_attn.shape[0]
    neighbours = 128 // share
    turn = lax.rem(seq_index * fsdp + lax.axis_index("fsdp"), neighbours) * share
    gains = jnp.zeros((16, 128), low)
    gains = lax.dynamic_update_slice(gains, jnp.stack([g_attn, g_ffn]), (0, turn))
    places = jnp.zeros((8, 128), jnp.int32)
    places = lax.dynamic_update_slice(places, own_offsets.reshape(-1, 128), (0, 0))
    first = (w_query, w_key, w_value, gains, places)
    half = w_key.shape[1] // 2
    first_plan = plan(
        [shard.shape[1] for shard in first],
        (0, None, "A"), (1, half, "A"), (1, half, "B"), (2, None, "C"), (3, None, "C"), (4, None, "C"),
    )
    later = (w_gate, w_up, w_down, w_out)
    later_plan = plan(
        [shard.shape[1] for shard in later],
        (0, None, "A"), (1, None, "A"), (2, None, "C"), (3, half, "A"), (3, half, "B"),
    )
    *wholes, whole_gains, whole_places = gather_all(first, first_plan, 0)
    proj_query, proj_key, proj_value = (whole.reshape(-1, whole.shape[2]) for whole in wholes)
    whole_gains = whole_gains.reshape(-1, neighbours, 16, 128).astype(jnp.float32).sum(1)
    gain_attn, gain_ffn = whole_gains[:, 0].reshape(-1), whole_gains[:, 1].reshape(-1)
    all_offsets = (
        whole_places[:, : tokens // 128].reshape(seq, fsdp, tokens).transpose(1, 0, 2).reshape(-1)
    )

    own = Owners(tokens)
    member = lax.rem(lax.axis_index("fsdp"), own.members)
    unit_begins = (jnp.arange(devices * tokens, dtype=jnp.int32) - all_offsets).reshape(
        own.units, own.members, UNIT
    )
    begin = lax.dynamic_index_in_dim(unit_begins, member, 1, keepdims=False).reshape(1, -1)
    pos = (
        (jnp.arange(own.units, dtype=jnp.int32)[:, None] * own.members + member) * UNIT
        + jnp.arange(UNIT, dtype=jnp.int32)[None]
    ).reshape(1, -1)

    cosine, sine_tab = angle_tables(own_offsets)
    input_f32 = layer_input.astype(jnp.float32)
    norm_attn = rms_scale(input_f32)
    normed_a = (input_f32 * norm_attn * gain_attn).astype(low)
    scale = jnp.asarray(HEAD_DIM**-0.5, low)
    q_tokens = rotate(lax.optimization_barrier(contract(proj_query, normed_a, 0, 1)), cosine, sine_tab).astype(low) * scale
    k_tokens = rotate(lax.optimization_barrier(contract(proj_key, normed_a, 0, 1)), cosine, sine_tab).astype(low)
    mixed = (
        0.5 * contract(proj_value, normed_a, 0, 1) + 0.5 * v_first.astype(jnp.float32).T
    ).astype(low)
    wholes, heads, (attended, lse, attn_tokens) = forward(
        q_tokens, k_tokens, mixed, pos, begin, later, later_plan, 1
    )
    proj_gate, proj_up, proj_down, proj_out = (whole.reshape(-1, whole.shape[2]) for whole in wholes)

    after_attn = input_f32 + contract(attn_tokens, proj_out, 0, 0)
    norm_ffn = rms_scale(after_attn)
    normed_f = (after_attn * norm_ffn * gain_ffn).astype(low)
    gate_act = matmul(normed_f, proj_gate)
    up_act = matmul(normed_f, proj_up)
    sigmoid_gate = jax.nn.sigmoid(gate_act)
    silu_gate = gate_act * sigmoid_gate
    hidden = (silu_gate * up_act).astype(low)
    result = (after_attn + matmul(hidden, proj_down)).astype(low)

    grad_down = contract(hidden, out_cot, 0, 0)
    grad_hidden = contract(out_cot, proj_down, 1, 1)
    grad_gate_low = (
        grad_hidden * up_act * sigmoid_gate * (1.0 + gate_act * (1.0 - sigmoid_gate))
    ).astype(low)
    grad_up_low = (grad_hidden * silu_gate).astype(low)
    grad_gate_w = contract(normed_f, grad_gate_low, 0, 0)
    grad_up_w = contract(normed_f, grad_up_low, 0, 0)
    grad_normed_f = contract(grad_gate_low, proj_gate, 1, 1) + contract(grad_up_low, proj_up, 1, 1)
    grad_gain_ffn = jnp.sum(grad_normed_f * after_attn * norm_ffn, axis=0)
    scaled_ffn = grad_normed_f * gain_ffn
    grad_after = (
        out_cot.astype(jnp.float32)
        + norm_ffn * scaled_ffn
        - after_attn * norm_ffn**3 * jnp.mean(scaled_ffn * after_attn, axis=-1, keepdims=True)
    )
    grad_attn_low = grad_after.astype(low)
    grad_out_w = contract(attn_tokens, grad_attn_low, 1, 0)
    grad_attended = contract(proj_out, grad_attn_low, 1, 1).astype(low)

    def terms(*grads):
        return [grad.astype(low).reshape(devices, -1, grad.shape[1]) for grad in grads]

    later_terms = terms(grad_gate_w, grad_up_w, grad_down, grad_out_w)
    early = devices <= 32
    (dq_rot, dk_rot, grad_mixed), later_sums = backward(
        grad_attended, *heads, attended, lse, pos, begin,
        later_terms if early else [], later_plan if early else [], 2,
    )
    grad_q = rotate(dq_rot.astype(jnp.float32), cosine, -sine_tab).astype(low)
    grad_k = rotate(dk_rot.astype(jnp.float32), cosine, -sine_tab).astype(low)
    grad_v = grad_mixed * jnp.asarray(0.5, low)
    grad_first = grad_v.T.astype(jnp.float32)
    grad_query_w = contract(normed_a, grad_q, 0, 1)
    grad_key_w = contract(normed_a, grad_k, 0, 1)
    grad_value_w = contract(normed_a, grad_v, 0, 1)
    grad_normed_a = (
        contract(grad_q, proj_query, 0, 1)
        + contract(grad_k, proj_key, 0, 1)
        + contract(grad_v, proj_value, 0, 1)
    )
    grad_gain_attn = jnp.sum(grad_normed_a * input_f32 * norm_attn, axis=0)
    scaled_attn = grad_normed_a * gain_attn
    grad_layer = (
        grad_after
        + norm_attn * scaled_attn
        - input_f32 * norm_attn**3 * jnp.mean(scaled_attn * input_f32, axis=-1, keepdims=True)
    )

    gain_terms = jnp.pad(jnp.stack([grad_gain_attn, grad_gain_ffn]), ((0, 6), (0, 0)))
    gain_terms = jnp.repeat(gain_terms.reshape(8, -1, 128).transpose(1, 0, 2), neighbours, axis=0)
    first_terms = [*terms(grad_query_w, grad_key_w, grad_value_w), gain_terms]
    if early:
        first_sums = reduce_all(first_terms, first_plan[:-1], 3)
    else:
        every = plan(
            [term.shape[2] for term in first_terms + later_terms],
            (0, None, "A"), (1, None, "B"), (2, None, "C"), (3, None, "C"),
            (4, None, "A"), (5, None, "A"), (6, None, "C"), (7, None, "C"),
        )
        all_sums = reduce_all(first_terms + later_terms, every, 3)
        first_sums, later_sums = all_sums[:4], all_sums[4:]
    *sums, sum_gains = publish([*first_sums[:3], *later_sums, first_sums[3]])
    sum_query, sum_key, sum_value, sum_gate, sum_up, sum_down, sum_out = sums
    sum_gains = lax.dynamic_slice_in_dim(sum_gains, turn, share, 1)
    return (
        result,
        grad_layer,
        grad_first,
        sum_gains[0],
        sum_query,
        sum_key,
        sum_value,
        sum_out,
        sum_gains[1],
        sum_gate,
        sum_up,
        sum_down,
    )


def solution(mesh):
    return jax.shard_map(
        per_device,
        mesh=mesh,
        in_specs=(
            P(("fsdp", "seq"), None),
            P(("fsdp", "seq"), None),
            P("fsdp"),
            P(("seq", "fsdp")),
            P(("seq", "fsdp"), None),
            P(("seq", "fsdp"), None),
            P(("seq", "fsdp"), None),
            P(("seq", "fsdp"), None),
            P(("seq", "fsdp")),
            P(("seq", "fsdp"), None),
            P(("seq", "fsdp"), None),
            P(("seq", "fsdp"), None),
            P(("fsdp", "seq"), None),
        ),
        out_specs=(
            P(("fsdp", "seq"), None),
            P(("fsdp", "seq"), None),
            P(("fsdp", "seq"), None),
            P(("seq", "fsdp")),
            P(("seq", "fsdp"), None),
            P(("seq", "fsdp"), None),
            P(("seq", "fsdp"), None),
            P(("seq", "fsdp"), None),
            P(("seq", "fsdp")),
            P(("seq", "fsdp"), None),
            P(("seq", "fsdp"), None),
            P(("seq", "fsdp"), None),
        ),
        check_vma=False,
    )
```

time: 528 us -> 441 us (0.84)
  Pallas kernels: 416 us -> 364 us
  local copies, waits for them, and re-layouts: 36.9 us -> 11.5 us
  matrix products: 52.4 us -> 46.1 us
    pallas_call x8 -> x5, Pallas kernels: 416 us -> 364 us  [the longest x1 147 us: backward(): pl.pallas_call(functools.partial(backward_kernel, tokens, pieces, n, len(...]
    dynamic_update_slice x4 -> x1, local copies, waits for them, and re-layouts: 11.3 us -> 0.21 us  [per_device(): lax.dynamic_update_slice(gains, jnp.stack([g_attn, g_ffn]), (0, turn))]
    unnamed x73 -> x34, local copies, waits for them, and re-layouts: 16.7 us -> 7.74 us
where the time goes in v3:
time: 441 us; the launch traced here: 434 us
  Pallas kernels  364 us (83%)
  matrix products  46.1 us (10%)
  local copies, waits for them, and re-layouts  11.5 us (3%)
  other arithmetic  11.2 us (3%)
    pallas_call x1, Pallas kernels, backward(): pl.pallas_call(functools.partial(backward_kernel, tokens, pieces, n, len(...  147 us
    pallas_call x1, Pallas kernels, forward(): pl.pallas_call(functools.partial(forward_kernel, tokens, pieces, n), out_...  130 us
    pallas_call x1, Pallas kernels, reduce_all(): pl.pallas_call(functools.partial(reduce_kernel, pieces, n), out_shape=sum...  42.1 us
    pallas_call x1, Pallas kernels, gather_all(): pl.pallas_call(functools.partial(gather_kernel, pieces, n), out_shape=gat...  41.9 us
    dot_general x18, matrix products, contract(): lax.dot_general(left, right, (((left_dim,), (right_dim,)), ((), ())), pre...  40.2 us

profile of v3, /device:TPU:0, one launch (start us, length us, event | category | flops | bytes accessed | tf_op | source)
XLA Modules:
  0.0 433.7 jit_solution(14020171367495939132)
XLA Ops:
  6.4 41.9 %shard_map.220 = (bf16[32,32,1024]{2,1,0:T(8,128)(2,1)}, bf16[32,32,1024]{2,1,0:T(8,128)(2,1)}, bf16[32,32,1024]{2,1,0:T(8,128)(2,1)}, bf16[32,16,128]{2,1,0:T(8,128)(2,1)}, s32[32,8,128]{2,1,0:T(8,128)}) custom-call(bf16[32,1024]{1,0:T(8,128)(2,1)} %refs_0_.1, bf16[32,1024]{1,0:T(8,128)(2,1)} %refs_1_.1, bf16[32,1024]{1,0:T(8,128)(2,1)} %refs_2_.1, ...), custom_call_target="tpu_custom_call" | custom-call | bytes 6553600 | tf_op jit(solution)/shard_map/pallas_call | solution.py:266
  50.9 3.4 fusion.3.refs_2_
  58.1 129.8 %shard_map.221 = (bf16[32,32,2816]{2,1,0:T(8,128)(2,1)}, bf16[32,32,2816]{2,1,0:T(8,128)(2,1)}, bf16[32,88,1024]{2,1,0:T(8,128)(2,1)}, bf16[32,32,1024]{2,1,0:T(...) custom-call(bf16[1024,256]{1,0:T(8,128)(2,1)} %bitcast.110, ...), custom_call_target="tpu_custom_call" | custom-call | flops 2863311360 | bytes 19398656 | tf_op jit(solution)/shard_map/pallas_call | solution.py:920
  187.9 2.7 multiply_reduce_fusion.2
  191.4 1.7 fusion.34
  193.4 1.7 fusion.33
  195.3 3.4 multiply_convert_fusion
  198.8 2.5 fusion.2
  201.2 1.7 fusion.35
  202.9 1.9 multiply_reduce_fusion
  205.1 1.2 copy-done.4
  206.4 1.5 convolution_convert_fusion.7.refs_0_
  207.9 2.1 convolution_convert_fusion.6
  210.0 4.1 convolution_convert_fusion
  214.2 4.3 convolution_convert_fusion.1
  218.5 4.2 convolution_convert_fusion.2
  222.7 147.4 %shard_map.222 = (bf16[1024,256]{1,0:T(8,128)(2,1)}, bf16[1024,256]{1,0:T(8,128)(2,1)}, bf16[1024,256]{1,0:T(8,128)(2,1)}, f32[32,2816]{1,0:T(8,128)}, f32[32,28...) custom-call(bf16[1024,256]{1,0:T(8,128)(2,1)} %convolution_convert_fusion.7.refs_0_, ...), custom_call_target="tpu_custom_call" | custom-call | flops 7158278144 | bytes 22544384 | tf_op jit(solution)/shard_map/pallas_call | solution.py:1163
  377.6 1.3 fusion.8
  379.7 1.3 copy.31
  381.0 2.2 convolution_convert_fusion.3
  383.2 2.2 convolution_convert_fusion.4
  385.4 2.2 convolution_convert_fusion.5
  387.6 42.1 %shard_map.223 = (f32[32,1024]{1,0:T(8,128)}, f32[32,1024]{1,0:T(8,128)}, f32[32,1024]{1,0:T(8,128)}, f32[8,128]{1,0:T(8,128)}) custom-call(bf16[32,32,1024]{2,1,0:T(8,128)(2,1)} %bitcast.93, bf16[32,32,1024]{2,1,0:T(8,128)(2,1)} %bitcast.92, bf16[32,32,1024]{2,1,0:T(8,128)(2,1)} %bitcast.91, f32[32,8,128]{2,1,0:T(8,128)} %bitcast.109), custom_call_target="tpu_custom_call" | custom-call | bytes 12845056 | tf_op jit(solution)/shard_map/pallas_call | solution.py:476
  429.7 2.5 shard_map.224
  (74 shorter events, 23.1 us)
Async XLA Ops:
  0.6 50.2 %copy-start = (bf16[256,1024]{1,0:T(8,128)(2,1)S(1)}, bf16[256,1024]{1,0:T(8,128)(2,1)}, u32[]{:S(2)}) copy-start(bf16[256,1024]{1,0:T(8,128)(2,1)} %param.13) | copy-start | bytes 1572868
  4.3 2.1 copy-start.9
  50.9 3.4 copy-start.5
  54.2 1.6 copy-start.2
  187.9 3.4 copy-start.11
  190.7 2.4 slice-start
  191.4 2.0 slice-start.1
  191.4 3.7 slice-start.2
  193.4 1.7 copy-start.8
  193.4 1.9 slice-start.3
  204.8 1.6 copy-start.4
  206.4 1.5 copy-start.1
  372.4 1.6 copy-start.3
  372.8 1.9 copy-start.6
  374.7 1.0 copy-start.7
  374.7 1.8 copy-start.10

commit v4 on v3

--- a/solution.py
+++ b/solution.py
@@ -104,11 +104,20 @@
     def slots(self, order):
         first, count, width = [], 0, 1
         for dim in order:
-            width *= self.size[dim]
+            n = self.size[dim]
             first.append(count)
-            if self.size[dim] > 1:
-                count += width * len(self.dirs(dim))
+            count += width * {1: 0, 2: 1}.get(n, n + 1)
+            width *= n
         return first, count
+
+    def slot(self, order, j, w, at):
+        first, _ = self.slots(order)
+        dim = order[j]
+        place = self.rank(order, at, j)
+        if self.size[dim] == 2:
+            return first[j] + place
+        width = math.prod(self.size[d] for d in order[:j])
+        return first[j] + place + width * (at[dim] + w)
 
     def branch(self, order, j, way, at):
         dim = order[j]
@@ -133,15 +142,19 @@
     def __init__(self, grid, pieces, sources, outs, sems):
         self.grid, self.pieces, self.sources, self.outs = grid, pieces, sources, outs
         self.recv, self.send, self.core_send, self.own_sem = sems
+        self.base, slots = [], 0
+        for piece in pieces:
+            self.base.append(slots)
+            slots += grid.slots(ORDERS[piece[3]])[1]
         self.places = grid.places(ORDERS["A"])
 
     @staticmethod
     def semaphores(grid, pieces, arrays):
-        slots = max(grid.slots(order)[1] for order in ORDERS.values())
+        slots = sum(grid.slots(ORDERS[piece[3]])[1] for piece in pieces)
         dma = pltpu.SemaphoreType.DMA
         return [
             dma((len(pieces), grid.total)),
-            dma((len(pieces), slots)),
+            dma((slots,)),
             dma((len(pieces), grid.plane)),
             dma((arrays,)),
         ]
@@ -156,7 +169,6 @@
     def sends(self, p, at, source, act):
         grid = self.grid
         order = ORDERS[self.pieces[p][3]]
-        first, _ = grid.slots(order)
         number = grid.linear(at, grid.core)
         target = self.view(self.outs[self.pieces[p][0]].at[number], p)
 
@@ -175,12 +187,12 @@
                 continue
             ways = grid.dirs(dim)
             for w, way in enumerate(ways):
-                slot = first[j] + grid.rank(order, at, j + 1) * len(ways) + w
+                slot = grid.slot(order, j, w, at)
                 device = grid.partner(dim) if way == 0 else grid.step(dim, way)
 
                 @pl.when(grid.branch(order, j, way, at))
                 def _(device=device, slot=slot):
-                    act(copy(self.send.at[p, slot], device))
+                    act(copy(self.send.at[self.base[p] + slot], device))
 
         act(copy(self.core_send.at[p, grid.rank(order, at, 3)], grid.step("core", 1)))
 
@@ -278,10 +290,8 @@
     def __init__(self, grid, pieces, parts, outs, scratch):
         n = len(pieces)
         self.grid, self.pieces, self.parts, self.outs = grid, pieces, parts, outs
-        self.pair, self.slot, self.held, self.total = (
-            scratch[i * n : (i + 1) * n] for i in range(4)
-        )
-        sems = scratch[4 * n :]
+        self.pair, self.slot, self.held = (scratch[i * n : (i + 1) * n] for i in range(3))
+        sems = scratch[3 * n :]
         self.core_send, self.core_recv, self.tree_send, self.tree_recv, self.own_sem = sems
         self.places = grid.places(ORDERS["A"])
 
@@ -297,7 +307,6 @@
             [pltpu.VMEM((grid.plane, *s), k) for s, k in zip(shape, kind)]
             + [pltpu.VMEM((c, *s), k) for c, s, k in zip(count, shape, kind)]
             + [pltpu.VMEM((2, *s), k) for s, k in zip(shape, kind)]
-            + [pltpu.VMEM(s, jnp.float32) for s in shape]
             + [dma((n, grid.plane)), dma((n, grid.plane)), dma((n, grid.plane)), dma((n, most)), dma((n, 2))]
         )
 
@@ -340,7 +349,6 @@
     def to_parent(self, p, at, act):
         grid = self.grid
         order = ORDERS[self.pieces[p][3]]
-        first, _ = grid.slots(order)
         rank = self.rank(p, at)
         for j, dim in enumerate(order):
             if grid.size[dim] == 1:
@@ -351,7 +359,7 @@
                 same = at[later] == grid.me[later]
                 ok = same if ok is None else ok & same
             for w, way in enumerate(ways):
-                slot = first[j] + grid.rank(order, at, j + 1) * len(ways) + w
+                slot = grid.slot(order, j, w, at)
                 if way == 0:
                     here, device = at[dim] != grid.me[dim], grid.partner(dim)
                 elif way == 1:
@@ -373,36 +381,81 @@
                         )
                     )
 
+    def add(self, p, at, number, children, out):
+        held, pair, slots = self.held[p], self.pair[p], self.slot[p]
+        slot, rank = lax.rem(number, 2), self.rank(p, at)
+        rows, columns = held.shape[1:]
+        width = max(
+            w for w in range(128, columns + 1, 128) if columns % w == 0 and (w == 128 or rows * w <= 49152)
+        )
+        array, lower, _, _ = self.pieces[p]
+
+        def one(step, carry):
+            first = pl.multiple_of(step * width, 128)
+            here = pl.ds(first, width)
+            total = held[slot, :, here].astype(jnp.float32) + pair[rank, :, here].astype(jnp.float32)
+            for child in children:
+                total = total + slots[child, :, here].astype(jnp.float32)
+            if out:
+                self.outs[array][:, pl.ds(lower + first, width)] = total
+            else:
+                pair[rank, :, here] = total.astype(pair.dtype)
+            return carry
+
+        lax.fori_loop(0, columns // width, one, 0)
+
     def combine(self, p, at, number):
         grid = self.grid
         order = ORDERS[self.pieces[p][3]]
-        first, _ = grid.slots(order)
         rank = self.rank(p, at)
-        total, slots = self.total[p], self.slot[p]
         self.to_sibling(p, at).wait_recv()
         self.fetch(p, at, number).wait()
-        total[...] = self.held[p][lax.rem(number, 2)].astype(jnp.float32) + self.pair[p][
-            rank
-        ].astype(jnp.float32)
-        for j in reversed(range(3)):
+
+        def arrived(slot):
+            there = self.slot[p].at[slot]
+            pltpu.make_async_remote_copy(
+                src_ref=there,
+                dst_ref=there,
+                send_sem=self.tree_send.at[p, rank],
+                recv_sem=self.tree_recv.at[p, slot],
+                device_id=grid.step("core", 1),
+                device_id_type=MESH,
+            ).wait_recv()
+            return slot
+
+        def level(j, children):
+            if j < 0:
+                self.add(p, at, number, children, True)
+                return
             dim = order[j]
-            if grid.size[dim] == 1:
-                continue
-            ways = grid.dirs(dim)
-            for w, way in enumerate(ways):
-                slot = first[j] + grid.rank(order, at, j + 1) * len(ways) + w
-
-                @pl.when(grid.branch(order, j, way, at))
-                def _(slot=slot):
-                    pltpu.make_async_remote_copy(
-                        src_ref=slots.at[slot],
-                        dst_ref=slots.at[slot],
-                        send_sem=self.tree_send.at[p, rank],
-                        recv_sem=self.tree_recv.at[p, slot],
-                        device_id=grid.step("core", 1),
-                        device_id_type=MESH,
-                    ).wait_recv()
-                    total[...] += slots[slot].astype(jnp.float32)
+            n, me = grid.size[dim], grid.me[dim]
+            if n == 1:
+                level(j - 1, children)
+                return
+            same = at[dim] == me
+            if n == 2:
+                pl.when(jnp.logical_not(same))(lambda: self.add(p, at, number, children, False))
+                pl.when(same)(lambda: level(j - 1, children + [arrived(grid.slot(order, j, 0, at))]))
+                return
+            up, down = me < n - 1, me > 0
+            more = at[dim] > me
+            behind = ((at[dim] < me) & up) | (more & down)
+
+            @pl.when(jnp.logical_not(same) & behind)
+            def _():
+                w = jnp.where(more, 1, 0)
+                self.add(p, at, number, children + [arrived(grid.slot(order, j, w, at))], False)
+
+            pl.when(jnp.logical_not(same | behind))(lambda: self.add(p, at, number, children, False))
+
+            def sides(*ways):
+                level(j - 1, children + [arrived(grid.slot(order, j, w, at)) for w in ways])
+
+            pl.when(same & up & down)(lambda: sides(0, 1))
+            pl.when(same & up & jnp.logical_not(down))(lambda: sides(0))
+            pl.when(same & jnp.logical_not(up) & down)(lambda: sides(1))
+
+        level(2, [])
 
     def start(self):
         places = self.places
@@ -420,7 +473,6 @@
 
         def work(p, at):
             self.combine(p, at, number)
-            self.pair[p][self.rank(p, at)] = self.total[p][...].astype(self.pair[p].dtype)
             self.to_parent(p, at, lambda copy: copy.start())
 
         self.each(number, work)
@@ -428,8 +480,6 @@
     def finish(self):
         def root(p, at):
             self.combine(p, at, 0)
-            array, lower, count, _ = self.pieces[p]
-            self.outs[array][:, lower : lower + count] = self.total[p][...]
 
         self.each(0, root)
 
@@ -462,7 +512,7 @@
     tree.finish()
 
 
-VMEM_LIMIT = 60 << 20
+VMEM_LIMIT = 62 << 20
 
 
 def summed_shapes(arrays):
@@ -639,8 +689,11 @@
 
 QUERIES = 512
 KEYS = 1024
-BESIDE_EXCHANGE = 2
+BESIDE_PROJECT = 2
+BESIDE_EXCHANGE = 3
 BESIDE_TILES = 2
+LATER_AT = 14
+COLUMNS = 256
 ANY = pl.BlockSpec(memory_space=pl.ANY)
 WHOLE = pl.BlockSpec(memory_space=pltpu.VMEM)
 
@@ -693,7 +746,7 @@
 
     def body(tile, causal, current):
         number, top, total, summed = current
-        number = step(number)
+        number = now_and_then(tile, BESIDE_TILES, step, number)
         scores = shown(first_dims(k_ref[:, key_lanes(tile)], queries), tile, causal, pos, begin)
         new_top = jnp.maximum(top, jnp.max(scores, axis=0, keepdims=True))
         weights = jnp.exp(scores - new_top)
@@ -738,30 +791,30 @@
             dma((2, own.total // own.members * (own.members - 1))),
         ]
 
-    def keys(self, act):
+    def keys(self, i, act):
         own = self.own
+        source, target = self.pairs[i]
 
         def to_head(delta, carry):
             head = lax.rem(own.head + delta, HEADS)
-            for i, (source, target) in enumerate(self.pairs):
-                piece = source.at[head_rows(head), :]
-                there = target.at[:, lanes(own.block, own.tokens)]
-
-                @pl.when(head == own.head)
-                def _(piece=piece, there=there, i=i):
-                    copy = pltpu.make_async_copy(piece, there, self.local.at[i])
-                    copy.start() if act == "start" else copy.wait()
-
-                @pl.when(head != own.head)
-                def _(piece=piece, there=there, i=i):
-                    copy = remote(
-                        piece,
-                        there,
-                        self.send.at[i, head],
-                        self.recv.at[i, own.block],
-                        own.of_head(head, own.member),
-                    )
-                    copy.start() if act == "start" else copy.wait_send()
+            piece = source.at[head_rows(head), :]
+            there = target.at[:, lanes(own.block, own.tokens)]
+
+            @pl.when(head == own.head)
+            def _(piece=piece, there=there, i=i):
+                copy = pltpu.make_async_copy(piece, there, self.local.at[i])
+                copy.start() if act == "start" else copy.wait()
+
+            @pl.when(head != own.head)
+            def _(piece=piece, there=there, i=i):
+                copy = remote(
+                    piece,
+                    there,
+                    self.send.at[i, head],
+                    self.recv.at[i, own.block],
+                    own.of_head(head, own.member),
+                )
+                copy.start() if act == "start" else copy.wait_send()
 
             return carry
 
@@ -780,9 +833,9 @@
             )
             copy.start() if act == "start" else copy.wait_send()
 
-    def hand_own(self, act):
-        for i, (source, _) in enumerate(self.pairs):
-            self.hand(i, self.shares - 1, self.own.block, source.at[head_rows(self.own.head), :], act)
+    def hand_own(self, i, act):
+        source = self.pairs[i][0].at[head_rows(self.own.head), :]
+        self.hand(i, self.shares - 1, self.own.block, source, act)
 
     def block_of(self, step):
         order = lax.rem(self.mine + step, self.shares)
@@ -796,10 +849,12 @@
         ).wait_recv()
         return there
 
-    def start(self):
-        self.keys("start")
+    def start_keys(self, i):
+        self.keys(i, "start")
+        self.hand_own(i, "start")
+
+    def start_queries(self):
         spread_units(self.own, self.q_ref, self.q_out, self.q_send, self.q_recv, self.q_local, "start")
-        self.hand_own("start")
 
     def relay(self, step):
         block = self.block_of(step)
@@ -819,9 +874,10 @@
 
         lax.fori_loop(0, own.total, rest, 0)
         await_units(own, self.q_out, self.q_send, self.q_recv)
-        self.keys("wait")
         spread_units(own, self.q_ref, self.q_out, self.q_send, self.q_recv, self.q_local, "wait")
-        self.hand_own("wait")
+        for i in range(2):
+            self.keys(i, "wait")
+            self.hand_own(i, "wait")
 
         def settle(step, carry):
             block = self.block_of(step)
@@ -832,48 +888,133 @@
         lax.fori_loop(1, self.shares, settle, 0)
 
 
-def forward_kernel(tokens, pieces, n, *refs):
-    tokens_of = refs[:3]
-    pos_ref, begin_ref = refs[3:5]
-    sources = refs[5 : 5 + n]
-    wholes = refs[5 + n : 5 + 2 * n]
-    keep = refs[5 + 2 * n : 8 + 2 * n]
-    out_ref, lse_ref, back_ref = refs[8 + 2 * n : 11 + 2 * n]
-    *heads, low_ref = refs[11 + 2 * n : 15 + 2 * n]
-    sems = refs[15 + 2 * n :]
+def now_and_then(index, every, act, number):
+    return lax.cond(lax.rem(index, every) == 0, act, lambda x: x, number)
+
+
+class Front:
+    def __init__(self, grid, own, plan, sources, inputs, landed, tokens_of, outs, sems):
+        self.grid, self.own = grid, own
+        self.xn_ref, self.vf_ref, self.cos_ref, self.sin_ref, self.pos_ref = inputs
+        self.landed, self.tokens_of = landed, tokens_of
+        self.keep, (self.gain_ref, self.normed_ref, self.begin_ref) = outs[:3], outs[3:]
+        self.keep_sem = sems[-1]
+        self.tree = Gather(grid, plan, sources, landed, sems[:-1])
+
+    def keeping(self, i):
+        return pltpu.make_async_copy(self.landed[i], self.keep[i], self.keep_sem.at[i])
+
+    def gather(self, between):
+        def one(number, carry):
+            self.tree.relay(number)
+            between(number)
+            return carry
+
+        lax.fori_loop(1, self.tree.places, one, 0)
+        self.tree.finish()
+        for i in range(3):
+            self.keeping(i).start()
+
+    def prepare(self):
+        gains, places = self.landed[3:]
+        near = self.grid.total // 8
+        rows = []
+        for lane_block in range(8):
+            rows.append(
+                sum(
+                    gains[lane_block * near + i, :8, :].astype(jnp.float32) for i in range(near)
+                )
+            )
+        gain = jnp.concatenate(rows, axis=1)
+        self.gain_ref[...] = gain
+        self.normed_ref[...] = (self.xn_ref[...] * gain[:1]).astype(self.normed_ref.dtype)
+        own = self.own
+
+        def unit(place, carry):
+            number = place * own.members + own.member
+            block, half = lax.div(number, own.halves), lax.rem(number, own.halves)
+            device = lax.rem(block, own.seq) * own.fsdp + lax.div(block, own.seq)
+            here = lanes(place, UNIT)
+            self.begin_ref[:, here] = self.pos_ref[:, here] - places[device, pl.ds(half, 1), :]
+            return carry
+
+        lax.fori_loop(0, own.units, unit, 0)
+
+    def project(self, i, part):
+        columns = pl.ds(pl.multiple_of(part * COLUMNS, COLUMNS), COLUMNS)
+        weights = self.landed[i][:, :, columns].reshape(-1, COLUMNS)
+        found = plain(self.normed_ref[...], weights).T
+        target = self.tokens_of[i]
+        if i == 2:
+            mixed = 0.5 * found + 0.5 * self.vf_ref[columns, :].astype(jnp.float32)
+            target[columns, :] = mixed.astype(target.dtype)
+            return
+        cosine, sine_tab = self.cos_ref[...], self.sin_ref[...]
+        half, turned = HEAD_DIM // 2, []
+        for first in range(0, COLUMNS, HEAD_DIM):
+            front, back = found[first : first + half], found[first + half : first + HEAD_DIM]
+            turned += [front * cosine - back * sine_tab, back * cosine + front * sine_tab]
+        turned = jnp.concatenate(turned, axis=0).astype(target.dtype)
+        target[columns, :] = turned * jnp.asarray(HEAD_DIM**-0.5, target.dtype) if i == 0 else turned
+
+
+def forward_kernel(tokens, plans, counts, *refs):
+    refs = list(refs)
+
+    def take(count):
+        taken = refs[:count]
+        del refs[:count]
+        return taken
+
+    n_first, n = counts
+    inputs, sources_first, sources = take(5), take(n_first), take(n)
+    wholes, first_outs, keep = take(n), take(6), take(3)
+    out_ref, lse_ref, back_ref = take(3)
+    heads, (low_ref,) = take(3), take(1)
+    landed, tokens_of = take(n_first), take(3)
+    tree_sems, exchange_sems, (out_send, out_recv, out_local, keep_sem) = take(4), take(7), take(4)
+    first_sems = take(5)
     grid, own = Grid(), Owners(tokens)
     grid.locate()
     own.locate()
-    tree = Gather(grid, pieces, sources, wholes, sems[:4])
-    exchange = ToHeads(own, tokens_of, heads, sems[4:11])
-    out_send, out_recv, out_local, keep_sem = sems[11:]
+    front = Front(
+        grid, own, plans[0], sources_first, inputs, landed, tokens_of, first_outs, first_sems
+    )
+    tree = Gather(grid, plans[1], sources, wholes, tree_sems)
+    exchange = ToHeads(own, tokens_of, heads, exchange_sems)
     tiles = Tiles(own)
+    pos_ref, begin_ref = inputs[4], first_outs[5]
 
     own.barrier()
-    exchange.start()
-    tree.start()
-
-    def paced(every, first):
-        def advance(count):
-            number = lax.div(count, every)
-
-            @pl.when((lax.rem(count, every) == 0) & (number < tree.places))
-            def _():
-                tree.relay(number)
-
-            return count + 1
-
-        return advance, first * every
-
-    beside, count = paced(BESIDE_EXCHANGE, 1)
-
-    def relay(step, count):
+    front.tree.start()
+    front.gather(lambda number: pl.when(number == LATER_AT)(tree.start))
+    front.prepare()
+
+    def advance(number):
+        @pl.when(number < tree.places)
+        def _():
+            tree.relay(number)
+
+        return number + 1
+
+    number = jnp.int32(1)
+    for i in (1, 2, 0):
+
+        def part(index, number, i=i):
+            front.project(i, index)
+            return now_and_then(index, BESIDE_PROJECT, advance, number)
+
+        number = lax.fori_loop(0, HEADS * HEAD_DIM // COLUMNS, part, number)
+        if i:
+            exchange.start_keys(i - 1)
+        else:
+            exchange.start_queries()
+
+    def relay(step, number):
         exchange.relay(step)
-        return beside(count)
-
-    count = lax.fori_loop(1, exchange.shares, relay, jnp.int32(count))
-    number = lax.div(count + BESIDE_EXCHANGE - 1, BESIDE_EXCHANGE)
-    advance, number = paced(BESIDE_TILES, number)
+        return now_and_then(step, BESIDE_EXCHANGE, advance, number)
+
+    number = lax.fori_loop(1, exchange.shares, relay, number)
     exchange.finish()
     keeping = [pltpu.make_async_copy(heads[i], keep[i], keep_sem.at[i]) for i in range(3)]
     for copy in keeping:
@@ -894,7 +1035,6 @@
         return number
 
     number = lax.fori_loop(0, tiles.groups, one_group, number)
-    number = lax.div(number + BESIDE_TILES - 1, BESIDE_TILES)
 
     def last(number, carry):
         tree.relay(number)
@@ -906,41 +1046,54 @@
     tree.finish()
     for copy in keeping:
         copy.wait()
-
-
-def forward(q, k, v, pos, begin, arrays, pieces, ident):
-    tokens, kind = q.shape[1], q.dtype
+    for i in range(3):
+        front.keeping(i).wait()
+
+
+def forward(inputs, first, first_plan, later, later_plan, ident):
+    tokens, features, kind = inputs[1].shape[1], inputs[1].shape[0], inputs[1].dtype
     grid, own = Grid(), Owners(tokens)
-    n = len(arrays)
+    n, n_first = len(later), len(first)
     count = own.units * UNIT
     dma = pltpu.SemaphoreType.DMA
     heads = [(HEAD_DIM, count)] + [(HEAD_DIM, own.total * tokens)] * 2
     pairs = count * own.total * tokens // 3
-    moved = sum(a.size * a.dtype.itemsize for a in arrays) * grid.total
+    moved = sum(a.size * a.dtype.itemsize for a in (*first, *later)) * grid.total
+    landed = gathered_shapes(grid, first)
     outs = pl.pallas_call(
-        functools.partial(forward_kernel, tokens, pieces, n),
-        out_shape=gathered_shapes(grid, arrays)
+        functools.partial(forward_kernel, tokens, (first_plan, later_plan), (n_first, n)),
+        out_shape=gathered_shapes(grid, later)
+        + landed[:3]
+        + [
+            jax.ShapeDtypeStruct((8, features), jnp.float32),
+            jax.ShapeDtypeStruct((tokens, features), kind),
+            jax.ShapeDtypeStruct((1, count), jnp.int32),
+        ]
         + [jax.ShapeDtypeStruct(s, kind) for s in heads]
         + [
             jax.ShapeDtypeStruct((HEAD_DIM, count), jnp.float32),
             jax.ShapeDtypeStruct((1, count), jnp.float32),
-            jax.ShapeDtypeStruct(q.shape, kind),
+            jax.ShapeDtypeStruct((features, tokens), kind),
         ],
-        in_specs=[ANY] * 3 + [WHOLE] * 2 + [ANY] * n,
-        out_specs=[ANY] * (n + 3) + [WHOLE] * 2 + [ANY],
+        in_specs=[WHOLE] * 5 + [ANY] * (n_first + n),
+        out_specs=[ANY] * (n + 3) + [WHOLE] * 3 + [ANY] * 3 + [WHOLE] * 2 + [ANY],
         scratch_shapes=[pltpu.VMEM(s, kind) for s in heads]
         + [pltpu.VMEM((HEAD_DIM, count), kind)]
-        + Gather.semaphores(grid, pieces, n)
+        + [pltpu.VMEM(a.shape, a.dtype) for a in landed]
+        + [pltpu.VMEM((features, tokens), kind)] * 3
+        + Gather.semaphores(grid, later_plan, n)
         + ToHeads.semaphores(own)
-        + [dma((own.units,)), dma((HEADS, own.halves)), dma((own.halves,)), dma((3,))],
+        + [dma((own.units,)), dma((HEADS, own.halves)), dma((own.halves,)), dma((3,))]
+        + Gather.semaphores(grid, first_plan, n_first)
+        + [dma((3,))],
         compiler_params=pltpu.CompilerParams(
             collective_id=ident, has_side_effects=True, vmem_limit_bytes=VMEM_LIMIT
         ),
         cost_estimate=pl.CostEstimate(
             flops=pairs * 4 * HEAD_DIM, bytes_accessed=moved, transcendentals=pairs
         ),
-    )(q, k, v, pos, begin, *arrays)
-    return outs[:n], outs[n : n + 3], outs[n + 3 :]
+    )(*inputs, *first, *later)
+    return outs[:n], outs[n : n + 3], outs[n + 3 : n + 6], outs[n + 6 : n + 9], outs[n + 9 :]
 
 
 class GradsBack:
@@ -948,9 +1101,7 @@
         self.own, self.sums, self.outs = own, sums, outs
         self.give_from, self.given, self.held = give_from, given, held
         self.give_send, self.give_recv, self.send, self.recv, self.local = sems
-        self.shares = own.total // own.members
         self.others = own.members - 1
-        self.mine = lax.div(own.f, own.members) * own.seq + own.s
 
     @staticmethod
     def scratch(own, kind):
@@ -968,44 +1119,35 @@
             dma((2,)),
         ]
 
-    def block_of(self, order, member):
-        f = member + self.own.members * lax.div(order, self.own.seq)
-        return f * self.own.seq + lax.rem(order, self.own.seq)
-
-    def given_at(self, i, slot):
-        there = self.given.at[i, slot]
-        remote(
-            there, there, self.give_send.at[i, 0], self.give_recv.at[i, slot], self.own.of_block(0)
-        ).wait_recv()
-        return self.given[i, slot].astype(jnp.float32)
-
-    def give(self, act):
+    def split(self, block):
+        f = lax.div(block, self.own.seq)
+        order = lax.div(f, self.own.members) * self.own.seq + lax.rem(block, self.own.seq)
+        return lax.rem(f, self.own.members), order
+
+    def give(self, block, act):
         own = self.own
-
-        def one(step, carry):
-            order = lax.rem(self.mine + step, self.shares)
-            for away in range(1, own.members):
-                member = lax.rem(own.member + away, own.members)
-                columns = lanes(self.block_of(order, member), own.tokens)
-                out, back = order * self.others + away - 1, order * self.others + self.others - away
-                for i in range(2):
-                    if act == "start":
-                        self.give_from[i, out] = self.sums[i][:, columns].astype(self.held.dtype)
-                    copy = remote(
-                        self.give_from.at[i, out],
-                        self.given.at[i, back],
-                        self.give_send.at[i, out],
-                        self.give_recv.at[i, back],
-                        own.of_head(own.head, member),
-                    )
-                    copy.start() if act == "start" else copy.wait_send()
-            return carry
-
-        lax.fori_loop(1, self.shares + 1, one, 0)
-
-    def back(self, order, i, act):
+        member, order = self.split(block)
+        away = lax.rem(member - own.member + own.members, own.members)
+
+        @pl.when(away > 0)
+        def _():
+            columns = lanes(block, own.tokens)
+            out = order * self.others + away - 1
+            back = order * self.others + self.others - away
+            for i in range(2):
+                if act == "start":
+                    self.give_from[i, out] = self.sums[i][:, columns].astype(self.held.dtype)
+                copy = remote(
+                    self.give_from.at[i, out],
+                    self.given.at[i, back],
+                    self.give_send.at[i, out],
+                    self.give_recv.at[i, back],
+                    own.of_head(own.head, member),
+                )
+                copy.start() if act == "start" else copy.wait_send()
+
+    def back(self, block, order, i, act):
         own = self.own
-        block = self.block_of(order, own.member)
         there = self.outs[i].at[head_rows(own.head), :]
 
         @pl.when(block == own.block)
@@ -1024,15 +1166,34 @@
             )
             copy.start() if act == "start" else copy.wait_send()
 
-    def add(self, step):
-        order = lax.rem(self.mine + step, self.shares)
-        columns = lanes(self.block_of(order, self.own.member), self.own.tokens)
-        for i in range(2):
-            total = self.sums[i][:, columns]
-            for j in range(self.others):
-                total = total + self.given_at(i, order * self.others + j)
-            self.held[i, order] = total.astype(self.held.dtype)
-            self.back(order, i, "start")
+    def add(self, block):
+        member, order = self.split(block)
+
+        @pl.when(member == self.own.member)
+        def _():
+            columns = lanes(block, self.own.tokens)
+            for i in range(2):
+                total = self.sums[i][:, columns]
+                for j in range(self.others):
+                    slot = order * self.others + j
+                    there = self.given.at[i, slot]
+                    remote(
+                        there,
+                        there,
+                        self.give_send.at[i, 0],
+                        self.give_recv.at[i, slot],
+                        self.own.of_block(0),
+                    ).wait_recv()
+                    total = total + self.given[i, slot].astype(jnp.float32)
+                self.held[i, order] = total.astype(self.held.dtype)
+                self.back(block, order, i, "start")
+
+    def over(self, first, count, act):
+        def one(step, carry):
+            act(first + step)
+            return carry
+
+        lax.fori_loop(0, count, one, 0)
 
     def finish(self):
         def arrive(head, carry):
@@ -1047,34 +1208,118 @@
             return carry
 
         lax.fori_loop(0, HEADS, arrive, 0)
-        self.give("wait")
-
-        def settle(order, carry):
-            for i in range(2):
-                self.back(order, i, "wait")
-            return carry
-
-        lax.fori_loop(0, self.shares, settle, 0)
-
-
-def backward_kernel(tokens, pieces, n, n_tree, *refs):
-    g_ref, q_ref, k_ref, v_ref, out_ref, lse_ref, pos_ref, begin_ref = refs[:8]
-    parts = refs[8 : 8 + n]
-    dq_out, dk_out, dv_out = refs[8 + n : 11 + n]
-    sums = refs[11 + n : 11 + 2 * n]
-    rest = refs[11 + 2 * n :]
-    tree_scratch, rest = rest[:n_tree], rest[n_tree:]
-    grads_ref, dq_ref, dk_sum, dv_sum = rest[:4]
-    back_scratch, sems = rest[4:12], rest[12:]
+
+        def settle(block):
+            self.give(block, "wait")
+            member, order = self.split(block)
+
+            @pl.when(member == self.own.member)
+            def _():
+                for i in range(2):
+                    self.back(block, order, i, "wait")
+
+        self.over(0, self.own.total, settle)
+
+
+class Tail:
+    def __init__(self, grid, inputs, landed, outs, scratch):
+        self.grid = grid
+        self.normed_ref, self.xn_ref, self.cos_ref, self.sin_ref, self.ffn_ref = inputs[:5]
+        self.weights = inputs[5:]
+        self.landed = landed
+        self.dh_ref, self.dv_ref = outs
+        *self.terms, self.gain_terms, self.weight, self.turned, self.sem = scratch
+
+    @staticmethod
+    def scratch(grid, features, tokens, kind):
+        rows = features // grid.total
+        return (
+            [pltpu.VMEM((grid.total, rows, features), kind)] * 3
+            + [
+                pltpu.VMEM((grid.total, 8, 128), jnp.float32),
+                pltpu.VMEM((2, grid.total, rows, features), kind),
+                pltpu.VMEM((tokens, features), kind),
+                pltpu.SemaphoreType.DMA((2,)),
+            ]
+        )
+
+    def load(self, step, i):
+        return pltpu.make_async_copy(self.weights[i], self.weight.at[step % 2], self.sem.at[step % 2])
+
+    def unrotate(self, i, part):
+        columns = pl.ds(pl.multiple_of(part * COLUMNS, COLUMNS), COLUMNS)
+        found = self.landed[i][columns, :].astype(jnp.float32)
+        if i == 2:
+            found = 0.5 * found
+        else:
+            cosine, sine_tab = self.cos_ref[...], self.sin_ref[...]
+            half, turned = HEAD_DIM // 2, []
+            for first in range(0, COLUMNS, HEAD_DIM):
+                front, back = found[first : first + half], found[first + half : first + HEAD_DIM]
+                turned += [front * cosine + back * sine_tab, back * cosine - front * sine_tab]
+            found = jnp.concatenate(turned, axis=0)
+        turned = found.T.astype(self.turned.dtype)
+        self.turned[:, columns] = turned
+        if i == 2:
+            self.dv_ref[:, columns] = turned
+
+    def project(self, i, step, part, first):
+        columns = pl.ds(pl.multiple_of(part * COLUMNS, COLUMNS), COLUMNS)
+        per = self.grid.total * COLUMNS // self.normed_ref.shape[1]
+        blocks = pl.ds(part * per, per)
+        terms = first_dims(self.normed_ref[:, columns], self.turned[...])
+        self.terms[i][blocks] = terms.reshape(per, -1, terms.shape[1]).astype(self.terms[i].dtype)
+        weights = self.weight[step % 2, blocks].reshape(COLUMNS, -1)
+        term = last_dims(self.turned[...], weights)
+        self.dh_ref[:, columns] = term if first else self.dh_ref[:, columns] + term
+
+    def gains(self):
+        attn = jnp.sum(self.dh_ref[...] * self.xn_ref[...], axis=0, keepdims=True)
+        row = lax.broadcasted_iota(jnp.int32, (8, 1), 0)
+        both = jnp.where(row == 0, attn, jnp.where(row == 1, self.ffn_ref[...], 0.0))
+        near = self.grid.total // 8
+        for block in range(8):
+            for i in range(near):
+                self.gain_terms[block * near + i] = both[:, block * 128 : (block + 1) * 128]
+
+
+REDUCE_FIRST = 14
+REDUCE_TILES = 3
+REDUCE_TAIL = 1
+
+
+def backward_kernel(tokens, plans, counts, *refs):
+    refs = list(refs)
+
+    def take(count):
+        taken = refs[:count]
+        del refs[:count]
+        return taken
+
+    n, n_tree, n_first = counts
+    g_ref, q_ref, k_ref, v_ref, out_ref, lse_ref, pos_ref, begin_ref = take(8)
+    tail_inputs = take(8) if n else None
+    parts = take(n)
+    outs = take(2 if n else 3)
+    sums = take(n)
+    first_sums = take(4 if n else 0)
+    grads_ref, dq_ref, dk_sum, dv_sum = take(4)
+    back_scratch = take(8)
+    g_send, g_recv, g_local, dq_send, dq_recv, dq_local = take(6)
     own = Owners(tokens)
     own.locate()
     tree = None
+    dq_out, dk_out, dv_out = landed = take(3) if n else outs
     if n:
         grid = Grid()
         grid.locate()
-        tree = Reduce(grid, pieces, parts, sums, tree_scratch)
+        tree = Reduce(grid, plans[0], parts, sums, take(n_tree))
+        first_scratch = take(n_first)
+        tail = Tail(grid, tail_inputs, landed, outs, refs)
+        tree_first = Reduce(
+            grid, plans[1], (*tail.terms, tail.gain_terms), first_sums, first_scratch
+        )
     grads_back = GradsBack(own, (dk_sum, dv_sum), (dk_out, dv_out), *back_scratch[:3], back_scratch[3:])
-    g_send, g_recv, g_local, dq_send, dq_recv, dq_local = sems
     tiles = Tiles(own)
 
     own.barrier()
@@ -1093,12 +1338,14 @@
 
         return number + 1
 
-    number = advance(jnp.int32(0))
+    number = lax.fori_loop(0, REDUCE_FIRST, lambda step, number: advance(number), jnp.int32(0))
     await_units(own, grads_ref, g_send, g_recv)
     spread_units(own, g_ref, grads_ref, g_send, g_recv, g_local, "wait")
     units = QUERIES // UNIT
-
-    def one_group(group, number):
+    blocks = tiles.span // tokens
+
+    def one_group(step, number):
+        group = tiles.groups - 1 - step
         here = group_lanes(group)
         queries, grads = q_ref[:, here], grads_ref[:, here]
         pos, begin, lse = pos_ref[:, here], begin_ref[:, here], lse_ref[:, here]
@@ -1106,7 +1353,7 @@
 
         def body(tile, causal, current):
             number, dq = current
-            number = advance(number)
+            number = now_and_then(tile, REDUCE_TILES, advance, number)
             there = key_lanes(tile)
             keys = k_ref[:, there]
             scores = shown(first_dims(keys, queries), tile, causal, pos, begin)
@@ -1123,62 +1370,108 @@
         collect_units(
             own, dq_ref, dq_out, dq_send, dq_recv, dq_local, "start", group * units, units
         )
+        grads_back.over(group * blocks, blocks, lambda block: grads_back.give(block, "start"))
+
+        @pl.when(step > 0)
+        def _():
+            grads_back.over((group + 1) * blocks, blocks, grads_back.add)
+
         return number
 
     number = lax.fori_loop(0, tiles.groups, one_group, number)
-    grads_back.give("start")
-
-    def add(step, number):
-        grads_back.add(step)
-        return number
-
-    number = lax.fori_loop(1, grads_back.shares + 1, add, number)
-    if tree:
-
-        def last(number, carry):
-            tree.climb(number)
-            return carry
-
-        lax.fori_loop(number, tree.places - 1, last, 0)
+    grads_back.over(0, blocks, grads_back.add)
     await_heads(own, dq_out, dq_send, dq_recv)
     collect_units(own, dq_ref, dq_out, dq_send, dq_recv, dq_local, "wait", 0, own.units)
     grads_back.finish()
-    if tree:
-        tree.finish()
-
-
-def backward(grads, q, k, v, out, lse, pos, begin, arrays, pieces, ident):
-    tokens, kind = grads.shape[1], grads.dtype
+    if not tree:
+        return
+
+    parts_of = HEADS * HEAD_DIM // COLUMNS
+    order = (0, 1, 2)
+    tail.load(0, order[0]).start()
+    for step, i in enumerate(order):
+        tail.load(step, i).wait()
+        if step < 2:
+            tail.load(step + 1, order[step + 1]).start()
+
+        def turn(part, number, i=i):
+            tail.unrotate(i, part)
+            return now_and_then(part, REDUCE_TAIL, advance, number)
+
+        def project(part, number, i=i, step=step):
+            tail.project(i, step, part, step == 0)
+            return now_and_then(part, REDUCE_TAIL, advance, number)
+
+        number = lax.fori_loop(0, parts_of, turn, number)
+        number = lax.fori_loop(0, parts_of, project, number)
+    tail.gains()
+    tree_first.start()
+
+    def climb(step, number):
+        tree_first.climb(step)
+        return advance(number)
+
+    number = lax.fori_loop(0, tree_first.places - 1, climb, number)
+
+    def last(number, carry):
+        tree.climb(number)
+        return carry
+
+    lax.fori_loop(number, tree.places - 1, last, 0)
+    tree_first.finish()
+    tree.finish()
+
+
+def backward(grads, q, k, v, out, lse, pos, begin, ident, tail=(), arrays=(), plans=((), ())):
+    tokens, features, kind = grads.shape[1], grads.shape[0], grads.dtype
     grid, own = Grid(), Owners(tokens)
     n = len(arrays)
     count = own.units * UNIT
     dma = pltpu.SemaphoreType.DMA
-    tree_scratch = Reduce.scratch(grid, pieces, arrays) if n else []
     pairs = count * own.total * tokens // 3
     moved = sum(a.size * a.dtype.itemsize for a in arrays) + 6 * k.size
-    unit_sems = [
-        [dma((HEADS, own.halves)), dma((own.units,)), dma((own.halves,))],
-        [dma((own.units,)), dma((HEADS, own.halves)), dma((own.halves,))],
-    ]
-    outs = pl.pallas_call(
-        functools.partial(backward_kernel, tokens, pieces, n, len(tree_scratch)),
-        out_shape=[jax.ShapeDtypeStruct(grads.shape, kind)] * 3 + summed_shapes(arrays),
-        in_specs=[ANY] + [WHOLE] * 7 + [ANY] * n,
-        out_specs=[ANY] * 3 + [WHOLE] * n,
-        scratch_shapes=tree_scratch
-        + [pltpu.VMEM((HEAD_DIM, count), kind)] * 2
+    back = jax.ShapeDtypeStruct(grads.shape, kind)
+    scratch = (
+        [pltpu.VMEM((HEAD_DIM, count), kind)] * 2
         + [pltpu.VMEM(k.shape, jnp.float32)] * 2
         + GradsBack.scratch(own, kind)
-        + unit_sems[0]
-        + unit_sems[1],
+        + [dma((HEADS, own.halves)), dma((own.units,)), dma((own.halves,))]
+        + [dma((own.units,)), dma((HEADS, own.halves)), dma((own.halves,))]
+    )
+    tree_scratch = first_scratch = []
+    if n:
+        tail_scratch = Tail.scratch(grid, features, tokens, kind)
+        first = [jax.ShapeDtypeStruct((grid.total, features // grid.total, features), kind)] * 3
+        first.append(jax.ShapeDtypeStruct((grid.total, 8, 128), jnp.float32))
+        tree_scratch = Reduce.scratch(grid, plans[0], arrays)
+        first_scratch = Reduce.scratch(grid, plans[1], first)
+        scratch += [pltpu.VMEM(grads.shape, kind)] * 3 + tree_scratch + first_scratch + tail_scratch
+        out_shape = [
+            jax.ShapeDtypeStruct((tokens, features), jnp.float32),
+            jax.ShapeDtypeStruct((tokens, features), kind),
+        ]
+        out_shape += summed_shapes(arrays) + summed_shapes(first)
+        out_specs = [WHOLE] * len(out_shape)
+        in_specs = [ANY] + [WHOLE] * 12 + [ANY] * (3 + n)
+    else:
+        out_shape, out_specs = [back] * 3, [ANY] * 3
+        in_specs = [ANY] + [WHOLE] * 7
+    outs = pl.pallas_call(
+        functools.partial(
+            backward_kernel, tokens, plans, (n, len(tree_scratch), len(first_scratch))
+        ),
+        out_shape=out_shape,
+        in_specs=in_specs,
+        out_specs=out_specs,
+        scratch_shapes=scratch,
         compiler_params=pltpu.CompilerParams(
             collective_id=ident, has_side_effects=True, vmem_limit_bytes=VMEM_LIMIT
         ),
         cost_estimate=pl.CostEstimate(
             flops=pairs * 10 * HEAD_DIM, bytes_accessed=moved, transcendentals=pairs
         ),
-    )(grads, q, k, v, out, lse, pos, begin, *arrays)
-    return outs[:3], outs[3:]
+    )(grads, q, k, v, out, lse, pos, begin, *tail, *arrays)
+    return (outs[:2], outs[2 : 2 + n], outs[2 + n :]) if n else outs
 
 
 def publish_kernel(*refs):
@@ -1200,8 +1493,10 @@
 def plan(columns, *pieces):
     found, used = [], [0] * len(columns)
     for array, part, order in pieces:
-        count = columns[array] if part is None else part
-        count = min(count, columns[array] - used[array])
+        left = columns[array] - used[array]
+        if not left:
+            continue
+        count = left if part is None else min(part, left)
         found.append((array, used[array], count, order))
         used[array] += count
     return found
@@ -1265,7 +1560,7 @@
     places = jnp.zeros((8, 128), jnp.int32)
     places = lax.dynamic_update_slice(places, own_offsets.reshape(-1, 128), (0, 0))
     first = (w_query, w_key, w_value, gains, places)
-    half = w_key.shape[1] // 2
+    half = w_key.shape[1] // 2 if devices <= 32 else None
     first_plan = plan(
         [shard.shape[1] for shard in first],
         (0, None, "A"), (1, half, "A"), (1, half, "B"), (2, None, "C"), (3, None, "C"), (4, None, "C"),
@@ -1275,38 +1570,24 @@
         [shard.shape[1] for shard in later],
         (0, None, "A"), (1, None, "A"), (2, None, "C"), (3, half, "A"), (3, half, "B"),
     )
-    *wholes, whole_gains, whole_places = gather_all(first, first_plan, 0)
-    proj_query, proj_key, proj_value = (whole.reshape(-1, whole.shape[2]) for whole in wholes)
-    whole_gains = whole_gains.reshape(-1, neighbours, 16, 128).astype(jnp.float32).sum(1)
-    gain_attn, gain_ffn = whole_gains[:, 0].reshape(-1), whole_gains[:, 1].reshape(-1)
-    all_offsets = (
-        whole_places[:, : tokens // 128].reshape(seq, fsdp, tokens).transpose(1, 0, 2).reshape(-1)
-    )
 
     own = Owners(tokens)
     member = lax.rem(lax.axis_index("fsdp"), own.members)
-    unit_begins = (jnp.arange(devices * tokens, dtype=jnp.int32) - all_offsets).reshape(
-        own.units, own.members, UNIT
-    )
-    begin = lax.dynamic_index_in_dim(unit_begins, member, 1, keepdims=False).reshape(1, -1)
     pos = (
         (jnp.arange(own.units, dtype=jnp.int32)[:, None] * own.members + member) * UNIT
         + jnp.arange(UNIT, dtype=jnp.int32)[None]
     ).reshape(1, -1)
-
     cosine, sine_tab = angle_tables(own_offsets)
     input_f32 = layer_input.astype(jnp.float32)
     norm_attn = rms_scale(input_f32)
-    normed_a = (input_f32 * norm_attn * gain_attn).astype(low)
-    scale = jnp.asarray(HEAD_DIM**-0.5, low)
-    q_tokens = rotate(lax.optimization_barrier(contract(proj_query, normed_a, 0, 1)), cosine, sine_tab).astype(low) * scale
-    k_tokens = rotate(lax.optimization_barrier(contract(proj_key, normed_a, 0, 1)), cosine, sine_tab).astype(low)
-    mixed = (
-        0.5 * contract(proj_value, normed_a, 0, 1) + 0.5 * v_first.astype(jnp.float32).T
-    ).astype(low)
-    wholes, heads, (attended, lse, attn_tokens) = forward(
-        q_tokens, k_tokens, mixed, pos, begin, later, later_plan, 1
+    normed_input = input_f32 * norm_attn
+    wholes, first_wholes, front, heads, (attended, lse, attn_tokens) = forward(
+        (normed_input, v_first.T, cosine[0], sine_tab[0], pos),
+        first, first_plan, later, later_plan, 0,
     )
+    gain_rows, normed_a, begin = front
+    gain_attn, gain_ffn = gain_rows[0], gain_rows[1]
+    proj_query, proj_key, proj_value = (whole.reshape(-1, whole.shape[2]) for whole in first_wholes)
     proj_gate, proj_up, proj_down, proj_out = (whole.reshape(-1, whole.shape[2]) for whole in wholes)
 
     after_attn = input_f32 + contract(attn_tokens, proj_out, 0, 0)
@@ -1343,24 +1624,42 @@
         return [grad.astype(low).reshape(devices, -1, grad.shape[1]) for grad in grads]
 
     later_terms = terms(grad_gate_w, grad_up_w, grad_down, grad_out_w)
-    early = devices <= 32
-    (dq_rot, dk_rot, grad_mixed), later_sums = backward(
-        grad_attended, *heads, attended, lse, pos, begin,
-        later_terms if early else [], later_plan if early else [], 2,
-    )
-    grad_q = rotate(dq_rot.astype(jnp.float32), cosine, -sine_tab).astype(low)
-    grad_k = rotate(dk_rot.astype(jnp.float32), cosine, -sine_tab).astype(low)
-    grad_v = grad_mixed * jnp.asarray(0.5, low)
-    grad_first = grad_v.T.astype(jnp.float32)
-    grad_query_w = contract(normed_a, grad_q, 0, 1)
-    grad_key_w = contract(normed_a, grad_k, 0, 1)
-    grad_value_w = contract(normed_a, grad_v, 0, 1)
-    grad_normed_a = (
-        contract(grad_q, proj_query, 0, 1)
-        + contract(grad_k, proj_key, 0, 1)
-        + contract(grad_v, proj_value, 0, 1)
-    )
-    grad_gain_attn = jnp.sum(grad_normed_a * input_f32 * norm_attn, axis=0)
+    attention = (grad_attended, *heads, attended, lse, pos, begin)
+    if devices <= 32:
+        (grad_normed_a, grad_v), later_sums, first_sums = backward(
+            *attention, 1,
+            (
+                normed_a, normed_input, cosine[0], sine_tab[0], grad_gain_ffn[None],
+                *first_wholes,
+            ),
+            later_terms, (later_plan, first_plan[:-1]),
+        )
+        grad_first = grad_v.astype(jnp.float32)
+    else:
+        dq_rot, dk_rot, grad_mixed = backward(*attention, 1)
+        grad_q = rotate(dq_rot.astype(jnp.float32), cosine, -sine_tab).astype(low)
+        grad_k = rotate(dk_rot.astype(jnp.float32), cosine, -sine_tab).astype(low)
+        grad_v = grad_mixed * jnp.asarray(0.5, low)
+        grad_first = grad_v.T.astype(jnp.float32)
+        grad_query_w = contract(normed_a, grad_q, 0, 1)
+        grad_key_w = contract(normed_a, grad_k, 0, 1)
+        grad_value_w = contract(normed_a, grad_v, 0, 1)
+        grad_normed_a = (
+            contract(grad_q, proj_query, 0, 1)
+            + contract(grad_k, proj_key, 0, 1)
+            + contract(grad_v, proj_value, 0, 1)
+        )
+        grad_gain_attn = jnp.sum(grad_normed_a * normed_input, axis=0)
+        gain_terms = jnp.pad(jnp.stack([grad_gain_attn, grad_gain_ffn]), ((0, 6), (0, 0)))
+        gain_terms = jnp.repeat(gain_terms.reshape(8, -1, 128).transpose(1, 0, 2), neighbours, axis=0)
+        first_terms = [*terms(grad_query_w, grad_key_w, grad_value_w), gain_terms]
+        every = plan(
+            [term.shape[2] for term in first_terms + later_terms],
+            (0, None, "A"), (1, None, "B"), (2, None, "C"), (3, None, "C"),
+            (4, None, "A"), (5, None, "A"), (6, None, "C"), (7, None, "C"),
+        )
+        all_sums = reduce_all(first_terms + later_terms, every, 2)
+        first_sums, later_sums = all_sums[:4], all_sums[4:]
     scaled_attn = grad_normed_a * gain_attn
     grad_layer = (
         grad_after
@@ -1368,19 +1667,6 @@
         - input_f32 * norm_attn**3 * jnp.mean(scaled_attn * input_f32, axis=-1, keepdims=True)
     )
 
-    gain_terms = jnp.pad(jnp.stack([grad_gain_attn, grad_gain_ffn]), ((0, 6), (0, 0)))
-    gain_terms = jnp.repeat(gain_terms.reshape(8, -1, 128).transpose(1, 0, 2), neighbours, axis=0)
-    first_terms = [*terms(grad_query_w, grad_key_w, grad_value_w), gain_terms]
-    if early:
-        first_sums = reduce_all(first_terms, first_plan[:-1], 3)
-    else:
-        every = plan(
-            [term.shape[2] for term in first_terms + later_terms],
-            (0, None, "A"), (1, None, "B"), (2, None, "C"), (3, None, "C"),
-            (4, None, "A"), (5, None, "A"), (6, None, "C"), (7, None, "C"),
-        )
-        all_sums = reduce_all(first_terms + later_terms, every, 3)
-        first_sums, later_sums = all_sums[:4], all_sums[4:]
     *sums, sum_gains = publish([*first_sums[:3], *later_sums, first_sums[3]])
     sum_query, sum_key, sum_value, sum_gate, sum_up, sum_down, sum_out = sums
     sum_gains = lax.dynamic_slice_in_dim(sum_gains, turn, share, 1)

time: 441 us -> 415 us (0.941)
  matrix products: 46.1 us -> 32.5 us
  Pallas kernels: 364 us -> 356 us
    dot_general x18 -> x9, matrix products: 40.2 us -> 26.6 us  [contract(): lax.dot_general(left, right, (((left_dim,), (right_dim,)), ((), ())), pre...]
    pallas_call x4 -> x2, Pallas kernels: 361 us -> 354 us  [the longest x1 188 us: backward(): pl.pallas_call(functools.partial(backward_kernel, tokens, plans, (n, len(...]
where the time goes in v4:
time: 415 us; the launch traced here: 409 us
  Pallas kernels  356 us (86%)
  matrix products  32.5 us (8%)
  other arithmetic  11.9 us (3%)
  local copies, waits for them, and re-layouts  7.29 us (2%)
    pallas_call x1, Pallas kernels, backward(): pl.pallas_call(functools.partial(backward_kernel, tokens, plans, (n, len(...  188 us
    pallas_call x1, Pallas kernels, forward(): pl.pallas_call(functools.partial(forward_kernel, tokens, (first_plan, lat...  166 us
    dot_general x9, matrix products, contract(): lax.dot_general(left, right, (((left_dim,), (right_dim,)), ((), ())), pre...  26.6 us

profile of v4, /device:TPU:0, one launch (start us, length us, event | category | flops | bytes accessed | tf_op | source)
XLA Modules:
  0.0 409.3 jit_solution(9371777468309555826)
XLA Ops:
  1.4 1.2 fusion.2
  4.9 0.8 multiply_sine_fusion
  5.7 2.0 copy.25
  7.7 2.1 convert_multiply_fusion.2.refs_0_.refs_9_
  9.9 166.3 %shard_map.220 = (bf16[32,32,2816]{2,1,0:T(8,128)(2,1)}, bf16[32,32,2816]{2,1,0:T(8,128)(2,1)}, bf16[32,88,1024]{2,1,0:T(8,128)(2,1)}, bf16[32,32,1024]{2,1,0:T(...) custom-call(f32[256,1024]{1,0:T(8,128)} %convert_multiply_fusion.2.r, ...), custom_call_target="tpu_custom_call" | custom-call | flops 2863311360 | bytes 25952256 | tf_op jit(solution)/shard_map/pallas_call | solution.py:1063
  176.2 0.8 fusion.8
  177.1 2.7 multiply_reduce_fusion.2
  180.5 1.7 fusion.10
  182.6 1.7 fusion.9
  184.5 3.4 multiply_convert_fusion
  187.9 2.5 fusion.1
  190.4 1.7 fusion.11
  192.1 2.5 multiply_reduce_fusion
  195.0 1.3 copy-done.2
  196.2 1.5 convolution_convert_fusion.4.refs_0_
  197.8 2.1 convolution_convert_fusion.3
  199.9 4.2 %convolution_convert_fusion = bf16[2816,1024]{1,0:T(8,128)(2,1)} fusion(bf16[256,2816]{1,0:T(8,128)(2,1)S(1)} %get-tuple-element.84, bf16[256,1024]{1,0:T(8,128)(2,1)S(1)} %copy-done.3), kind=kOutput, calls=%fused_computation | convolution fusion | flops 1479278592 | bytes 7733248 | tf_op jit(solution)/shard_map/dot_general | solution.py:1528
  204.1 4.3 %convolution_convert_fusion.1 = bf16[1024,2816]{1,0:T(8,128)(2,1)} fusion(bf16[256,1024]{1,0:T(8,128)(2,1)S(1)} %multiply_convert_fusion.3, bf16[256,2816]{1,0:T(8,128)(2,1)S(1)} %get-tuple-element.82), kind=kOutput, calls=%fused_computation.1 | convolution fusion | flops 1479278592 | bytes 7733248 | tf_op jit(solution)/shard_map/dot_general | solution.py:1528
  208.3 4.2 %convolution_convert_fusion.2 = bf16[1024,2816]{1,0:T(8,128)(2,1)} fusion(bf16[256,1024]{1,0:T(8,128)(2,1)S(1)} %multiply_convert_fusion.3, bf16[256,2816]{1,0:T(8,128)(2,1)S(1)} %get-tuple-element.83), kind=kOutput, calls=%fused_computation.2 | convolution fusion | flops 1479278592 | bytes 7733248 | tf_op jit(solution)/shard_map/dot_general | solution.py:1528
  212.5 187.6 %shard_map.221 = (f32[256,1024]{1,0:T(8,128)}, bf16[256,1024]{1,0:T(8,128)(2,1)}, f32[32,2816]{1,0:T(8,128)}, f32[32,2816]{1,0:T(8,128)}, f32[88,1024]{1,0:T(8,1...) custom-call(bf16[1024,256]{1,0:T(8,128)(2,1)} %convolution_convert_f, ...), custom_call_target="tpu_custom_call" | custom-call | flops 7158278144 | bytes 22544384 | tf_op jit(solution)/shard_map/pallas_call | solution.py:1459
  400.1 1.5 fusion.5
  401.6 2.5 fusion.4
  404.1 1.1 convert_element_type.59
  405.2 2.5 shard_map.222
  (39 shorter events, 5.8 us)
Async XLA Ops:
  4.2 5.7 %copy-start.5 = (bf16[16,128]{1,0:T(8,128)(2,1)}, bf16[16,128]{1,0:T(8,128)(2,1)S(1)}, u32[]{:S(2)}) copy-start(bf16[16,128]{1,0:T(8,128)(2,1)S(1)} %dynamic_update_slice.6.refs_8_) | copy-start | bytes 12292
  9.9 167.2 %copy-start = (bf16[256,1024]{1,0:T(8,128)(2,1)S(1)}, bf16[256,1024]{1,0:T(8,128)(2,1)}, u32[]{:S(2)}) copy-start(bf16[256,1024]{1,0:T(8,128)(2,1)} %param.13) | copy-start | bytes 1572868
  177.1 3.4 copy-start.6
  179.8 2.4 slice-start
  180.5 2.0 slice-start.1
  180.5 3.8 slice-start.2
  182.6 1.7 copy-start.3
  182.6 1.9 slice-start.3
  194.6 1.6 copy-start.2
  196.2 1.6 copy-start.1
  400.1 4.0 copy-start.4

commit v5 on v4

--- a/solution.py
+++ b/solution.py
@@ -73,6 +73,22 @@
         pl.semaphore_wait(sem, count)
 
     def digits(self, order, number):
+        at, rest = {}, number
+        for dim in order:
+            n, me = self.size[dim], self.me[dim]
+            digit = lax.rem(rest, n)
+            rest = lax.div(rest, n)
+            if n == 2:
+                at[dim] = lax.rem(me + digit, 2)
+                continue
+            both = jnp.minimum(me, n - 1 - me)
+            away = lax.div(digit + 1, 2)
+            side = jnp.where(lax.rem(digit, 2) == 1, me - away, me + away)
+            far = jnp.where(me > both, me - (digit - both), me + (digit - both))
+            at[dim] = jnp.where(digit <= 2 * both, side, far)
+        return at
+
+    def spaced_digits(self, order, number):
         at, ok = {}, None
         rest = number
         for dim in order:
@@ -91,8 +107,8 @@
                 ok = inside if ok is None else ok & inside
         return at, ok
 
-    def places(self, order):
-        return math.prod(2 if self.size[d] == 2 else 2 * self.size[d] - 1 for d in order)
+    def spaced_places(self):
+        return math.prod(2 if n == 2 else 2 * n - 1 for n in self.size.values())
 
     def rank(self, order, at, upto):
         value, width = 0, 1
@@ -146,7 +162,7 @@
         for piece in pieces:
             self.base.append(slots)
             slots += grid.slots(ORDERS[piece[3]])[1]
-        self.places = grid.places(ORDERS["A"])
+        self.places = grid.plane
 
     @staticmethod
     def semaphores(grid, pieces, arrays):
@@ -208,16 +224,10 @@
         ).wait_recv()
 
     def each(self, number, act):
-        for p in range(len(self.pieces)):
-            at, ok = self.grid.digits(ORDERS[self.pieces[p][3]], number)
-
-            def run(p=p, at=at):
-                act(p, at)
-
-            if ok is None:
-                run()
-            else:
-                pl.when(ok)(run)
+        used = sorted({piece[3] for piece in self.pieces})
+        at = {order: self.grid.digits(ORDERS[order], number) for order in used}
+        for p, piece in enumerate(self.pieces):
+            act(p, at[piece[3]])
 
     def start(self):
         for i in range(len(self.sources)):
@@ -293,7 +303,7 @@
         self.pair, self.slot, self.held = (scratch[i * n : (i + 1) * n] for i in range(3))
         sems = scratch[3 * n :]
         self.core_send, self.core_recv, self.tree_send, self.tree_recv, self.own_sem = sems
-        self.places = grid.places(ORDERS["A"])
+        self.places = grid.spaced_places()
 
     @staticmethod
     def scratch(grid, pieces, arrays):
@@ -311,8 +321,10 @@
         )
 
     def each(self, number, act):
-        for p in range(len(self.pieces)):
-            at, ok = self.grid.digits(ORDERS[self.pieces[p][3]], number)
+        used = {piece[3] for piece in self.pieces}
+        places = {order: self.grid.spaced_digits(ORDERS[order], number) for order in sorted(used)}
+        for p, piece in enumerate(self.pieces):
+            at, ok = places[piece[3]]
 
             def run(p=p, at=at):
                 act(p, at)
@@ -689,10 +701,10 @@
 
 QUERIES = 512
 KEYS = 1024
-BESIDE_PROJECT = 2
-BESIDE_EXCHANGE = 3
-BESIDE_TILES = 2
-LATER_AT = 14
+BESIDE_PROJECT = 4
+BESIDE_EXCHANGE = 5
+BESIDE_TILES = 5
+LATER_AT = 4
 COLUMNS = 256
 ANY = pl.BlockSpec(memory_space=pl.ANY)
 WHOLE = pl.BlockSpec(memory_space=pltpu.VMEM)
@@ -892,12 +904,16 @@
     return lax.cond(lax.rem(index, every) == 0, act, lambda x: x, number)
 
 
+def rms_scale(tensor):
+    return lax.rsqrt(jnp.mean(tensor * tensor, axis=-1, keepdims=True) + EPSILON)
+
+
 class Front:
     def __init__(self, grid, own, plan, sources, inputs, landed, tokens_of, outs, sems):
         self.grid, self.own = grid, own
-        self.xn_ref, self.vf_ref, self.cos_ref, self.sin_ref, self.pos_ref = inputs
+        self.x_ref, self.vf_ref, self.cos_ref, self.sin_ref, self.pos_ref = inputs
         self.landed, self.tokens_of = landed, tokens_of
-        self.keep, (self.gain_ref, self.normed_ref, self.begin_ref) = outs[:3], outs[3:]
+        self.keep, (self.gain_ref, self.normed_ref, self.begin_ref, self.xn_ref) = outs[:3], outs[3:]
         self.keep_sem = sems[-1]
         self.tree = Gather(grid, plan, sources, landed, sems[:-1])
 
@@ -914,6 +930,10 @@
         self.tree.finish()
         for i in range(3):
             self.keeping(i).start()
+
+    def norm(self):
+        x = self.x_ref[...].astype(jnp.float32)
+        self.xn_ref[...] = x * rms_scale(x)
 
     def prepare(self):
         gains, places = self.landed[3:]
@@ -943,12 +963,13 @@
     def project(self, i, part):
         columns = pl.ds(pl.multiple_of(part * COLUMNS, COLUMNS), COLUMNS)
         weights = self.landed[i][:, :, columns].reshape(-1, COLUMNS)
-        found = plain(self.normed_ref[...], weights).T
+        found = plain(self.normed_ref[...], weights)
         target = self.tokens_of[i]
         if i == 2:
-            mixed = 0.5 * found + 0.5 * self.vf_ref[columns, :].astype(jnp.float32)
-            target[columns, :] = mixed.astype(target.dtype)
+            mixed = 0.5 * found + 0.5 * self.vf_ref[:, columns].astype(jnp.float32)
+            target[columns, :] = mixed.T.astype(target.dtype)
             return
+        found = found.T
         cosine, sine_tab = self.cos_ref[...], self.sin_ref[...]
         half, turned = HEAD_DIM // 2, []
         for first in range(0, COLUMNS, HEAD_DIM):
@@ -968,7 +989,7 @@
 
     n_first, n = counts
     inputs, sources_first, sources = take(5), take(n_first), take(n)
-    wholes, first_outs, keep = take(n), take(6), take(3)
+    wholes, first_outs, keep = take(n), take(7), take(3)
     out_ref, lse_ref, back_ref = take(3)
     heads, (low_ref,) = take(3), take(1)
     landed, tokens_of = take(n_first), take(3)
@@ -987,6 +1008,7 @@
 
     own.barrier()
     front.tree.start()
+    front.norm()
     front.gather(lambda number: pl.when(number == LATER_AT)(tree.start))
     front.prepare()
 
@@ -1051,7 +1073,7 @@
 
 
 def forward(inputs, first, first_plan, later, later_plan, ident):
-    tokens, features, kind = inputs[1].shape[1], inputs[1].shape[0], inputs[1].dtype
+    (tokens, features), kind = inputs[1].shape, inputs[1].dtype
     grid, own = Grid(), Owners(tokens)
     n, n_first = len(later), len(first)
     count = own.units * UNIT
@@ -1068,6 +1090,7 @@
             jax.ShapeDtypeStruct((8, features), jnp.float32),
             jax.ShapeDtypeStruct((tokens, features), kind),
             jax.ShapeDtypeStruct((1, count), jnp.int32),
+            jax.ShapeDtypeStruct((tokens, features), jnp.float32),
         ]
         + [jax.ShapeDtypeStruct(s, kind) for s in heads]
         + [
@@ -1076,7 +1099,7 @@
             jax.ShapeDtypeStruct((features, tokens), kind),
         ],
         in_specs=[WHOLE] * 5 + [ANY] * (n_first + n),
-        out_specs=[ANY] * (n + 3) + [WHOLE] * 3 + [ANY] * 3 + [WHOLE] * 2 + [ANY],
+        out_specs=[ANY] * (n + 3) + [WHOLE] * 4 + [ANY] * 3 + [WHOLE] * 2 + [ANY],
         scratch_shapes=[pltpu.VMEM(s, kind) for s in heads]
         + [pltpu.VMEM((HEAD_DIM, count), kind)]
         + [pltpu.VMEM(a.shape, a.dtype) for a in landed]
@@ -1093,7 +1116,7 @@
             flops=pairs * 4 * HEAD_DIM, bytes_accessed=moved, transcendentals=pairs
         ),
     )(*inputs, *first, *later)
-    return outs[:n], outs[n : n + 3], outs[n + 3 : n + 6], outs[n + 6 : n + 9], outs[n + 9 :]
+    return outs[:n], outs[n : n + 3], outs[n + 3 : n + 7], outs[n + 7 : n + 10], outs[n + 10 :]
 
 
 class GradsBack:
@@ -1296,7 +1319,7 @@
         del refs[:count]
         return taken
 
-    n, n_tree, n_first = counts
+    n, n_tree, first_counts = counts
     g_ref, q_ref, k_ref, v_ref, out_ref, lse_ref, pos_ref, begin_ref = take(8)
     tail_inputs = take(8) if n else None
     parts = take(n)
@@ -1314,11 +1337,13 @@
         grid = Grid()
         grid.locate()
         tree = Reduce(grid, plans[0], parts, sums, take(n_tree))
-        first_scratch = take(n_first)
+        first_scratch = [take(count) for count in first_counts]
         tail = Tail(grid, tail_inputs, landed, outs, refs)
-        tree_first = Reduce(
-            grid, plans[1], (*tail.terms, tail.gain_terms), first_sums, first_scratch
-        )
+        parts_first = (*tail.terms, tail.gain_terms)
+        trees = [
+            Reduce(grid, plan, parts_first, first_sums, scratch)
+            for plan, scratch in zip(plans[1], first_scratch)
+        ]
     grads_back = GradsBack(own, (dk_sum, dv_sum), (dk_out, dv_out), *back_scratch[:3], back_scratch[3:])
     tiles = Tiles(own)
 
@@ -1405,20 +1430,20 @@
         number = lax.fori_loop(0, parts_of, turn, number)
         number = lax.fori_loop(0, parts_of, project, number)
     tail.gains()
-    tree_first.start()
+    trees[0].start()
 
     def climb(step, number):
-        tree_first.climb(step)
+        trees[0].climb(step)
         return advance(number)
 
-    number = lax.fori_loop(0, tree_first.places - 1, climb, number)
+    number = lax.fori_loop(0, trees[0].places - 1, climb, number)
 
     def last(number, carry):
         tree.climb(number)
         return carry
 
     lax.fori_loop(number, tree.places - 1, last, 0)
-    tree_first.finish()
+    trees[0].finish()
     tree.finish()
 
 
@@ -1444,8 +1469,9 @@
         first = [jax.ShapeDtypeStruct((grid.total, features // grid.total, features), kind)] * 3
         first.append(jax.ShapeDtypeStruct((grid.total, 8, 128), jnp.float32))
         tree_scratch = Reduce.scratch(grid, plans[0], arrays)
-        first_scratch = Reduce.scratch(grid, plans[1], first)
-        scratch += [pltpu.VMEM(grads.shape, kind)] * 3 + tree_scratch + first_scratch + tail_scratch
+        first_scratch = [Reduce.scratch(grid, plan, first) for plan in plans[1]]
+        scratch += [pltpu.VMEM(grads.shape, kind)] * 3 + tree_scratch + sum(first_scratch, [])
+        scratch += tail_scratch
         out_shape = [
             jax.ShapeDtypeStruct((tokens, features), jnp.float32),
             jax.ShapeDtypeStruct((tokens, features), kind),
@@ -1458,7 +1484,7 @@
         in_specs = [ANY] + [WHOLE] * 7
     outs = pl.pallas_call(
         functools.partial(
-            backward_kernel, tokens, plans, (n, len(tree_scratch), len(first_scratch))
+            backward_kernel, tokens, plans, (n, len(tree_scratch), [len(one) for one in first_scratch])
         ),
         out_shape=out_shape,
         in_specs=in_specs,
@@ -1474,20 +1500,30 @@
     return (outs[:2], outs[2 : 2 + n], outs[2 + n :]) if n else outs
 
 
-def publish_kernel(*refs):
-    half = len(refs) // 2
-    for source, target in zip(refs[:half], refs[half:]):
+def publish_kernel(x_ref, gain_ref, dh_ref, dy_ref, dv_ref, *refs):
+    grad_ref, first_ref = refs[len(refs) // 2 - 1 : len(refs) // 2 + 1]
+    sources, targets = refs[: len(refs) // 2 - 1], refs[len(refs) // 2 + 1 :]
+    for source, target in zip(sources, targets):
         target[...] = source[...]
-
-
-def publish(arrays):
+    x = x_ref[...].astype(jnp.float32)
+    norm = rms_scale(x)
+    scaled = dh_ref[...] * gain_ref[:1]
+    normed = x * norm
+    grad_ref[...] = dy_ref[...] + norm * (
+        scaled - normed * jnp.mean(scaled * normed, axis=-1, keepdims=True)
+    )
+    first_ref[...] = dv_ref[...].astype(jnp.float32)
+
+
+def publish(x, gains, grad_normed, grad_after, grad_v, arrays):
+    wide = jax.ShapeDtypeStruct(x.shape, jnp.float32)
     return pl.pallas_call(
         publish_kernel,
-        out_shape=[jax.ShapeDtypeStruct(a.shape, a.dtype) for a in arrays],
-        in_specs=[WHOLE] * len(arrays),
-        out_specs=[WHOLE] * len(arrays),
+        out_shape=[wide, wide] + [jax.ShapeDtypeStruct(a.shape, a.dtype) for a in arrays],
+        in_specs=[WHOLE] * (5 + len(arrays)),
+        out_specs=[WHOLE] * (2 + len(arrays)),
         compiler_params=pltpu.CompilerParams(vmem_limit_bytes=VMEM_LIMIT),
-    )(*arrays)
+    )(x, gains, grad_normed, grad_after, grad_v, *arrays)
 
 
 def plan(columns, *pieces):
@@ -1500,10 +1536,6 @@
         found.append((array, used[array], count, order))
         used[array] += count
     return found
-
-
-def rms_scale(tensor):
-    return lax.rsqrt(jnp.mean(tensor * tensor, axis=-1, keepdims=True) + EPSILON)
 
 
 def angle_tables(offsets):
@@ -1579,14 +1611,12 @@
     ).reshape(1, -1)
     cosine, sine_tab = angle_tables(own_offsets)
     input_f32 = layer_input.astype(jnp.float32)
-    norm_attn = rms_scale(input_f32)
-    normed_input = input_f32 * norm_attn
     wholes, first_wholes, front, heads, (attended, lse, attn_tokens) = forward(
-        (normed_input, v_first.T, cosine[0], sine_tab[0], pos),
+        (layer_input, v_first, cosine[0], sine_tab[0], pos),
         first, first_plan, later, later_plan, 0,
     )
-    gain_rows, normed_a, begin = front
-    gain_attn, gain_ffn = gain_rows[0], gain_rows[1]
+    gain_rows, normed_a, begin, normed_input = front
+    gain_ffn = gain_rows[1]
     proj_query, proj_key, proj_value = (whole.reshape(-1, whole.shape[2]) for whole in first_wholes)
     proj_gate, proj_up, proj_down, proj_out = (whole.reshape(-1, whole.shape[2]) for whole in wholes)
 
@@ -1600,14 +1630,11 @@
     hidden = (silu_gate * up_act).astype(low)
     result = (after_attn + matmul(hidden, proj_down)).astype(low)
 
-    grad_down = contract(hidden, out_cot, 0, 0)
     grad_hidden = contract(out_cot, proj_down, 1, 1)
     grad_gate_low = (
         grad_hidden * up_act * sigmoid_gate * (1.0 + gate_act * (1.0 - sigmoid_gate))
     ).astype(low)
     grad_up_low = (grad_hidden * silu_gate).astype(low)
-    grad_gate_w = contract(normed_f, grad_gate_low, 0, 0)
-    grad_up_w = contract(normed_f, grad_up_low, 0, 0)
     grad_normed_f = contract(grad_gate_low, proj_gate, 1, 1) + contract(grad_up_low, proj_up, 1, 1)
     grad_gain_ffn = jnp.sum(grad_normed_f * after_attn * norm_ffn, axis=0)
     scaled_ffn = grad_normed_f * gain_ffn
@@ -1617,13 +1644,15 @@
         - after_attn * norm_ffn**3 * jnp.mean(scaled_ffn * after_attn, axis=-1, keepdims=True)
     )
     grad_attn_low = grad_after.astype(low)
-    grad_out_w = contract(attn_tokens, grad_attn_low, 1, 0)
     grad_attended = contract(proj_out, grad_attn_low, 1, 1).astype(low)
 
     def terms(*grads):
         return [grad.astype(low).reshape(devices, -1, grad.shape[1]) for grad in grads]
 
-    later_terms = terms(grad_gate_w, grad_up_w, grad_down, grad_out_w)
+    later_terms = terms(
+        contract(normed_f, grad_gate_low, 0, 0), contract(normed_f, grad_up_low, 0, 0),
+        contract(hidden, out_cot, 0, 0), contract(attn_tokens, grad_attn_low, 1, 0),
+    )
     attention = (grad_attended, *heads, attended, lse, pos, begin)
     if devices <= 32:
         (grad_normed_a, grad_v), later_sums, first_sums = backward(
@@ -1632,15 +1661,13 @@
                 normed_a, normed_input, cosine[0], sine_tab[0], grad_gain_ffn[None],
                 *first_wholes,
             ),
-            later_terms, (later_plan, first_plan[:-1]),
+            later_terms, (later_plan, [first_plan[:-1]]),
         )
-        grad_first = grad_v.astype(jnp.float32)
     else:
         dq_rot, dk_rot, grad_mixed = backward(*attention, 1)
         grad_q = rotate(dq_rot.astype(jnp.float32), cosine, -sine_tab).astype(low)
         grad_k = rotate(dk_rot.astype(jnp.float32), cosine, -sine_tab).astype(low)
         grad_v = grad_mixed * jnp.asarray(0.5, low)
-        grad_first = grad_v.T.astype(jnp.float32)
         grad_query_w = contract(normed_a, grad_q, 0, 1)
         grad_key_w = contract(normed_a, grad_k, 0, 1)
         grad_value_w = contract(normed_a, grad_v, 0, 1)
@@ -1650,6 +1677,7 @@
             + contract(grad_v, proj_value, 0, 1)
         )
         grad_gain_attn = jnp.sum(grad_normed_a * normed_input, axis=0)
+        grad_v = grad_v.T
         gain_terms = jnp.pad(jnp.stack([grad_gain_attn, grad_gain_ffn]), ((0, 6), (0, 0)))
         gain_terms = jnp.repeat(gain_terms.reshape(8, -1, 128).transpose(1, 0, 2), neighbours, axis=0)
         first_terms = [*terms(grad_query_w, grad_key_w, grad_value_w), gain_terms]
@@ -1660,14 +1688,10 @@
         )
         all_sums = reduce_all(first_terms + later_terms, every, 2)
         first_sums, later_sums = all_sums[:4], all_sums[4:]
-    scaled_attn = grad_normed_a * gain_attn
-    grad_layer = (
-        grad_after
-        + norm_attn * scaled_attn
-        - input_f32 * norm_attn**3 * jnp.mean(scaled_attn * input_f32, axis=-1, keepdims=True)
+    grad_layer, grad_first, *sums, sum_gains = publish(
+        layer_input, gain_rows, grad_normed_a, grad_after, grad_v,
+        [*first_sums[:3], *later_sums, first_sums[3]],
     )
-
-    *sums, sum_gains = publish([*first_sums[:3], *later_sums, first_sums[3]])
     sum_query, sum_key, sum_value, sum_gate, sum_up, sum_down, sum_out = sums
     sum_gains = lax.dynamic_slice_in_dim(sum_gains, turn, share, 1)
     return (

time: 415 us -> 400 us (0.964)
  other arithmetic: 11.9 us -> 3.45 us
where the time goes in v5:
time: 400 us; the launch traced here: 395 us
  Pallas kernels  353 us (88%)
  matrix products  32.3 us (8%)
  local copies, waits for them, and re-layouts  5.18 us (1%)
    pallas_call x1, Pallas kernels, backward(): pl.pallas_call(functools.partial(backward_kernel, tokens, plans, (n, len(...  185 us
    pallas_call x1, Pallas kernels, forward(): pl.pallas_call(functools.partial(forward_kernel, tokens, (first_plan, lat...  163 us
    dot_general x9, matrix products, contract(): lax.dot_general(left, right, (((left_dim,), (right_dim,)), ((), ())), pre...  26.5 us

profile of v5, /device:TPU:0, one launch (start us, length us, event | category | flops | bytes accessed | tf_op | source)
XLA Modules:
  0.0 395.0 jit_solution(11372006124397655547)
XLA Ops:
  0.7 0.7 pad_maximum_fusion
  1.4 0.8 dynamic-slice_bitcast_fusion
  2.1 0.6 dynamic_update_slice.7.refs_9_
  3.0 0.7 iota_add_fusion
  3.6 0.8 multiply_sine_fusion
  4.5 163.0 %shard_map.220 = (bf16[32,32,2816]{2,1,0:T(8,128)(2,1)}, bf16[32,32,2816]{2,1,0:T(8,128)(2,1)}, bf16[32,88,1024]{2,1,0:T(8,128)(2,1)}, bf16[32,32,1024]{2,1,0:T(...) custom-call(bf16[256,1024]{1,0:T(8,128)(2,1)} %x_ref.1, ...), custom_call_target="tpu_custom_call" | custom-call | flops 2863311360 | bytes 25952256 | tf_op jit(solution)/shard_map/pallas_call | solution.py:1085
  167.5 0.8 slice.9
  168.2 2.7 multiply_reduce_fusion.2
  171.7 1.7 fusion.5
  173.7 1.7 fusion.4
  175.6 3.3 multiply_convert_fusion
  178.9 2.5 fusion.1
  181.4 1.7 fusion.6
  183.1 2.5 multiply_reduce_fusion
  185.9 1.3 copy-done.2
  187.1 1.5 convolution_convert_fusion.4.refs_0_
  188.7 2.1 convolution_convert_fusion.3
  190.8 4.1 %convolution_convert_fusion = bf16[2816,1024]{1,0:T(8,128)(2,1)} fusion(bf16[256,2816]{1,0:T(8,128)(2,1)S(1)} %get-tuple-element.90, bf16[256,1024]{1,0:T(8,128)(2,1)S(1)} %copy-done.4), kind=kOutput, calls=%fused_computation | convolution fusion | flops 1479278592 | bytes 7733248 | tf_op jit(solution)/shard_map/dot_general | solution.py:1560
  194.9 4.3 %convolution_convert_fusion.1 = bf16[1024,2816]{1,0:T(8,128)(2,1)} fusion(bf16[256,1024]{1,0:T(8,128)(2,1)S(1)} %multiply_convert_fusion.3, bf16[256,2816]{1,0:T(8,128)(2,1)S(1)} %get-tuple-element.88), kind=kOutput, calls=%fused_computation.1 | convolution fusion | flops 1479278592 | bytes 7733248 | tf_op jit(solution)/shard_map/dot_general | solution.py:1560
  199.2 4.2 %convolution_convert_fusion.2 = bf16[1024,2816]{1,0:T(8,128)(2,1)} fusion(bf16[256,1024]{1,0:T(8,128)(2,1)S(1)} %multiply_convert_fusion.3, bf16[256,2816]{1,0:T(8,128)(2,1)S(1)} %get-tuple-element.89), kind=kOutput, calls=%fused_computation.2 | convolution fusion | flops 1479278592 | bytes 7733248 | tf_op jit(solution)/shard_map/dot_general | solution.py:1560
  203.4 185.4 %shard_map.221 = (f32[256,1024]{1,0:T(8,128)}, bf16[256,1024]{1,0:T(8,128)(2,1)}, f32[32,2816]{1,0:T(8,128)}, f32[32,2816]{1,0:T(8,128)}, f32[88,1024]{1,0:T(8,1...) custom-call(bf16[1024,256]{1,0:T(8,128)(2,1)} %convolution_convert_f, ...), custom_call_target="tpu_custom_call" | custom-call | flops 7158278144 | bytes 22544384 | tf_op jit(solution)/shard_map/pallas_call | solution.py:1485
  388.8 4.6 %shard_map.222 = (f32[256,1024]{1,0:T(8,128)}, f32[256,1024]{1,0:T(8,128)}, f32[32,1024]{1,0:T(8,128)}, f32[32,1024]{1,0:T(8,128)}, f32[32,1024]{1,0:T(8,128)}, ...) custom-call(bf16[256,1024]{1,0:T(8,128)(2,1)} %x_ref.1, ...), custom_call_target="tpu_custom_call" | custom-call | tf_op jit(solution)/shard_map/pallas_call | solution.py:1520
  393.4 0.7 constant_dynamic-slice_fusion
  394.2 0.5 slice_bitcast_fusion
  (31 shorter events, 1.8 us)
Async XLA Ops:
  2.9 1.5 copy-start.5
  4.5 163.8 %copy-start.3 = (bf16[256,1024]{1,0:T(8,128)(2,1)S(1)}, bf16[256,1024]{1,0:T(8,128)(2,1)}, u32[]{:S(2)}) copy-start(bf16[256,1024]{1,0:T(8,128)(2,1)} %x_ref.1) | copy-start | bytes 1572868
  168.2 3.4 copy-start.6
  171.0 2.4 slice-start
  171.6 2.0 slice-start.1
  171.6 3.7 slice-start.2
  173.7 1.7 copy-start.4
  173.7 1.9 slice-start.3
  185.5 1.6 copy-start.2
  187.1 1.5 copy-start
  187.1 1.6 copy-start.1

commit v6 on v5

--- a/solution.py
+++ b/solution.py
@@ -1306,7 +1306,7 @@
                 self.gain_terms[block * near + i] = both[:, block * 128 : (block + 1) * 128]
 
 
-REDUCE_FIRST = 14
+REDUCE_FIRST = 11
 REDUCE_TILES = 3
 REDUCE_TAIL = 1
 

time: 400 us -> 395 us (0.988)
  Pallas kernels: 353 us -> 348 us
    pallas_call x1, Pallas kernels: 185 us -> 181 us  [backward(): pl.pallas_call(functools.partial(backward_kernel, tokens, plans, (n, len(...]
where the time goes in v6:
time: 395 us; the launch traced here: 390 us
  Pallas kernels  348 us (88%)
  matrix products  32.3 us (8%)
  local copies, waits for them, and re-layouts  5.18 us (1%)
    pallas_call x1, Pallas kernels, backward(): pl.pallas_call(functools.partial(backward_kernel, tokens, plans, (n, len(...  181 us
    pallas_call x1, Pallas kernels, forward(): pl.pallas_call(functools.partial(forward_kernel, tokens, (first_plan, lat...  163 us
    dot_general x9, matrix products, contract(): lax.dot_general(left, right, (((left_dim,), (right_dim,)), ((), ())), pre...  26.5 us

profile of v6, /device:TPU:0, one launch (start us, length us, event | category | flops | bytes accessed | tf_op | source)
XLA Modules:
  0.0 390.4 jit_solution(3664344363951990916)
XLA Ops:
  0.7 0.7 pad_maximum_fusion
  1.4 0.8 dynamic-slice_bitcast_fusion
  2.1 0.6 dynamic_update_slice.7.refs_9_
  3.0 0.7 iota_add_fusion
  3.6 0.8 multiply_sine_fusion
  4.5 163.0 %shard_map.220 = (bf16[32,32,2816]{2,1,0:T(8,128)(2,1)}, bf16[32,32,2816]{2,1,0:T(8,128)(2,1)}, bf16[32,88,1024]{2,1,0:T(8,128)(2,1)}, bf16[32,32,1024]{2,1,0:T(...) custom-call(bf16[256,1024]{1,0:T(8,128)(2,1)} %x_ref.1, ...), custom_call_target="tpu_custom_call" | custom-call | flops 2863311360 | bytes 25952256 | tf_op jit(solution)/shard_map/pallas_call | solution.py:1085
  167.5 0.8 slice.9
  168.2 2.7 multiply_reduce_fusion.2
  171.7 1.7 fusion.5
  173.7 1.7 fusion.4
  175.6 3.3 multiply_convert_fusion
  178.9 2.5 fusion.1
  181.4 1.7 fusion.6
  183.1 2.5 multiply_reduce_fusion
  185.9 1.3 copy-done.2
  187.1 1.5 convolution_convert_fusion.4.refs_0_
  188.7 2.1 convolution_convert_fusion.3
  190.8 4.1 %convolution_convert_fusion = bf16[2816,1024]{1,0:T(8,128)(2,1)} fusion(bf16[256,2816]{1,0:T(8,128)(2,1)S(1)} %get-tuple-element.90, bf16[256,1024]{1,0:T(8,128)(2,1)S(1)} %copy-done.4), kind=kOutput, calls=%fused_computation | convolution fusion | flops 1479278592 | bytes 7733248 | tf_op jit(solution)/shard_map/dot_general | solution.py:1560
  194.9 4.3 %convolution_convert_fusion.1 = bf16[1024,2816]{1,0:T(8,128)(2,1)} fusion(bf16[256,1024]{1,0:T(8,128)(2,1)S(1)} %multiply_convert_fusion.3, bf16[256,2816]{1,0:T(8,128)(2,1)S(1)} %get-tuple-element.88), kind=kOutput, calls=%fused_computation.1 | convolution fusion | flops 1479278592 | bytes 7733248 | tf_op jit(solution)/shard_map/dot_general | solution.py:1560
  199.2 4.2 %convolution_convert_fusion.2 = bf16[1024,2816]{1,0:T(8,128)(2,1)} fusion(bf16[256,1024]{1,0:T(8,128)(2,1)S(1)} %multiply_convert_fusion.3, bf16[256,2816]{1,0:T(8,128)(2,1)S(1)} %get-tuple-element.89), kind=kOutput, calls=%fused_computation.2 | convolution fusion | flops 1479278592 | bytes 7733248 | tf_op jit(solution)/shard_map/dot_general | solution.py:1560
  203.4 180.8 %shard_map.221 = (f32[256,1024]{1,0:T(8,128)}, bf16[256,1024]{1,0:T(8,128)(2,1)}, f32[32,2816]{1,0:T(8,128)}, f32[32,2816]{1,0:T(8,128)}, f32[88,1024]{1,0:T(8,1...) custom-call(bf16[1024,256]{1,0:T(8,128)(2,1)} %convolution_convert_f, ...), custom_call_target="tpu_custom_call" | custom-call | flops 7158278144 | bytes 22544384 | tf_op jit(solution)/shard_map/pallas_call | solution.py:1485
  384.2 4.6 %shard_map.222 = (f32[256,1024]{1,0:T(8,128)}, f32[256,1024]{1,0:T(8,128)}, f32[32,1024]{1,0:T(8,128)}, f32[32,1024]{1,0:T(8,128)}, f32[32,1024]{1,0:T(8,128)}, ...) custom-call(bf16[256,1024]{1,0:T(8,128)(2,1)} %x_ref.1, ...), custom_call_target="tpu_custom_call" | custom-call | tf_op jit(solution)/shard_map/pallas_call | solution.py:1520
  388.8 0.7 constant_dynamic-slice_fusion
  389.6 0.5 slice_bitcast_fusion
  (31 shorter events, 1.8 us)
Async XLA Ops:
  2.9 1.5 copy-start.5
  4.5 163.8 %copy-start.3 = (bf16[256,1024]{1,0:T(8,128)(2,1)S(1)}, bf16[256,1024]{1,0:T(8,128)(2,1)}, u32[]{:S(2)}) copy-start(bf16[256,1024]{1,0:T(8,128)(2,1)} %x_ref.1) | copy-start | bytes 1572868
  168.2 3.4 copy-start.6
  171.0 2.4 slice-start
  171.6 2.0 slice-start.1
  171.6 3.7 slice-start.2
  173.7 1.7 copy-start.4
  173.7 1.9 slice-start.3
  185.5 1.6 copy-start.2
  187.1 1.5 copy-start
  187.1 1.6 copy-start.1

commit v7 on v6

--- a/solution.py
+++ b/solution.py
@@ -702,9 +702,9 @@
 QUERIES = 512
 KEYS = 1024
 BESIDE_PROJECT = 4
-BESIDE_EXCHANGE = 5
+BESIDE_EXCHANGE = 4
 BESIDE_TILES = 5
-LATER_AT = 4
+LATER_AT = 8
 COLUMNS = 256
 ANY = pl.BlockSpec(memory_space=pl.ANY)
 WHOLE = pl.BlockSpec(memory_space=pltpu.VMEM)
@@ -1613,7 +1613,12 @@
     input_f32 = layer_input.astype(jnp.float32)
     wholes, first_wholes, front, heads, (attended, lse, attn_tokens) = forward(
         (layer_input, v_first, cosine[0], sine_tab[0], pos),
-        first, first_plan, later, later_plan, 0,
+        first, first_plan, later,
+        plan(
+            [shard.shape[1] for shard in later],
+            (0, None, "A"), (1, None, "A"), (2, None, "C"), (3, None, "A"),
+        ),
+        0,
     )
     gain_rows, normed_a, begin, normed_input = front
     gain_ffn = gain_rows[1]

time: 395 us -> 393 us (level)
  no operation moved by 1% of the time
where the time goes in v7:
time: 393 us; the launch traced here: 388 us
  Pallas kernels  346 us (88%)
  matrix products  32.3 us (8%)
  local copies, waits for them, and re-layouts  5.18 us (1%)
    pallas_call x1, Pallas kernels, backward(): pl.pallas_call(functools.partial(backward_kernel, tokens, plans, (n, len(...  180 us
    pallas_call x1, Pallas kernels, forward(): pl.pallas_call(functools.partial(forward_kernel, tokens, (first_plan, lat...  162 us
    dot_general x9, matrix products, contract(): lax.dot_general(left, right, (((left_dim,), (right_dim,)), ((), ())), pre...  26.5 us

profile of v7, /device:TPU:0, one launch (start us, length us, event | category | flops | bytes accessed | tf_op | source)
XLA Modules:
  0.0 388.2 jit_solution(6160984904419059543)
XLA Ops:
  0.7 0.7 pad_maximum_fusion
  1.4 0.8 dynamic-slice_bitcast_fusion
  2.1 0.6 dynamic_update_slice.7.refs_9_
  3.0 0.7 iota_add_fusion
  3.6 0.8 multiply_sine_fusion
  4.5 161.8 %shard_map.220 = (bf16[32,32,2816]{2,1,0:T(8,128)(2,1)}, bf16[32,32,2816]{2,1,0:T(8,128)(2,1)}, bf16[32,88,1024]{2,1,0:T(8,128)(2,1)}, bf16[32,32,1024]{2,1,0:T(...) custom-call(bf16[256,1024]{1,0:T(8,128)(2,1)} %x_ref.1, ...), custom_call_target="tpu_custom_call" | custom-call | flops 2863311360 | bytes 25952256 | tf_op jit(solution)/shard_map/pallas_call | solution.py:1085
  166.2 0.8 slice.9
  167.0 2.7 multiply_reduce_fusion.2
  170.4 1.7 fusion.5
  172.5 1.7 fusion.4
  174.4 3.3 multiply_convert_fusion
  177.7 2.5 fusion.1
  180.1 1.7 fusion.6
  181.8 2.5 multiply_reduce_fusion
  184.6 1.3 copy-done.2
  185.9 1.5 convolution_convert_fusion.4.refs_0_
  187.4 2.1 convolution_convert_fusion.3
  189.6 4.1 %convolution_convert_fusion = bf16[2816,1024]{1,0:T(8,128)(2,1)} fusion(bf16[256,2816]{1,0:T(8,128)(2,1)S(1)} %get-tuple-element.90, bf16[256,1024]{1,0:T(8,128)(2,1)S(1)} %copy-done.4), kind=kOutput, calls=%fused_computation | convolution fusion | flops 1479278592 | bytes 7733248 | tf_op jit(solution)/shard_map/dot_general | solution.py:1560
  193.7 4.3 %convolution_convert_fusion.1 = bf16[1024,2816]{1,0:T(8,128)(2,1)} fusion(bf16[256,1024]{1,0:T(8,128)(2,1)S(1)} %multiply_convert_fusion.3, bf16[256,2816]{1,0:T(8,128)(2,1)S(1)} %get-tuple-element.88), kind=kOutput, calls=%fused_computation.1 | convolution fusion | flops 1479278592 | bytes 7733248 | tf_op jit(solution)/shard_map/dot_general | solution.py:1560
  198.0 4.2 %convolution_convert_fusion.2 = bf16[1024,2816]{1,0:T(8,128)(2,1)} fusion(bf16[256,1024]{1,0:T(8,128)(2,1)S(1)} %multiply_convert_fusion.3, bf16[256,2816]{1,0:T(8,128)(2,1)S(1)} %get-tuple-element.89), kind=kOutput, calls=%fused_computation.2 | convolution fusion | flops 1479278592 | bytes 7733248 | tf_op jit(solution)/shard_map/dot_general | solution.py:1560
  202.2 179.9 %shard_map.221 = (f32[256,1024]{1,0:T(8,128)}, bf16[256,1024]{1,0:T(8,128)(2,1)}, f32[32,2816]{1,0:T(8,128)}, f32[32,2816]{1,0:T(8,128)}, f32[88,1024]{1,0:T(8,1...) custom-call(bf16[1024,256]{1,0:T(8,128)(2,1)} %convolution_convert_f, ...), custom_call_target="tpu_custom_call" | custom-call | flops 7158278144 | bytes 22544384 | tf_op jit(solution)/shard_map/pallas_call | solution.py:1485
  382.1 4.6 %shard_map.222 = (f32[256,1024]{1,0:T(8,128)}, f32[256,1024]{1,0:T(8,128)}, f32[32,1024]{1,0:T(8,128)}, f32[32,1024]{1,0:T(8,128)}, f32[32,1024]{1,0:T(8,128)}, ...) custom-call(bf16[256,1024]{1,0:T(8,128)(2,1)} %x_ref.1, ...), custom_call_target="tpu_custom_call" | custom-call | tf_op jit(solution)/shard_map/pallas_call | solution.py:1520
  386.7 0.7 constant_dynamic-slice_fusion
  387.5 0.5 slice_bitcast_fusion
  (31 shorter events, 1.8 us)
Async XLA Ops:
  2.9 1.5 copy-start.5
  4.5 162.5 %copy-start.3 = (bf16[256,1024]{1,0:T(8,128)(2,1)S(1)}, bf16[256,1024]{1,0:T(8,128)(2,1)}, u32[]{:S(2)}) copy-start(bf16[256,1024]{1,0:T(8,128)(2,1)} %x_ref.1) | copy-start | bytes 1572868
  167.0 3.4 copy-start.6
  169.7 2.4 slice-start
  170.4 2.0 slice-start.1
  170.4 3.7 slice-start.2
  172.5 1.7 copy-start.4
  172.5 1.9 slice-start.3
  184.3 1.6 copy-start.2
  185.9 1.5 copy-start
  185.9 1.5 copy-start.1
